TPU v7x, 32 devices: a whole 2x2x4 slice. The times are simulated.
32 devices in a mesh: groups: 2 (over x), frames: 16 (over z, y, core).
Axes of the slice: x: 2, y: 2, z: 4, core: 2. Of those that a mesh axis runs over, the one named last changes fastest.
Arguments:
- features: bfloat16 [4096, 1024], P(('groups', 'frames')), parts along dimension 0, may hold values from -6 to 6
- valid_length: int32 [2], P('groups'), parts along dimension 0, may hold values from 1024 to 2048
- ln1_gain: float32 [1024], replicated, may hold values from 0.5 to 1.5
- w_qkv: bfloat16 [1024, 1536], P('frames'), may hold values from -3 to 3
- w_out: bfloat16 [512, 1024], P('frames'), may hold values from -0.25 to 0.25
- ln2_gain: float32 [1024], replicated, may hold values from 0.5 to 1.5
- w_pw1: bfloat16 [1024, 2048], P('frames'), may hold values from -0.1875 to 0.1875
- w_dw: float32 [9, 1024], replicated, may hold values from -2 to 2
- bn_scale: float32 [1024], replicated, may hold values from 0.5 to 2
- bn_shift: float32 [1024], replicated, may hold values from -3 to 3
- w_pw2: bfloat16 [1024, 1024], P('frames'), may hold values from -0.1875 to 0.1875
Outputs:
- block_out: bfloat16 [4096, 1024], P(('groups', 'frames')), parts along dimension 0
There are 2 independent parts, one for each index of `groups`. A program takes and returns all parts, laid end to end along the dimension named above; an argument that names none is the same for every part. Nothing has to cross between parts.
All inputs are finite; a program needn't handle non-finite values.
Results may differ from a plain program's by a relative error of at most 0.0098.
Values may be sent and summed in bfloat16 or wider, within the bound.
No kernel may reach another device: no remote copies, remote signals or barrier semaphores. Data moves between devices by JAX's collectives and lax.ppermute only.
A program may use at most 128 MiB of HBM per device.

v0:
```python
import math

import jax
import jax.numpy as jnp
from jax import lax
from jax.sharding import PartitionSpec as P

HEADS = 4
HD = 128


EPSILON = 1e-05


def extended(cells, sides, width):
    for axis, dim in sides:
        count = lax.axis_size(axis)
        ends = count - 1
        head = lax.slice_in_dim(cells, 0, width, axis=dim)
        tail = lax.slice_in_dim(cells, cells.shape[dim] - width, cells.shape[dim], axis=dim)
        cells = jnp.concatenate(
            [
                lax.ppermute(tail, axis, [(i, (i + 1) % count) for i in range(ends)]),
                cells,
                lax.ppermute(head, axis, [((i + 1) % count, i) for i in range(ends)]),
            ],
            axis=dim,
        )
    return cells


def layer_norm(values, gain):
    values = values.astype(jnp.float32)
    mean = jnp.mean(values, axis=-1, keepdims=True)
    centred = values - mean
    variance = jnp.mean(centred * centred, axis=-1, keepdims=True)
    return (centred * lax.rsqrt(variance + EPSILON) * gain).astype(jnp.bfloat16)


def per_device(
    features, valid_length, ln1_gain, w_qkv, w_out, ln2_gain, w_pw1, w_dw, bn_scale, bn_shift, w_pw2
):
    limit = valid_length[0]
    local_rows = features.shape[0]
    width = features.shape[1]
    att_width = w_qkv.shape[1] // 3
    scale = 1.0 / math.sqrt(HD)
    tails = (
        lax.all_gather(w_out, "frames", axis=0, tiled=True),
        lax.all_gather(w_pw1, "frames", axis=0, tiled=True),
        lax.all_gather(w_pw2, "frames", axis=0, tiled=True),
    )
    full_out, full_pw1, full_pw2 = tails
    normed1 = layer_norm(features, ln1_gain)
    qkv = jnp.dot(
        normed1,
        lax.all_gather(w_qkv, "frames", axis=0, tiled=True),
        preferred_element_type=jnp.float32,
    ).astype(jnp.bfloat16)
    query_heads = qkv[:, :att_width].reshape(local_rows, HEADS, HD)
    keys = qkv[:, att_width : 2 * att_width]
    values = qkv[:, 2 * att_width :]
    maxima = jnp.full((HEADS, local_rows), -1e30, jnp.float32)
    key_rows = lax.all_gather(keys, "frames", axis=0, tiled=True)
    value_rows = lax.all_gather(values, "frames", axis=0, tiled=True)
    count = key_rows.shape[0]
    key_heads = key_rows.reshape(count, HEADS, HD)
    value_heads = value_rows.reshape(count, HEADS, HD)
    scores = (
        jnp.einsum("qhd,khd->hqk", query_heads, key_heads, preferred_element_type=jnp.float32)
        * scale
    )
    position = jnp.arange(count, dtype=jnp.int32)
    valid = (position < limit)[None, None, :]
    scores = jnp.where(valid, scores, -1e30)
    fresh = jnp.maximum(maxima, jnp.max(scores, axis=-1))
    weights = jnp.where(valid, jnp.exp(scores - fresh[..., None]), 0.0)
    totals = jnp.sum(weights, axis=-1)
    update = jnp.einsum(
        "hqk,khd->hqd",
        weights.astype(jnp.bfloat16),
        value_heads,
        preferred_element_type=jnp.float32,
    )
    summed = update
    maxima, totals, summed = (fresh, totals, summed)
    context = (
        (summed / totals[..., None])
        .transpose(1, 0, 2)
        .reshape(local_rows, att_width)
        .astype(jnp.bfloat16)
    )
    attended = features.astype(jnp.float32) + jnp.dot(
        context, full_out, preferred_element_type=jnp.float32
    )
    normed2 = layer_norm(attended, ln2_gain)
    both = jnp.dot(normed2, full_pw1, preferred_element_type=jnp.float32)
    frame_index = lax.axis_index("frames") * local_rows + jnp.arange(local_rows, dtype=jnp.int32)
    frame_valid = (frame_index < limit)[:, None]
    gated = jnp.where(frame_valid, both[:, :width] * jax.nn.sigmoid(both[:, width:]), 0.0).astype(
        jnp.bfloat16
    )
    half_window = (w_dw.shape[0] - 1) // 2
    widened = extended(gated, (("frames", 0),), half_window)
    widened = widened.astype(jnp.float32)
    conv = jnp.zeros((local_rows, width), jnp.float32)
    for tap in range(w_dw.shape[0]):
        conv = conv + w_dw[tap][None, :] * widened[tap : tap + local_rows]
    activated = jax.nn.silu(bn_scale * conv + bn_shift).astype(jnp.bfloat16)
    result = attended + jnp.dot(activated, full_pw2, preferred_element_type=jnp.float32)
    return result.astype(jnp.bfloat16)


def solution(mesh):
    placed = (
        P(("groups", "frames"), None),
        P("groups"),
        P(),
        P("frames", None),
        P("frames", None),
        P(),
        P("frames", None),
        P(),
        P(),
        P(),
        P("frames", None),
    )
    return jax.shard_map(
        per_device,
        mesh=mesh,
        in_specs=placed,
        out_specs=P(("groups", "frames"), None),
        check_vma=False,
    )
```

profile of v0, /device:TPU:0, one launch (start us, length us, event | category | flops | bytes accessed | tf_op | source)
XLA Modules:
  0.0 286.1 jit_solution(17644636704648669902)
XLA Ops:
  6.5 0.7 all-gather.7.cloned.1.call-update
  7.3 0.0 all-gather.11.cloned.1.call-start
  7.3 1.1 convert_reduce_fusion
  8.4 1.2 fusion.21
  9.6 48.0 %all-gather.7.cloned.1.call-done = bf16[1024,1536]{1,0:T(8,128)(2,1)} async-done(((bf16[64,1536]{1,0:T(8,128)(2,1)}), bf16[1024,1536]{1,0:T(8,128)(2,1)}) %all-gather.7.cloned.1.call-update) | async-done | bytes 3145744 | tf_op jit(solution)/shard_map/all_gather | solution.py:57
  57.6 2.6 convolution_convert_fusion
  60.2 0.7 slice_bitcast_fusion
  61.0 0.0 all-gather.9.cloned.1.call-start
  61.0 0.7 all-gather.9.cloned.1.call-update
  61.7 0.0 all-gather.13.cloned.1.call-start
  61.7 0.5 all-gather.13.cloned.1.call-update
  62.3 0.5 all-gather.15.cloned.1.call-update
  62.9 0.0 all-gather.17.cloned.1.call-start
  62.9 0.5 all-gather.17.cloned.1.call-update
  64.1 37.2 %all-gather.11.cloned.1.call-done = bf16[2048,512]{1,0:T(8,128)(2,1)} async-done(((bf16[128,512]{1,0:T(8,128)(2,1)}), bf16[2048,512]{1,0:T(8,128)(2,1)}) %all-gather.11.cloned.1.call-update) | async-done | bytes 2097168 | tf_op jit(solution)/shard_map/all_gather | solution.py:65
  101.3 2.9 %copy.15 = bf16[2048,512]{0,1:T(8,128)(2,1)S(1)} copy(bf16[2048,512]{1,0:T(8,128)(2,1)} %all-gather.11.cloned.1.call-done) | data formatting | bytes 4194304 | tf_op jit(solution)/shard_map/reshape | solution.py:68
  104.3 39.4 %all-gather.9.cloned.1.call-done = bf16[2048,512]{1,0:T(8,128)(2,1)} async-done(((bf16[128,512]{1,0:T(8,128)(2,1)}), bf16[2048,512]{1,0:T(8,128)(2,1)}) %all-gather.9.cloned.1.call-update) | async-done | bytes 2097168 | tf_op jit(solution)/shard_map/all_gather | solution.py:64
  143.7 2.5 fusion
  146.2 1.1 fusion.1
  147.3 1.3 fusion.16
  148.6 33.8 %all-gather.13.cloned.1.call-done = bf16[512,1024]{1,0:T(8,128)(2,1)} async-done(((bf16[32,1024]{1,0:T(8,128)(2,1)}), bf16[512,1024]{1,0:T(8,128)(2,1)}) %all-gather.13.cloned.1.call-update) | async-done | bytes 1048592 | tf_op jit(solution)/shard_map/all_gather | solution.py:49
  182.5 1.6 fusion.68
  184.1 0.2 multiply_reduce_fusion
  184.4 49.6 %all-gather.15.cloned.1.call-done = bf16[1024,2048]{1,0:T(8,128)(2,1)} async-done(((bf16[64,2048]{1,0:T(8,128)(2,1)}), bf16[1024,2048]{1,0:T(8,128)(2,1)}) %all-gather.15.cloned.1.call-update) | async-done | bytes 4194320 | tf_op jit(solution)/shard_map/all_gather | solution.py:50
  234.0 3.0 %fusion.40 = f32[128,2048]{1,0:T(8,128)S(1)} fusion(bf16[1024,2048]{1,0:T(8,128)(2,1)} %all-gather.15.cloned.1.call-done, f32[128,1024]{1,0:T(8,128)S(1)} %get-tuple-element.22, f32[1024]{0:T(1024)S(1)} %copy-done.2, f32[128]{0:T(128)S(1)} %add_rsqrt_fusion, f32[128]{0:T(128)S(1)} %broadcast_multiply_fusion), kind=kOutput, calls=%fused_computation.54 | convolution fusion | flops 537395200 | bytes 5772288 | tf_op jit(solution)/shard_map/dot_general | solution.py:97
  236.9 0.2 fusion.39
  237.1 2.2 collective-permute-start
  239.3 1.3 collective-permute-start.1
  240.7 1.7 collective-permute-done.1
  242.4 0.1 maximum_convert_fusion
  242.4 33.5 %all-gather.17.cloned.1.call-done = bf16[1024,1024]{1,0:T(8,128)(2,1)} async-done(((bf16[64,1024]{1,0:T(8,128)(2,1)}), bf16[1024,1024]{1,0:T(8,128)(2,1)}) %all-gather.17.cloned.1.call-update) | async-done | bytes 2097168 | tf_op jit(solution)/shard_map/all_gather | solution.py:51
  275.9 3.3 %fusion.9 = bf16[128,1024]{1,0:T(8,128)(2,1)} fusion(f32[128,1024]{1,0:T(8,128)S(1)} %get-tuple-element.22, bf16[1024,1024]{1,0:T(8,128)(2,1)} %all-gather.17.cloned.1.call-done, f32[136,1024]{1,0:T(8,128)S(1)} %maximum_convert_fusion, f32[1024]{0:T(1024)S(1)} %copy-done.3, f32[1024]{0:T(1024)S(1)} %bitcast.52, f32[1024]{0:T(1024)S(1)} %bitcast.53, ...), kind=kOutput, calls=%fused_computation.13 | convolution fusion | flops 271843328 | bytes 7647232 | tf_op jit(solution)/shard_map/dot_general | solution.py:110
  (23 shorter events, 0.2 us)
Async XLA Ops:
  6.5 51.0 %all-gather.7.cloned.1.call-start = ((), (), s32[]{:S(2)}) async-start(), calls=%async_computation | async-start | bytes 3342336 | tf_op jit(solution)/shard_map/all_gather | solution.py:57
  7.3 94.1 %all-gather.11.cloned.1.call-start = ((), (), s32[]{:S(2)}) async-start(), calls=%async_computation.2 | async-start | bytes 2228224 | tf_op jit(solution)/shard_map/all_gather | solution.py:65
  61.0 82.7 %all-gather.9.cloned.1.call-start = ((), (), s32[]{:S(2)}) async-start(), calls=%async_computation.1 | async-start | bytes 2228224 | tf_op jit(solution)/shard_map/all_gather | solution.py:64
  61.7 120.8 %all-gather.13.cloned.1.call-start = ((), (), s32[]{:S(2)}) async-start(), calls=%async_computation.3 | async-start | bytes 1114112 | tf_op jit(solution)/shard_map/all_gather | solution.py:49
  62.3 171.7 %all-gather.15.cloned.1.call-start = ((), (), s32[]{:S(2)}) async-start(), calls=%async_computation.4 | async-start | bytes 4456448 | tf_op jit(solution)/shard_map/all_gather | solution.py:50
  62.9 213.1 %all-gather.17.cloned.1.call-start = ((), (), s32[]{:S(2)}) async-start(), calls=%async_computation.5 | async-start | bytes 2228224 | tf_op jit(solution)/shard_map/all_gather | solution.py:51
  147.3 35.2 %copy-start = (bf16[128,1024]{1,0:T(8,128)(2,1)S(1)}, bf16[128,1024]{1,0:T(8,128)(2,1)}, u32[]{:S(2)}) copy-start(bf16[128,1024]{1,0:T(8,128)(2,1)} %param.11) | copy-start | bytes 786436
  147.3 86.7 %copy-start.2 = (f32[1024]{0:T(1024)S(1)}, f32[1024]{0:T(1024)}, u32[]{:S(2)}) copy-start(f32[1024]{0:T(1024)} %param.16) | copy-start | bytes 12292
  184.1 56.5 %copy-start.1 = (f32[9,1024]{1,0:T(8,128)S(1)}, f32[9,1024]{1,0:T(8,128)}, u32[]{:S(2)}) copy-start(f32[9,1024]{1,0:T(8,128)} %param.18) | copy-start | bytes 110596
  184.1 91.8 %copy-start.3 = (f32[1024]{0:T(1024)S(1)}, f32[1024]{0:T(1024)}, u32[]{:S(2)}) copy-start(f32[1024]{0:T(1024)} %param.20) | copy-start | bytes 12292
  184.1 91.8 %copy-start.4 = (f32[1024]{0:T(1024)S(1)}, f32[1024]{0:T(1024)}, u32[]{:S(2)}) copy-start(f32[1024]{0:T(1024)} %param.19) | copy-start | bytes 12292
  237.1 3.5 %collective-permute-start = (bf16[4,1024]{1,0:T(4,128)(2,1)S(1)}, bf16[4,1024]{1,0:T(4,128)(2,1)S(1)}, u32[]{:S(2)}, u32[]{:S(2)}) collective-permute-start(bf16[4,1024]{1,0:T(4,128)(2,1)S(1)} %get-tuple-element.8), channel_id=1, source_target_pairs={{0,1},{1,2},{2,3},{3,4},{4,5},{5,6},{6,7},{7,8},{8,9},{9,10},{10,1... | collective-permute-start | bytes 24584 | tf_op jit(solution)/shard_map/ppermute | solution.py:23
  239.3 3.1 %collective-permute-start.1 = (bf16[4,1024]{1,0:T(4,128)(2,1)S(1)}, bf16[4,1024]{1,0:T(4,128)(2,1)S(1)}, u32[]{:S(2)}, u32[]{:S(2)}) collective-permute-start(bf16[4,1024]{1,0:T(4,128)(2,1)S(1)} %get-tuple-element.9), channel_id=1, source_target_pairs={{1,0},{2,1},{3,2},{4,3},{5,4},{6,5},{7,6},{8,7},{9,8},{10,9},{11,1... | collective-permute-start | bytes 24584 | tf_op jit(solution)/shard_map/ppermute | solution.py:25
Sparse Core Ops, SparseCore 0:
  9.6 47.8 all-gather.6
  61.1 40.1 all-gather.10
  103.5 40.1 all-gather.8
  145.7 36.7 all-gather.12
  184.5 49.4 all-gather.14
  236.0 39.8 all-gather.16
where the time goes:
time: 287 us; the launch traced here: 286 us
  waiting for transfers between devices  246 us (86%)
  matrix products  14.4 us (5%)
  between operations  14.3 us (5%)
  other arithmetic  3.81 us (1%)
  local copies, waits for them, and re-layouts  3.71 us (1%)
  starting transfers between devices  3.65 us (1%)
    all_gather x1, waiting for transfers between devices, per_device(): lax.all_gather(w_pw1, 'frames', axis=0, tiled=True)  49.6 us
    all_gather x1, waiting for transfers between devices, per_device(): lax.all_gather(w_qkv, 'frames', axis=0, tiled=True)  48 us
    all_gather x1, waiting for transfers between devices, per_device(): key_rows = lax.all_gather(keys, 'frames', axis=0, tiled=True)  39.4 us
    all_gather x1, waiting for transfers between devices, per_device(): value_rows = lax.all_gather(values, 'frames', axis=0, tiled=True)  37.2 us
    all_gather x1, waiting for transfers between devices, per_device(): lax.all_gather(w_out, 'frames', axis=0, tiled=True)  33.8 us
    all_gather x1, waiting for transfers between devices, per_device(): lax.all_gather(w_pw2, 'frames', axis=0, tiled=True)  33.5 us
  transfers between devices with their start and end apart: 8, of which 7 were waited for; matrix products, arithmetic and copies ran while one was open for 5% of the time, Pallas kernels for 0%

commit v1 on v0

--- a/solution.py
+++ b/solution.py
@@ -1,15 +1,23 @@
+import functools
 import math
 
 import jax
 import jax.numpy as jnp
 from jax import lax
+from jax.experimental import pallas as pl
+from jax.experimental.pallas import tpu as pltpu
 from jax.sharding import PartitionSpec as P
 
 HEADS = 4
 HD = 128
 
-
 EPSILON = 1e-05
+EDGE = 16
+LOG2E = 1.4426950408889634
+
+ORDER_EVEN = (8, 4, 2)
+ORDER_ODD = (2, 8, 4)
+ALONG_Z = (0, 8, 4, 12)
 
 
 def extended(cells, sides, width):
@@ -37,7 +45,7 @@
     return (centred * lax.rsqrt(variance + EPSILON) * gain).astype(jnp.bfloat16)
 
 
-def per_device(
+def per_device_general(
     features, valid_length, ln1_gain, w_qkv, w_out, ln2_gain, w_pw1, w_dw, bn_scale, bn_shift, w_pw2
 ):
     limit = valid_length[0]
@@ -45,12 +53,9 @@
     width = features.shape[1]
     att_width = w_qkv.shape[1] // 3
     scale = 1.0 / math.sqrt(HD)
-    tails = (
-        lax.all_gather(w_out, "frames", axis=0, tiled=True),
-        lax.all_gather(w_pw1, "frames", axis=0, tiled=True),
-        lax.all_gather(w_pw2, "frames", axis=0, tiled=True),
-    )
-    full_out, full_pw1, full_pw2 = tails
+    full_out = lax.all_gather(w_out, "frames", axis=0, tiled=True)
+    full_pw1 = lax.all_gather(w_pw1, "frames", axis=0, tiled=True)
+    full_pw2 = lax.all_gather(w_pw2, "frames", axis=0, tiled=True)
     normed1 = layer_norm(features, ln1_gain)
     qkv = jnp.dot(
         normed1,
@@ -58,32 +63,25 @@
         preferred_element_type=jnp.float32,
     ).astype(jnp.bfloat16)
     query_heads = qkv[:, :att_width].reshape(local_rows, HEADS, HD)
-    keys = qkv[:, att_width : 2 * att_width]
-    values = qkv[:, 2 * att_width :]
-    maxima = jnp.full((HEADS, local_rows), -1e30, jnp.float32)
-    key_rows = lax.all_gather(keys, "frames", axis=0, tiled=True)
-    value_rows = lax.all_gather(values, "frames", axis=0, tiled=True)
-    count = key_rows.shape[0]
-    key_heads = key_rows.reshape(count, HEADS, HD)
-    value_heads = value_rows.reshape(count, HEADS, HD)
+    pairs = lax.all_gather(qkv[:, att_width:], "frames", axis=0, tiled=True)
+    count = pairs.shape[0]
+    key_heads = pairs[:, :att_width].reshape(count, HEADS, HD)
+    value_heads = pairs[:, att_width:].reshape(count, HEADS, HD)
     scores = (
         jnp.einsum("qhd,khd->hqk", query_heads, key_heads, preferred_element_type=jnp.float32)
         * scale
     )
-    position = jnp.arange(count, dtype=jnp.int32)
-    valid = (position < limit)[None, None, :]
+    valid = (jnp.arange(count, dtype=jnp.int32) < limit)[None, None, :]
     scores = jnp.where(valid, scores, -1e30)
-    fresh = jnp.maximum(maxima, jnp.max(scores, axis=-1))
-    weights = jnp.where(valid, jnp.exp(scores - fresh[..., None]), 0.0)
+    maxima = jnp.max(scores, axis=-1)
+    weights = jnp.where(valid, jnp.exp(scores - maxima[..., None]), 0.0)
     totals = jnp.sum(weights, axis=-1)
-    update = jnp.einsum(
+    summed = jnp.einsum(
         "hqk,khd->hqd",
         weights.astype(jnp.bfloat16),
         value_heads,
         preferred_element_type=jnp.float32,
     )
-    summed = update
-    maxima, totals, summed = (fresh, totals, summed)
     context = (
         (summed / totals[..., None])
         .transpose(1, 0, 2)
@@ -101,8 +99,7 @@
         jnp.bfloat16
     )
     half_window = (w_dw.shape[0] - 1) // 2
-    widened = extended(gated, (("frames", 0),), half_window)
-    widened = widened.astype(jnp.float32)
+    widened = extended(gated, (("frames", 0),), half_window).astype(jnp.float32)
     conv = jnp.zeros((local_rows, width), jnp.float32)
     for tap in range(w_dw.shape[0]):
         conv = conv + w_dw[tap][None, :] * widened[tap : tap + local_rows]
@@ -111,6 +108,242 @@
     return result.astype(jnp.bfloat16)
 
 
+def swap(array, even, odd=None):
+    odd = even if odd is None else odd
+    pairs = [(i, i ^ (odd if i & 1 else even)) for i in range(16)]
+    return lax.ppermute(array, "frames", pairs)
+
+
+def block_masks(order):
+    masks = [0]
+    for bit in order:
+        masks = masks + [mask ^ bit for mask in masks]
+    return masks
+
+
+def after(arrays, others):
+    joined = lax.optimization_barrier(tuple(arrays) + tuple(others))
+    return joined[: len(arrays)]
+
+
+def source_of(me, j, even, odd, other_core):
+    origin = me ^ 1 if other_core else me
+    core = origin & 1
+    return origin ^ jnp.where(core == 0, even[j], odd[j])
+
+
+def attention_kernel(
+    scalars, own_x, other_x, own_w, other_w, *refs, rows, even, odd, w_masks, count
+):
+    outs, (x_all, w_all, keys, values, sems) = refs[:4], refs[4:]
+    me, limit = scalars[0], scalars[1]
+    depth = w_all.shape[0] // 16
+    for other_core, (xs, ws) in enumerate(((own_x, own_w), (other_x, other_w))):
+        for j in range(8):
+            src = source_of(me, j, w_masks, w_masks, other_core)
+            pltpu.make_async_copy(
+                ws.at[pl.ds(j * depth, depth)],
+                w_all.at[pl.ds(pl.multiple_of(src * depth, depth), depth)],
+                sems.at[0],
+            ).start()
+        for j in range(8):
+            src = source_of(me, j, even, odd, other_core)
+            pltpu.make_async_copy(
+                xs.at[pl.ds(j * rows, rows)],
+                x_all.at[pl.ds(pl.multiple_of(EDGE + src * rows, EDGE), rows)],
+                sems.at[1],
+            ).start()
+    width = x_all.shape[1]
+    x_all[0:EDGE, :] = jnp.zeros((EDGE, width), jnp.bfloat16)
+    x_all[EDGE + count : 2 * EDGE + count, :] = jnp.zeros((EDGE, width), jnp.bfloat16)
+    pltpu.make_async_copy(w_all, w_all, sems.at[0]).wait()
+    inner = x_all.at[pl.ds(EDGE, count)]
+    pltpu.make_async_copy(inner, inner, sems.at[1]).wait()
+    step = 512
+    for r in range(count // step):
+        both = jnp.dot(
+            x_all[EDGE + r * step : EDGE + (r + 1) * step, :],
+            w_all[:, HD:],
+            preferred_element_type=jnp.float32,
+        ).astype(jnp.bfloat16)
+        keys[r * step : (r + 1) * step, :] = both[:, :HD]
+        values[r * step : (r + 1) * step, :] = both[:, HD:]
+    wide = rows + 2 * EDGE
+    position = lax.broadcasted_iota(jnp.int32, (1, count), 1)
+    valid = position < limit
+    factor = LOG2E / math.sqrt(HD)
+    for mask, out in zip(ALONG_Z, outs):
+        start = pl.multiple_of((me ^ mask) * rows, EDGE)
+        query = jnp.dot(
+            x_all[pl.ds(start, wide), :], w_all[:, :HD], preferred_element_type=jnp.float32
+        ).astype(jnp.bfloat16)
+        scores = lax.dot_general(
+            query, keys[...], (((1,), (1,)), ((), ())), preferred_element_type=jnp.float32
+        )
+        scores = jnp.where(valid, scores * factor, -1e30)
+        weights = jnp.exp2(scores - jnp.max(scores, axis=-1, keepdims=True))
+        totals = jnp.sum(weights, axis=-1, keepdims=True)
+        summed = jnp.dot(
+            weights.astype(jnp.bfloat16), values[...], preferred_element_type=jnp.float32
+        )
+        out[...] = (summed / totals).astype(jnp.bfloat16)
+
+
+def tail_kernel(
+    scalars, c0, c1, c2, c3, feats, gain, taps, bn_scale, bn_shift, own, other, out,
+    w_out, w_value, w_gate, w_last, wide_gated, sems, *, rows, even, odd, parts
+):
+    me, limit = scalars[0], scalars[1]
+    size = sum(parts)
+    homes = (w_out, w_value, w_gate, w_last)
+    starts = [sum(parts[:i]) for i in range(len(parts))]
+    for i, home in enumerate(homes):
+        for other_core, held in enumerate((own, other)):
+            for j in range(8):
+                src = source_of(me, j, even, odd, other_core)
+                pltpu.make_async_copy(
+                    held.at[pl.ds(j * size + starts[i], parts[i])],
+                    home.at[pl.ds(pl.multiple_of(src * parts[i], parts[i]), parts[i])],
+                    sems.at[i],
+                ).start()
+    wide = rows + 2 * EDGE
+    attended = feats[...].astype(jnp.float32)
+    head = me // 4
+    pltpu.make_async_copy(w_out, w_out, sems.at[0]).wait()
+    for mask, part in zip(ALONG_Z, (c0, c1, c2, c3)):
+        start = pl.multiple_of((head ^ (mask // 4)) * HD, HD)
+        attended = attended + jnp.dot(
+            part[...], w_out[pl.ds(start, HD), :], preferred_element_type=jnp.float32
+        )
+    mean = jnp.mean(attended, axis=-1, keepdims=True)
+    centred = attended - mean
+    variance = jnp.mean(centred * centred, axis=-1, keepdims=True)
+    normed2 = (centred * lax.rsqrt(variance + EPSILON) * gain[...]).astype(jnp.bfloat16)
+    pltpu.make_async_copy(w_value, w_value, sems.at[1]).wait()
+    value = jnp.dot(normed2, w_value[...], preferred_element_type=jnp.float32)
+    pltpu.make_async_copy(w_gate, w_gate, sems.at[2]).wait()
+    gate = jnp.dot(normed2, w_gate[...], preferred_element_type=jnp.float32)
+    frame = me * rows - EDGE + lax.broadcasted_iota(jnp.int32, (wide, 1), 0)
+    inside = (frame >= 0) & (frame < limit)
+    gated = jnp.where(inside, value * jax.nn.sigmoid(gate), 0.0)
+    wide_gated[...] = gated.astype(jnp.bfloat16).astype(jnp.float32)
+    half = (taps.shape[0] - 1) // 2
+    conv = jnp.zeros((rows, out.shape[1]), jnp.float32)
+    for tap in range(taps.shape[0]):
+        at = EDGE - half + tap
+        conv = conv + taps[tap : tap + 1, :] * wide_gated[at : at + rows, :]
+    act = bn_scale[...] * conv + bn_shift[...]
+    activated = (act * jax.nn.sigmoid(act)).astype(jnp.bfloat16)
+    pltpu.make_async_copy(w_last, w_last, sems.at[3]).wait()
+    result = attended[EDGE : EDGE + rows, :] + jnp.dot(
+        activated, w_last[...], preferred_element_type=jnp.float32
+    )
+    out[...] = result.astype(jnp.bfloat16)
+
+
+def per_device(
+    features, valid_length, ln1_gain, w_qkv, w_out, ln2_gain, w_pw1, w_dw, bn_scale, bn_shift, w_pw2
+):
+    rows, width = features.shape
+    count = rows * 16
+    depth = w_qkv.shape[0]
+    me = lax.axis_index("frames")
+    z = me // 4
+    scalars = jnp.stack([me.astype(jnp.int32), valid_length[0]])
+    even, odd = block_masks(ORDER_EVEN), block_masks(ORDER_ODD)
+
+    normed1 = layer_norm(features, ln1_gain)
+    by_head = w_qkv.reshape(depth, 3, HEADS, HD).transpose(2, 0, 1, 3).reshape(HEADS, depth, 3 * HD)
+    pack = jnp.concatenate([w_out, w_pw1[:, :width], w_pw1[:, width:], w_pw2], axis=0)
+    parts = (w_out.shape[0], depth, depth, depth)
+
+    x1 = swap(normed1, ORDER_EVEN[0], ORDER_ODD[0])
+    w_z = [
+        swap(lax.dynamic_index_in_dim(by_head, z ^ (mask // 4), 0, keepdims=False), mask)
+        for mask in ALONG_Z[1:]
+    ]
+    w_mine = lax.dynamic_index_in_dim(by_head, z, 0, keepdims=False)
+    ahead = lax.ppermute(features[-EDGE:], "frames", [(i, i + 1) for i in range(15)])
+    behind = lax.ppermute(features[:EDGE], "frames", [(i + 1, i) for i in range(15)])
+    p1 = swap(pack, ORDER_EVEN[0], ORDER_ODD[0])
+    x = jnp.concatenate([normed1, x1], axis=0)
+    w4 = jnp.concatenate([w_mine] + w_z, axis=0)
+    pack = jnp.concatenate([pack, p1], axis=0)
+
+    x2 = swap(x, ORDER_EVEN[1], ORDER_ODD[1])
+    w2 = swap(w4, 2)
+    p2 = swap(pack, ORDER_EVEN[1], ORDER_ODD[1])
+    x = jnp.concatenate([x, x2], axis=0)
+    w8 = jnp.concatenate([w4, w2], axis=0)
+    pack = jnp.concatenate([pack, p2], axis=0)
+
+    x3 = swap(x, ORDER_EVEN[2], ORDER_ODD[2])
+    w_other = swap(w8, 1)
+    x = jnp.concatenate([x, x3], axis=0)
+    x_other = swap(x, 1)
+    p3 = swap(pack, ORDER_EVEN[2], ORDER_ODD[2])
+    pack = jnp.concatenate([pack, p3], axis=0)
+    pack_other = swap(pack, 1)
+
+    wide = rows + 2 * EDGE
+    w_masks = block_masks((8, 4, 2))
+    any_spec = pl.BlockSpec(memory_space=pl.ANY)
+    smem = pl.BlockSpec(memory_space=pltpu.SMEM)
+    vmem = pl.BlockSpec(memory_space=pltpu.VMEM)
+    contexts = pl.pallas_call(
+        functools.partial(
+            attention_kernel, rows=rows, even=even, odd=odd, w_masks=w_masks, count=count
+        ),
+        name="attention",
+        out_shape=[jax.ShapeDtypeStruct((wide, HD), jnp.bfloat16)] * 4,
+        in_specs=[smem] + [any_spec] * 4,
+        out_specs=[vmem] * 4,
+        scratch_shapes=[
+            pltpu.VMEM((count + 2 * EDGE, width), jnp.bfloat16),
+            pltpu.VMEM((16 * depth, 3 * HD), jnp.bfloat16),
+            pltpu.VMEM((count, HD), jnp.bfloat16),
+            pltpu.VMEM((count, HD), jnp.bfloat16),
+            pltpu.SemaphoreType.DMA((2,)),
+        ],
+        compiler_params=pltpu.CompilerParams(vmem_limit_bytes=40 << 20),
+        cost_estimate=pl.CostEstimate(
+            flops=4_000_000_000, bytes_accessed=8 << 20, transcendentals=4 * wide * count
+        ),
+    )(scalars, x, x_other, w8, w_other)
+    mine = [contexts[0]] + [swap(part, mask) for part, mask in zip(contexts[1:], ALONG_Z[1:])]
+
+    feats = jnp.concatenate([ahead, features, behind], axis=0)
+    return pl.pallas_call(
+        functools.partial(tail_kernel, rows=rows, even=even, odd=odd, parts=parts),
+        name="tail",
+        out_shape=jax.ShapeDtypeStruct((rows, width), jnp.bfloat16),
+        in_specs=[smem] + [vmem] * 9 + [any_spec] * 2,
+        out_specs=vmem,
+        scratch_shapes=[
+            pltpu.VMEM((16 * parts[0], width), jnp.bfloat16),
+            pltpu.VMEM((16 * depth, width), jnp.bfloat16),
+            pltpu.VMEM((16 * depth, width), jnp.bfloat16),
+            pltpu.VMEM((16 * depth, width), jnp.bfloat16),
+            pltpu.VMEM((wide, width), jnp.float32),
+            pltpu.SemaphoreType.DMA((4,)),
+        ],
+        compiler_params=pltpu.CompilerParams(vmem_limit_bytes=40 << 20),
+        cost_estimate=pl.CostEstimate(
+            flops=1_200_000_000, bytes_accessed=8 << 20, transcendentals=wide * width * 2
+        ),
+    )(
+        scalars,
+        *mine,
+        feats,
+        ln2_gain.reshape(1, -1),
+        w_dw,
+        bn_scale.reshape(1, -1),
+        bn_shift.reshape(1, -1),
+        pack,
+        pack_other,
+    )
+
+
 def solution(mesh):
     placed = (
         P(("groups", "frames"), None),
@@ -126,7 +359,7 @@
         P("frames", None),
     )
     return jax.shard_map(
-        per_device,
+        per_device if mesh.shape["frames"] == 16 else per_device_general,
         mesh=mesh,
         in_specs=placed,
         out_specs=P(("groups", "frames"), None),

time: 287 us -> 153 us (0.53)
  waiting for transfers between devices: 246 us -> 101 us
  starting transfers between devices: 3.65 us -> 26.2 us
  matrix products: 14.4 us -> 0 us
  Pallas kernels: 0 us -> 13.4 us
  between operations: 14.3 us -> 0.92 us
  local copies, waits for them, and re-layouts: 3.71 us -> 9.63 us
    all_gather x6 -> x0, waiting for transfers between devices: 242 us -> none  [the longest x1 49.6 us: per_device(): lax.all_gather(w_pw1, 'frames', axis=0, tiled=True)]
    ppermute x2 -> x18, waiting for transfers between devices: 1.71 us -> 101 us  [the longest x16 101 us: swap(): return lax.ppermute(array, 'frames', pairs)]
    ppermute x2 -> x18, starting transfers between devices: 3.45 us -> 26.2 us  [the longest x16 22.5 us: swap(): return lax.ppermute(array, 'frames', pairs)]
    dot_general x6 -> x0, matrix products: 14.4 us -> none  [the longest x1 3.33 us: per_device(): jnp.dot(activated, full_pw2, preferred_element_type=jnp.float32)]
    pallas_call x0 -> x2, Pallas kernels: none -> 13.4 us  [the longest x1 7.76 us: per_device(): pl.pallas_call(functools.partial(attention_kernel, rows=rows, even=even,...]
    unnamed x11 -> x28, local copies, waits for them, and re-layouts: 0.74 us -> 6.61 us
    unnamed x6 -> x0, waiting for transfers between devices: 2.99 us -> none
  transfers between devices with their start and end apart: 8 -> 18, of which waited for: 7 -> 11; matrix products, arithmetic and copies ran while one was open for 5% -> 3% of each run, Pallas kernels for 0% -> 5%
where the time goes in v1:
time: 153 us
  waiting for transfers between devices  101 us (66%)
  starting transfers between devices  26.2 us (17%)
  Pallas kernels  13.4 us (9%)
  local copies, waits for them, and re-layouts  9.63 us (6%)
  other arithmetic  1.9 us (1%)
    ppermute x16, waiting for transfers between devices, swap(): return lax.ppermute(array, 'frames', pairs)  101 us
    ppermute x16, starting transfers between devices, swap(): return lax.ppermute(array, 'frames', pairs)  22.5 us
    pallas_call x1, Pallas kernels, per_device(): pl.pallas_call(functools.partial(attention_kernel, rows=rows, even=even,...  7.76 us
    unnamed x28, local copies, waits for them, and re-layouts  6.61 us
    pallas_call x1, Pallas kernels, per_device(): pl.pallas_call(functools.partial(tail_kernel, rows=rows, even=even, odd=o...  5.64 us
  transfers between devices with their start and end apart: 18, of which 11 were waited for; matrix products, arithmetic and copies ran while one was open for 3% of the time, Pallas kernels for 5%

profile of v1, /device:TPU:0, one launch (start us, length us, event | category | flops | bytes accessed | tf_op | source)
XLA Modules:
  0.0 153.1 jit_solution(9365589611505680555)
XLA Ops:
  0.0 1.5 %constant_dynamic-update-slice_fusion.15 = (bf16[896,1024]{1,0:T(8,128)(2,1)S(1)}, bf16[448,1024]{1,0:T(8,128)(2,1)S(1)}, bf16[1792,1024]{1,0:T(8,128)(2,1)}) fusion(bf16[32,1024]{1,0:T(8,128)(2,1)} %param.15), kind=kLoop, calls=%fused_computation.33 | loop fusion | bytes 262144
  1.5 0.9 constant_dynamic-update-slice_fusion.14
  2.5 1.7 %constant_dynamic-update-slice_fusion.13 = (bf16[896,1024]{1,0:T(8,128)(2,1)S(1)}, bf16[448,1024]{1,0:T(8,128)(2,1)S(1)}, bf16[1792,1024]{1,0:T(8,128)(2,1)}, bf...) fusion(bf16[896,1024]{1,0:T(8,128)(2,1)S(1)} %constant_dynamic-update-slice_fusion.14, bf16[64,2048]{1,0:T(8,128)(2,1)} %param.17, ...), kind=kLoop, calls=%fused_computation.31 | loop fusion | bytes 917504
  4.2 0.9 pad_maximum_fusion.3
  5.2 4.1 %collective-permute-start.14 = (bf16[224,1024]{1,0:T(8,128)(2,1)S(1)}, bf16[224,1024]{1,0:T(8,128)(2,1)S(1)}, u32[]{:S(2)}, u32[]{:S(2)}) collective-permute-start(bf16[224,1024]{1,0:T(8,128)(2,1)S(1)} %pad_maximum_fusion.3), channel_id=1, source_target_pairs={{0,8},{1,3},{2,10},{3,1},{4,12},{5,7},{6,14},{7,5},{8,0},{9,11},{1... | collective-permute-start | bytes 1376264 | tf_op jit(solution)/shard_map/ppermute | solution.py:114
  9.9 0.7 constant_dynamic-update-slice_fusion.12
  10.6 21.9 %collective-permute-done.14 = bf16[224,1024]{1,0:T(8,128)(2,1)S(1)} collective-permute-done((bf16[224,1024]{1,0:T(8,128)(2,1)S(1)}, bf16[224,1024]{1,0:T(8,128)(2,1)S(1)}, u32[]{:S(2)}, u32[]{:S(2)}) %collective-permute-start.14) | collective-permute-done | bytes 458784 | tf_op jit(solution)/shard_map/ppermute | solution.py:114
  32.5 1.0 constant_dynamic-update-slice_fusion.11
  33.5 1.2 collective-permute-start.15
  34.8 27.0 %collective-permute-done.15 = bf16[448,1024]{1,0:T(8,128)(2,1)S(1)} collective-permute-done((bf16[448,1024]{1,0:T(8,128)(2,1)S(1)}, bf16[448,1024]{1,0:T(8,128)(2,1)S(1)}, u32[]{:S(2)}, u32[]{:S(2)}) %collective-permute-start.15) | collective-permute-done | bytes 917536 | tf_op jit(solution)/shard_map/ppermute | solution.py:114
  61.7 1.2 constant_dynamic-update-slice_fusion.10
  63.0 1.8 %collective-permute-start.16 = (bf16[896,1024]{1,0:T(8,128)(2,1)S(1)}, bf16[896,1024]{1,0:T(8,128)(2,1)S(1)}, u32[]{:S(2)}, u32[]{:S(2)}) collective-permute-start(bf16[896,1024]{1,0:T(8,128)(2,1)S(1)} %get-tuple-element.15), channel_id=1, source_target_pairs={{0,2},{1,5},{2,0},{3,7},{4,6},{5,1},{6,4},{7,3},{8,10},{9,13},{10,... | collective-permute-start | bytes 5505032 | tf_op jit(solution)/shard_map/ppermute | solution.py:114
  65.3 1.6 %collective-permute-start = (bf16[128,1024]{1,0:T(8,128)(2,1)S(1)}, bf16[128,1024]{1,0:T(8,128)(2,1)S(1)}, u32[]{:S(2)}, u32[]{:S(2)}) collective-permute-start(bf16[128,1024]{1,0:T(8,128)(2,1)S(1)} %fusion.4), channel_id=1, source_target_pairs={{0,8},{1,3},{2,10},{3,1},{4,12},{5,7},{6,14},{7,5},{8,0},{9,11},{1... | collective-permute-start | bytes 786440 | tf_op jit(solution)/shard_map/ppermute | solution.py:114
  66.9 12.9 %collective-permute-done = bf16[128,1024]{1,0:T(8,128)(2,1)S(1)} collective-permute-done((bf16[128,1024]{1,0:T(8,128)(2,1)S(1)}, bf16[128,1024]{1,0:T(8,128)(2,1)S(1)}, u32[]{:S(2)}, u32[]{:S(2)}) %collective-permute-start) | collective-permute-done | bytes 262176 | tf_op jit(solution)/shard_map/ppermute | solution.py:114
  79.9 14.8 %collective-permute-done.1 = bf16[256,1024]{1,0:T(8,128)(2,1)S(1)} collective-permute-done((bf16[256,1024]{1,0:T(8,128)(2,1)S(1)}, bf16[256,1024]{1,0:T(8,128)(2,1)S(1)}, u32[]{:S(2)}, u32[]{:S(2)}) %collective-permute-start.1) | collective-permute-done | bytes 524320 | tf_op jit(solution)/shard_map/ppermute | solution.py:114
  94.9 1.6 %collective-permute-start.2 = (bf16[512,1024]{1,0:T(8,128)(2,1)S(1)}, bf16[512,1024]{1,0:T(8,128)(2,1)S(1)}, u32[]{:S(2)}, u32[]{:S(2)}) collective-permute-start(bf16[512,1024]{1,0:T(8,128)(2,1)S(1)} %pad_maximum_fusion.1), channel_id=1, source_target_pairs={{0,2},{1,5},{2,0},{3,7},{4,6},{5,1},{6,4},{7,3},{8,10},{9,13},{10,... | collective-permute-start | bytes 3145736 | tf_op jit(solution)/shard_map/ppermute | solution.py:114
  96.5 1.4 constant_dynamic-update-slice_fusion.16.own
  97.8 11.9 %collective-permute-done.2 = bf16[512,1024]{1,0:T(8,128)(2,1)S(1)} collective-permute-done((bf16[512,1024]{1,0:T(8,128)(2,1)S(1)}, bf16[512,1024]{1,0:T(8,128)(2,1)S(1)}, u32[]{:S(2)}, u32[]{:S(2)}) %collective-permute-start.2) | collective-permute-done | bytes 1048608 | tf_op jit(solution)/shard_map/ppermute | solution.py:114
  110.5 1.6 %collective-permute-start.5 = (bf16[64,384]{1,0:T(8,128)(2,1)S(1)}, bf16[64,384]{1,0:T(8,128)(2,1)S(1)}, u32[]{:S(2)}, u32[]{:S(2)}) collective-permute-start(bf16[64,384]{1,0:T(8,128)(2,1)S(1)} %get-tuple-element.30), channel_id=1, source_target_pairs={{0,4},{1,5},{2,6},{3,7},{4,0},{5,1},{6,2},{7,3},{8,12},{9,13},{10,... | collective-permute-start | bytes 147464 | tf_op jit(solution)/shard_map/ppermute | solution.py:114
  112.0 2.8 %collective-permute-start.6 = (bf16[64,384]{1,0:T(8,128)(2,1)S(1)}, bf16[64,384]{1,0:T(8,128)(2,1)S(1)}, u32[]{:S(2)}, u32[]{:S(2)}) collective-permute-start(bf16[64,384]{1,0:T(8,128)(2,1)S(1)} %get-tuple-element.29), channel_id=1, source_target_pairs={{0,12},{1,13},{2,14},{3,15},{4,8},{5,9},{6,10},{7,11},{8,4},{9,5},... | collective-permute-start | bytes 147464 | tf_op jit(solution)/shard_map/ppermute | solution.py:114
  114.9 1.1 collective-permute-done.4
  116.0 2.0 %collective-permute-done.6 = bf16[64,384]{1,0:T(8,128)(2,1)S(1)} collective-permute-done((bf16[64,384]{1,0:T(8,128)(2,1)S(1)}, bf16[64,384]{1,0:T(8,128)(2,1)S(1)}, u32[]{:S(2)}, u32[]{:S(2)}) %collective-permute-start.6) | collective-permute-done | bytes 49184 | tf_op jit(solution)/shard_map/ppermute | solution.py:114
  118.0 1.6 %collective-permute-start.7 = (bf16[256,384]{1,0:T(8,128)(2,1)S(1)}, bf16[256,384]{1,0:T(8,128)(2,1)S(1)}, u32[]{:S(2)}, u32[]{:S(2)}) collective-permute-start(bf16[256,384]{1,0:T(8,128)(2,1)S(1)} %pad_maximum_fusion.5), channel_id=1, source_target_pairs={{0,2},{1,3},{2,0},{3,1},{4,6},{5,7},{6,4},{7,5},{8,10},{9,11},{10,... | collective-permute-start | bytes 589832 | tf_op jit(solution)/shard_map/ppermute | solution.py:114
  119.7 4.4 %collective-permute-done.7 = bf16[256,384]{1,0:T(8,128)(2,1)S(1)} collective-permute-done((bf16[256,384]{1,0:T(8,128)(2,1)S(1)}, bf16[256,384]{1,0:T(8,128)(2,1)S(1)}, u32[]{:S(2)}, u32[]{:S(2)}) %collective-permute-start.7) | collective-permute-done | bytes 196640 | tf_op jit(solution)/shard_map/ppermute | solution.py:114
  124.2 2.4 %collective-permute-start.12 = (bf16[16,1024]{1,0:T(8,128)(2,1)S(1)}, bf16[16,1024]{1,0:T(8,128)(2,1)S(1)}, u32[]{:S(2)}, u32[]{:S(2)}) collective-permute-start(bf16[16,1024]{1,0:T(8,128)(2,1)S(1)} %get-tuple-element.27), channel_id=1, source_target_pairs={{0,1},{1,2},{2,3},{3,4},{4,5},{5,6},{6,7},{7,8},{8,9},{9,10},{10,1... | collective-permute-start | bytes 98312 | tf_op jit(solution)/shard_map/ppermute | solution.py:266
  126.6 1.3 collective-permute-start.13
  128.6 7.8 %attention.1 = (bf16[160,128]{1,0:T(8,128)(2,1)S(1)}, bf16[160,128]{1,0:T(8,128)(2,1)S(1)}, bf16[160,128]{1,0:T(8,128)(2,1)S(1)}, bf16[160,128]{1,0:T(8,128)(2,1)S(1)}) custom-call(s32[2]{0:T(128)S(1)} %pad_add_fusion.scalars, bf16[1024,1024]{1,0:T(8,128)(2,1)S(1)} %pad_maximum_fusion.own_x, bf16[1024,1024]{1,0:T(8,128)(2,1)} %collective-permute-done.3.other_x, ...), custom_call_target="tpu_custom_call" | custom-call | flops 4000000000 | bytes 8388608 | tf_op jit(solution)/shard_map/attention/pallas_call | solution.py:293
  136.4 4.4 %collective-permute-start.10 = (bf16[160,128]{1,0:T(8,128)(2,1)S(1)}, bf16[160,128]{1,0:T(8,128)(2,1)S(1)}, u32[]{:S(2)}, u32[]{:S(2)}) collective-permute-start(bf16[160,128]{1,0:T(8,128)(2,1)S(1)} %get-tuple-element.11), channel_id=1, source_target_pairs={{0,4},{1,5},{2,6},{3,7},{4,0},{5,1},{6,2},{7,3},{8,12},{9,13},{10,... | collective-permute-start | bytes 122888 | tf_op jit(solution)/shard_map/ppermute | solution.py:114
  140.8 1.3 collective-permute-start.11
  142.8 3.8 %collective-permute-done.11.c3 = bf16[160,128]{1,0:T(8,128)(2,1)S(1)} collective-permute-done((bf16[160,128]{1,0:T(8,128)(2,1)S(1)}, bf16[160,128]{1,0:T(8,128)(2,1)S(1)}, u32[]{:S(2)}, u32[]{:S(2)}) %collective-permute-start.11) | collective-permute-done | bytes 40992 | tf_op jit(solution)/shard_map/ppermute | solution.py:114
  146.6 0.9 collective-permute-done.9.c1
  147.5 5.6 %tail.1 = bf16[128,1024]{1,0:T(8,128)(2,1)} custom-call(s32[2]{0:T(128)S(1)} %pad_add_fusion.scalars, bf16[160,128]{1,0:T(8,128)(2,1)S(1)} %get-tuple-element.9.c0, bf16[160,128]{1,0:T(8,128)(2,1)S(1)} %collective-permute-done.9.c1, bf16[160,128]{1,0:T(8,128)(2,1)S(1)} %collective-permute-done.10.c2, bf16[160,128]{1,0:T(8,128)(2,1)S(1)} %collective-permute-done.11.c3, ...), custom_call_target="tpu_custom_call" | custom-call | flops 1200000000 | bytes 8388608 | tf_op jit(solution)/shard_map/tail/pallas_call | solution.py:316
  (54 shorter events, 3.0 us)
Async XLA Ops:
  0.0 9.3 %copy-start.5 = (bf16[64,2048]{1,0:T(8,128)(2,1)S(1)}, bf16[64,2048]{1,0:T(8,128)(2,1)}, u32[]{:S(2)}) copy-start(bf16[64,2048]{1,0:T(8,128)(2,1)} %param.17) | copy-start | bytes 786436
  0.0 9.9 %copy-start.6 = (bf16[64,1024]{1,0:T(8,128)(2,1)S(1)}, bf16[64,1024]{1,0:T(8,128)(2,1)}, u32[]{:S(2)}) copy-start(bf16[64,1024]{1,0:T(8,128)(2,1)} %param.21) | copy-start | bytes 393220
  2.5 32.2 %copy-start.4 = (bf16[128,1024]{1,0:T(8,128)(2,1)S(1)}, bf16[128,1024]{1,0:T(8,128)(2,1)}, u32[]{:S(2)}) copy-start(bf16[128,1024]{1,0:T(8,128)(2,1)} %param.11) | copy-start | bytes 786436
  5.2 27.3 %collective-permute-start.14 = (bf16[224,1024]{1,0:T(8,128)(2,1)S(1)}, bf16[224,1024]{1,0:T(8,128)(2,1)S(1)}, u32[]{:S(2)}, u32[]{:S(2)}) collective-permute-start(bf16[224,1024]{1,0:T(8,128)(2,1)S(1)} %pad_maximum_fusion.3), channel_id=1, source_target_pairs={{0,8},{1,3},{2,10},{3,1},{4,12},{5,7},{6,14},{7,5},{8,0},{9,11},{1... | collective-permute-start | bytes 1376264 | tf_op jit(solution)/shard_map/ppermute | solution.py:114
  33.5 31.6 %copy-start.8 = (f32[1024]{0:T(1024)S(1)}, f32[1024]{0:T(1024)}, u32[]{:S(2)}) copy-start(f32[1024]{0:T(1024)} %param.13) | copy-start | bytes 12292
  33.5 28.3 %collective-permute-start.15 = (bf16[448,1024]{1,0:T(8,128)(2,1)S(1)}, bf16[448,1024]{1,0:T(8,128)(2,1)S(1)}, u32[]{:S(2)}, u32[]{:S(2)}) collective-permute-start(bf16[448,1024]{1,0:T(8,128)(2,1)S(1)} %get-tuple-element.19), channel_id=1, source_target_pairs={{0,4},{1,9},{2,6},{3,11},{4,0},{5,13},{6,2},{7,15},{8,12},{9,1},{1... | collective-permute-start | bytes 2752520 | tf_op jit(solution)/shard_map/ppermute | solution.py:114
  63.0 33.5 %collective-permute-start.16 = (bf16[896,1024]{1,0:T(8,128)(2,1)S(1)}, bf16[896,1024]{1,0:T(8,128)(2,1)S(1)}, u32[]{:S(2)}, u32[]{:S(2)}) collective-permute-start(bf16[896,1024]{1,0:T(8,128)(2,1)S(1)} %get-tuple-element.15), channel_id=1, source_target_pairs={{0,2},{1,5},{2,0},{3,7},{4,6},{5,1},{6,4},{7,3},{8,10},{9,13},{10,... | collective-permute-start | bytes 5505032 | tf_op jit(solution)/shard_map/ppermute | solution.py:114
  65.3 14.5 %collective-permute-start = (bf16[128,1024]{1,0:T(8,128)(2,1)S(1)}, bf16[128,1024]{1,0:T(8,128)(2,1)S(1)}, u32[]{:S(2)}, u32[]{:S(2)}) collective-permute-start(bf16[128,1024]{1,0:T(8,128)(2,1)S(1)} %fusion.4), channel_id=1, source_target_pairs={{0,8},{1,3},{2,10},{3,1},{4,12},{5,7},{6,14},{7,5},{8,0},{9,11},{1... | collective-permute-start | bytes 786440 | tf_op jit(solution)/shard_map/ppermute | solution.py:114
  79.9 14.9 %collective-permute-start.1 = (bf16[256,1024]{1,0:T(8,128)(2,1)S(1)}, bf16[256,1024]{1,0:T(8,128)(2,1)S(1)}, u32[]{:S(2)}, u32[]{:S(2)}) collective-permute-start(bf16[256,1024]{1,0:T(8,128)(2,1)S(1)} %pad_maximum_fusion.2), channel_id=1, source_target_pairs={{0,4},{1,9},{2,6},{3,11},{4,0},{5,13},{6,2},{7,15},{8,12},{9,1},{1... | collective-permute-start | bytes 1572872 | tf_op jit(solution)/shard_map/ppermute | solution.py:114
  94.9 14.9 %collective-permute-start.2 = (bf16[512,1024]{1,0:T(8,128)(2,1)S(1)}, bf16[512,1024]{1,0:T(8,128)(2,1)S(1)}, u32[]{:S(2)}, u32[]{:S(2)}) collective-permute-start(bf16[512,1024]{1,0:T(8,128)(2,1)S(1)} %pad_maximum_fusion.1), channel_id=1, source_target_pairs={{0,2},{1,5},{2,0},{3,7},{4,6},{5,1},{6,4},{7,3},{8,10},{9,13},{10,... | collective-permute-start | bytes 3145736 | tf_op jit(solution)/shard_map/ppermute | solution.py:114
  97.8 12.2 %copy-start.7 = (bf16[64,1536]{1,0:T(8,128)(2,1)S(1)}, bf16[64,1536]{1,0:T(8,128)(2,1)}, u32[]{:S(2)}) copy-start(bf16[64,1536]{1,0:T(8,128)(2,1)} %param.14) | copy-start | bytes 589828
  97.8 49.6 %collective-permute-start.17 = (bf16[1792,1024]{1,0:T(8,128)(2,1)}, bf16[1792,1024]{1,0:T(8,128)(2,1)}, u32[]{:S(2)}, u32[]{:S(2)}) collective-permute-start(bf16[1792,1024]{1,0:T(8,128)(2,1)} %constant_dynamic-update-slice_fusion.16.own), channel_id=1, source_target_pairs={{0,1},{1,0},{2,3},{3,2},{4,5},{5,4},{6,7},{7,6},{8,9},{9,8},{10,11... | collective-permute-start | bytes 11010056 | tf_op jit(solution)/shard_map/ppermute | solution.py:114
  109.9 18.7 %collective-permute-start.3 = (bf16[1024,1024]{1,0:T(8,128)(2,1)S(1)}, bf16[1024,1024]{1,0:T(8,128)(2,1)}, u32[]{:S(2)}, u32[]{:S(2)}) collective-permute-start(bf16[1024,1024]{1,0:T(8,128)(2,1)S(1)} %pad_maximum_fusion.own_x), channel_id=1, source_target_pairs={{0,1},{1,0},{2,3},{3,2},{4,5},{5,4},{6,7},{7,6},{8,9},{9,8},{10,11... | collective-permute-start | bytes 6291464 | tf_op jit(solution)/shard_map/ppermute | solution.py:114
  110.4 5.6 %collective-permute-start.4 = (bf16[64,384]{1,0:T(8,128)(2,1)S(1)}, bf16[64,384]{1,0:T(8,128)(2,1)S(1)}, u32[]{:S(2)}, u32[]{:S(2)}) collective-permute-start(bf16[64,384]{1,0:T(8,128)(2,1)S(1)} %get-tuple-element.31), channel_id=1, source_target_pairs={{0,8},{1,9},{2,10},{3,11},{4,12},{5,13},{6,14},{7,15},{8,0},{9,1},... | collective-permute-start | bytes 147464 | tf_op jit(solution)/shard_map/ppermute | solution.py:114
  110.5 5.5 %collective-permute-start.5 = (bf16[64,384]{1,0:T(8,128)(2,1)S(1)}, bf16[64,384]{1,0:T(8,128)(2,1)S(1)}, u32[]{:S(2)}, u32[]{:S(2)}) collective-permute-start(bf16[64,384]{1,0:T(8,128)(2,1)S(1)} %get-tuple-element.30), channel_id=1, source_target_pairs={{0,4},{1,5},{2,6},{3,7},{4,0},{5,1},{6,2},{7,3},{8,12},{9,13},{10,... | collective-permute-start | bytes 147464 | tf_op jit(solution)/shard_map/ppermute | solution.py:114
  112.0 5.9 %collective-permute-start.6 = (bf16[64,384]{1,0:T(8,128)(2,1)S(1)}, bf16[64,384]{1,0:T(8,128)(2,1)S(1)}, u32[]{:S(2)}, u32[]{:S(2)}) collective-permute-start(bf16[64,384]{1,0:T(8,128)(2,1)S(1)} %get-tuple-element.29), channel_id=1, source_target_pairs={{0,12},{1,13},{2,14},{3,15},{4,8},{5,9},{6,10},{7,11},{8,4},{9,5},... | collective-permute-start | bytes 147464 | tf_op jit(solution)/shard_map/ppermute | solution.py:114
  118.0 6.0 %collective-permute-start.7 = (bf16[256,384]{1,0:T(8,128)(2,1)S(1)}, bf16[256,384]{1,0:T(8,128)(2,1)S(1)}, u32[]{:S(2)}, u32[]{:S(2)}) collective-permute-start(bf16[256,384]{1,0:T(8,128)(2,1)S(1)} %pad_maximum_fusion.5), channel_id=1, source_target_pairs={{0,2},{1,3},{2,0},{3,1},{4,6},{5,7},{6,4},{7,5},{8,10},{9,11},{10,... | collective-permute-start | bytes 589832 | tf_op jit(solution)/shard_map/ppermute | solution.py:114
  124.1 4.5 %collective-permute-start.8 = (bf16[512,384]{1,0:T(8,128)(2,1)S(1)}, bf16[512,384]{1,0:T(8,128)(2,1)S(1)}, u32[]{:S(2)}, u32[]{:S(2)}) collective-permute-start(bf16[512,384]{1,0:T(8,128)(2,1)S(1)} %constant_dynamic-update-slice_fusion.own_w), channel_id=1, source_target_pairs={{0,1},{1,0},{2,3},{3,2},{4,5},{5,4},{6,7},{7,6},{8,9},{9,8},{10,11... | collective-permute-start | bytes 1179656 | tf_op jit(solution)/shard_map/ppermute | solution.py:114
  124.2 18.0 %collective-permute-start.12 = (bf16[16,1024]{1,0:T(8,128)(2,1)S(1)}, bf16[16,1024]{1,0:T(8,128)(2,1)S(1)}, u32[]{:S(2)}, u32[]{:S(2)}) collective-permute-start(bf16[16,1024]{1,0:T(8,128)(2,1)S(1)} %get-tuple-element.27), channel_id=1, source_target_pairs={{0,1},{1,2},{2,3},{3,4},{4,5},{5,6},{6,7},{7,8},{8,9},{9,10},{10,1... | collective-permute-start | bytes 98312 | tf_op jit(solution)/shard_map/ppermute | solution.py:266
  126.6 15.8 %collective-permute-start.13 = (bf16[16,1024]{1,0:T(8,128)(2,1)S(1)}, bf16[16,1024]{1,0:T(8,128)(2,1)S(1)}, u32[]{:S(2)}, u32[]{:S(2)}) collective-permute-start(bf16[16,1024]{1,0:T(8,128)(2,1)S(1)} %get-tuple-element.28), channel_id=1, source_target_pairs={{1,0},{2,1},{3,2},{4,3},{5,4},{6,5},{7,6},{8,7},{9,8},{10,9},{11,1... | collective-permute-start | bytes 98312 | tf_op jit(solution)/shard_map/ppermute | solution.py:267
  128.6 18.9 %copy-start = (f32[9,1024]{1,0:T(8,128)S(1)}, f32[9,1024]{1,0:T(8,128)}, u32[]{:S(2)}) copy-start(f32[9,1024]{1,0:T(8,128)} %taps.1) | copy-start | bytes 110596
  128.6 18.9 %copy-start.1 = (f32[1024]{0:T(1024)S(1)}, f32[1024]{0:T(1024)}, u32[]{:S(2)}) copy-start(f32[1024]{0:T(1024)} %param.16) | copy-start | bytes 12292
  128.6 18.9 %copy-start.2 = (f32[1024]{0:T(1024)S(1)}, f32[1024]{0:T(1024)}, u32[]{:S(2)}) copy-start(f32[1024]{0:T(1024)} %param.19) | copy-start | bytes 12292
  128.6 18.9 %copy-start.3 = (f32[1024]{0:T(1024)S(1)}, f32[1024]{0:T(1024)}, u32[]{:S(2)}) copy-start(f32[1024]{0:T(1024)} %param.20) | copy-start | bytes 12292
  136.4 6.4 %collective-permute-start.10 = (bf16[160,128]{1,0:T(8,128)(2,1)S(1)}, bf16[160,128]{1,0:T(8,128)(2,1)S(1)}, u32[]{:S(2)}, u32[]{:S(2)}) collective-permute-start(bf16[160,128]{1,0:T(8,128)(2,1)S(1)} %get-tuple-element.11), channel_id=1, source_target_pairs={{0,4},{1,5},{2,6},{3,7},{4,0},{5,1},{6,2},{7,3},{8,12},{9,13},{10,... | collective-permute-start | bytes 122888 | tf_op jit(solution)/shard_map/ppermute | solution.py:114
  140.8 5.8 %collective-permute-start.11 = (bf16[160,128]{1,0:T(8,128)(2,1)S(1)}, bf16[160,128]{1,0:T(8,128)(2,1)S(1)}, u32[]{:S(2)}, u32[]{:S(2)}) collective-permute-start(bf16[160,128]{1,0:T(8,128)(2,1)S(1)} %get-tuple-element.12), channel_id=1, source_target_pairs={{0,12},{1,13},{2,14},{3,15},{4,8},{5,9},{6,10},{7,11},{8,4},{9,5},... | collective-permute-start | bytes 122888 | tf_op jit(solution)/shard_map/ppermute | solution.py:114
  142.1 5.3 %collective-permute-start.9 = (bf16[160,128]{1,0:T(8,128)(2,1)S(1)}, bf16[160,128]{1,0:T(8,128)(2,1)S(1)}, u32[]{:S(2)}, u32[]{:S(2)}) collective-permute-start(bf16[160,128]{1,0:T(8,128)(2,1)S(1)} %get-tuple-element.10), channel_id=1, source_target_pairs={{0,8},{1,9},{2,10},{3,11},{4,12},{5,13},{6,14},{7,15},{8,0},{9,1},... | collective-permute-start | bytes 122888 | tf_op jit(solution)/shard_map/ppermute | solution.py:114

commit v2 on v1

--- a/solution.py
+++ b/solution.py
@@ -17,6 +17,8 @@
 
 ORDER_EVEN = (8, 4, 2)
 ORDER_ODD = (2, 8, 4)
+PACK_EVEN = (8, 4, 2, 16)
+PACK_ODD = (8, 2, 16, 4)
 ALONG_Z = (0, 8, 4, 12)
 
 
@@ -108,10 +110,13 @@
     return result.astype(jnp.bfloat16)
 
 
-def swap(array, even, odd=None):
+def swap(array, even, odd=None, groups=None):
     odd = even if odd is None else odd
-    pairs = [(i, i ^ (odd if i & 1 else even)) for i in range(16)]
-    return lax.ppermute(array, "frames", pairs)
+    if groups is None:
+        pairs = [(i, i ^ (odd if i & 1 else even)) for i in range(16)]
+        return lax.ppermute(array, "frames", pairs)
+    pairs = [(i, i ^ (odd if i & 1 else even)) for i in range(16 * groups)]
+    return lax.ppermute(array, ("groups", "frames"), pairs)
 
 
 def block_masks(order):
@@ -121,24 +126,52 @@
     return masks
 
 
-def after(arrays, others):
-    joined = lax.optimization_barrier(tuple(arrays) + tuple(others))
-    return joined[: len(arrays)]
-
-
 def source_of(me, j, even, odd, other_core):
     origin = me ^ 1 if other_core else me
     core = origin & 1
     return origin ^ jnp.where(core == 0, even[j], odd[j])
 
 
+def prepare_kernel(
+    scalars, feats_in, gain, w_qkv, w_out, w_pw1, w_pw2, normed, head0, head1, head2, head3, pack, feats, sems
+):
+    me, group = scalars[0], scalars[3]
+    load = pltpu.make_async_copy(feats_in, feats, sems.at[0])
+    load.start()
+    att = w_qkv.shape[1] // 3
+    width = feats.shape[1]
+    copies = []
+    for mask, out in zip(ALONG_Z, (head0, head1, head2, head3)):
+        head = (me ^ mask) // 4
+        for i in range(3):
+            start = pl.multiple_of(i * att + head * HD, HD)
+            copies.append((w_qkv.at[:, pl.ds(start, HD)], out.at[:, i * HD : (i + 1) * HD]))
+    half = pack.shape[0]
+    start = pl.multiple_of(group * half, half)
+    copies.append((w_pw1.at[pl.ds(start, half)], pack.at[:, 0 : 2 * width]))
+    copies.append((w_pw2.at[pl.ds(start, half)], pack.at[:, 2 * width : 3 * width]))
+    side = pl.multiple_of(group * (width // 2), width // 2)
+    copies.append((w_out.at[:, pl.ds(side, width // 2)], pack.at[:, 3 * width :]))
+    copies = [pltpu.make_async_copy(a, b, sems.at[1 + i]) for i, (a, b) in enumerate(copies)]
+    for copy in copies:
+        copy.start()
+    load.wait()
+    values = feats[...].astype(jnp.float32)
+    mean = jnp.mean(values, axis=-1, keepdims=True)
+    centred = values - mean
+    variance = jnp.mean(centred * centred, axis=-1, keepdims=True)
+    normed[...] = (centred * lax.rsqrt(variance + EPSILON) * gain[...]).astype(jnp.bfloat16)
+    for copy in copies:
+        copy.wait()
+
+
 def attention_kernel(
-    scalars, own_x, other_x, own_w, other_w, *refs, rows, even, odd, w_masks, count
+    scalars, xa, xb, xa_other, xb_other, own_w, other_w, *refs, rows, even, odd, w_masks, count
 ):
     outs, (x_all, w_all, keys, values, sems) = refs[:4], refs[4:]
     me, limit = scalars[0], scalars[1]
     depth = w_all.shape[0] // 16
-    for other_core, (xs, ws) in enumerate(((own_x, own_w), (other_x, other_w))):
+    for other_core, (xs, ws) in enumerate((((xa, xb), own_w), ((xa_other, xb_other), other_w))):
         for j in range(8):
             src = source_of(me, j, w_masks, w_masks, other_core)
             pltpu.make_async_copy(
@@ -149,7 +182,7 @@
         for j in range(8):
             src = source_of(me, j, even, odd, other_core)
             pltpu.make_async_copy(
-                xs.at[pl.ds(j * rows, rows)],
+                xs[j // 4].at[pl.ds((j % 4) * rows, rows)],
                 x_all.at[pl.ds(pl.multiple_of(EDGE + src * rows, EDGE), rows)],
                 sems.at[1],
             ).start()
@@ -189,40 +222,78 @@
         out[...] = (summed / totals).astype(jnp.bfloat16)
 
 
+def bit_of(number, position):
+    return (number >> position) & 1
+
+
+def lane_sources(place, lanes, step):
+    block = (lanes % (lanes.shape[1] // 2)) // step
+    other = lanes // (lanes.shape[1] // 2)
+    origin = place ^ other
+    core = origin & 1
+    for i, (even, odd) in enumerate(zip(PACK_EVEN, PACK_ODD)):
+        origin = origin ^ (bit_of(block, i) * jnp.where(core == 0, even, odd))
+    return origin
+
+
 def tail_kernel(
-    scalars, c0, c1, c2, c3, feats, gain, taps, bn_scale, bn_shift, own, other, out,
-    w_out, w_value, w_gate, w_last, wide_gated, sems, *, rows, even, odd, parts
+    scalars, c0, c1, c2, c3, feats, gain, taps, bn_scale, bn_shift, pa, pb, pa_other, pb_other, out,
+    v0, v1, v2, v3, wide_gated, sems, *, rows
 ):
-    me, limit = scalars[0], scalars[1]
-    size = sum(parts)
-    homes = (w_out, w_value, w_gate, w_last)
-    starts = [sum(parts[:i]) for i in range(len(parts))]
-    for i, home in enumerate(homes):
-        for other_core, held in enumerate((own, other)):
-            for j in range(8):
-                src = source_of(me, j, even, odd, other_core)
-                pltpu.make_async_copy(
-                    held.at[pl.ds(j * size + starts[i], parts[i])],
-                    home.at[pl.ds(pl.multiple_of(src * parts[i], parts[i]), parts[i])],
-                    sems.at[i],
-                ).start()
+    me, limit, place = scalars[0], scalars[1], scalars[2]
+    held = (v0, v1, v2, v3)
+    copies = [
+        pltpu.make_async_copy(a, b, sems.at[i])
+        for i, (a, b) in enumerate(zip((pa, pa_other, pb, pb_other), (v0, v2, v1, v3)))
+    ]
+    for copy in copies:
+        copy.start()
     wide = rows + 2 * EDGE
-    attended = feats[...].astype(jnp.float32)
-    head = me // 4
-    pltpu.make_async_copy(w_out, w_out, sems.at[0]).wait()
-    for mask, part in zip(ALONG_Z, (c0, c1, c2, c3)):
-        start = pl.multiple_of((head ^ (mask // 4)) * HD, HD)
-        attended = attended + jnp.dot(
-            part[...], w_out[pl.ds(start, HD), :], preferred_element_type=jnp.float32
-        )
+    width = out.shape[1]
+    quarter = width // 4
+    step = v0.shape[0] // 8
+    lanes = lax.broadcasted_iota(jnp.int32, (1, width), 1)
+    source = lane_sources(place, lanes, step)
+    index = (source & 15) * (2 * step) + (source // 16) * step + lanes % step
+    line = lax.broadcasted_iota(jnp.int32, (width, width), 0)
+    mixing = jnp.where(line == index, 1.0, 0.0).astype(jnp.bfloat16)
+
+    def mixed(array, by):
+        return jnp.dot(array, by, preferred_element_type=jnp.float32).astype(jnp.bfloat16)
+
+    def times(array, start, stop):
+        total = None
+        for i, part in enumerate(held):
+            term = jnp.dot(
+                array[:, i * quarter : (i + 1) * quarter],
+                part[:, start:stop],
+                preferred_element_type=jnp.float32,
+            )
+            total = term if total is None else total + term
+        return total
+
+    row_out = (source & 15) * step + lanes % step
+    side = source // 16
+    heads = [((me ^ mask) // 4) for mask in ALONG_Z]
+    halves = []
+    spreads = [0.0, 0.0]
+    small = lax.broadcasted_iota(jnp.int32, (HD, width), 0)
+    for head, part in zip(heads, (c0, c1, c2, c3)):
+        for h in range(2):
+            by = jnp.where((small + head * HD == row_out) & (side == h), 1.0, 0.0).astype(jnp.bfloat16)
+            spreads[h] = spreads[h] + jnp.dot(part[...], by, preferred_element_type=jnp.float32)
+    for copy in copies:
+        copy.wait()
+    for h in range(2):
+        halves.append(times(spreads[h].astype(jnp.bfloat16), 3 * width, 3 * width + width // 2))
+    attended = feats[...].astype(jnp.float32) + jnp.concatenate(halves, axis=1)
     mean = jnp.mean(attended, axis=-1, keepdims=True)
     centred = attended - mean
     variance = jnp.mean(centred * centred, axis=-1, keepdims=True)
     normed2 = (centred * lax.rsqrt(variance + EPSILON) * gain[...]).astype(jnp.bfloat16)
-    pltpu.make_async_copy(w_value, w_value, sems.at[1]).wait()
-    value = jnp.dot(normed2, w_value[...], preferred_element_type=jnp.float32)
-    pltpu.make_async_copy(w_gate, w_gate, sems.at[2]).wait()
-    gate = jnp.dot(normed2, w_gate[...], preferred_element_type=jnp.float32)
+    normed2 = mixed(normed2, mixing)
+    value = times(normed2, 0, width)
+    gate = times(normed2, width, 2 * width)
     frame = me * rows - EDGE + lax.broadcasted_iota(jnp.int32, (wide, 1), 0)
     inside = (frame >= 0) & (frame < limit)
     gated = jnp.where(inside, value * jax.nn.sigmoid(gate), 0.0)
@@ -234,10 +305,7 @@
         conv = conv + taps[tap : tap + 1, :] * wide_gated[at : at + rows, :]
     act = bn_scale[...] * conv + bn_shift[...]
     activated = (act * jax.nn.sigmoid(act)).astype(jnp.bfloat16)
-    pltpu.make_async_copy(w_last, w_last, sems.at[3]).wait()
-    result = attended[EDGE : EDGE + rows, :] + jnp.dot(
-        activated, w_last[...], preferred_element_type=jnp.float32
-    )
+    result = attended[EDGE : EDGE + rows, :] + times(mixed(activated, mixing), 2 * width, 3 * width)
     out[...] = result.astype(jnp.bfloat16)
 
 
@@ -248,55 +316,68 @@
     count = rows * 16
     depth = w_qkv.shape[0]
     me = lax.axis_index("frames")
-    z = me // 4
-    scalars = jnp.stack([me.astype(jnp.int32), valid_length[0]])
+    group = lax.axis_index("groups")
+    groups = lax.axis_size("groups")
+    scalars = jnp.stack([me, valid_length[0], 16 * group + me, group]).astype(jnp.int32)
     even, odd = block_masks(ORDER_EVEN), block_masks(ORDER_ODD)
-
-    normed1 = layer_norm(features, ln1_gain)
-    by_head = w_qkv.reshape(depth, 3, HEADS, HD).transpose(2, 0, 1, 3).reshape(HEADS, depth, 3 * HD)
-    pack = jnp.concatenate([w_out, w_pw1[:, :width], w_pw1[:, width:], w_pw2], axis=0)
-    parts = (w_out.shape[0], depth, depth, depth)
-
-    x1 = swap(normed1, ORDER_EVEN[0], ORDER_ODD[0])
-    w_z = [
-        swap(lax.dynamic_index_in_dim(by_head, z ^ (mask // 4), 0, keepdims=False), mask)
-        for mask in ALONG_Z[1:]
-    ]
-    w_mine = lax.dynamic_index_in_dim(by_head, z, 0, keepdims=False)
+    any_spec = pl.BlockSpec(memory_space=pl.ANY)
+    hbm = pl.BlockSpec(memory_space=pltpu.HBM)
+    smem = pl.BlockSpec(memory_space=pltpu.SMEM)
+    vmem = pl.BlockSpec(memory_space=pltpu.VMEM)
+
+    normed1, w_mine, w_8, w_4, w_12, pack = pl.pallas_call(
+        prepare_kernel,
+        name="prepare",
+        out_shape=[jax.ShapeDtypeStruct((rows, width), jnp.bfloat16)]
+        + [jax.ShapeDtypeStruct((depth, 3 * HD), jnp.bfloat16)] * 4
+        + [jax.ShapeDtypeStruct((depth // 2, 3 * width + width // 2), jnp.bfloat16)],
+        in_specs=[smem, hbm, vmem] + [hbm] * 4,
+        out_specs=[vmem] * 6,
+        scratch_shapes=[
+            pltpu.VMEM((rows, width), jnp.bfloat16),
+            pltpu.SemaphoreType.DMA((16,)),
+        ],
+        compiler_params=pltpu.CompilerParams(vmem_limit_bytes=16 << 20),
+    )(scalars, features, ln1_gain.reshape(1, -1), w_qkv, w_out, w_pw1, w_pw2)
+
+    def joined(*arrays):
+        return lax.optimization_barrier(jnp.concatenate(arrays, axis=0))
+
+    def pack_swap(held, stage):
+        return swap(held, PACK_EVEN[stage], PACK_ODD[stage], groups)
+
     ahead = lax.ppermute(features[-EDGE:], "frames", [(i, i + 1) for i in range(15)])
     behind = lax.ppermute(features[:EDGE], "frames", [(i + 1, i) for i in range(15)])
-    p1 = swap(pack, ORDER_EVEN[0], ORDER_ODD[0])
-    x = jnp.concatenate([normed1, x1], axis=0)
-    w4 = jnp.concatenate([w_mine] + w_z, axis=0)
-    pack = jnp.concatenate([pack, p1], axis=0)
-
-    x2 = swap(x, ORDER_EVEN[1], ORDER_ODD[1])
-    w2 = swap(w4, 2)
-    p2 = swap(pack, ORDER_EVEN[1], ORDER_ODD[1])
-    x = jnp.concatenate([x, x2], axis=0)
-    w8 = jnp.concatenate([w4, w2], axis=0)
-    pack = jnp.concatenate([pack, p2], axis=0)
-
-    x3 = swap(x, ORDER_EVEN[2], ORDER_ODD[2])
+    x1 = swap(normed1, ORDER_EVEN[0], ORDER_ODD[0])
+    w_z = [swap(part, mask) for part, mask in zip((w_8, w_4, w_12), ALONG_Z[1:])]
+    p2 = joined(pack, pack_swap(pack, 0))
+    x2 = joined(normed1, x1)
+    w4 = joined(w_mine, *w_z)
+    x2, w4, ahead, behind = lax.optimization_barrier((x2, w4, ahead, behind))
+
+    w8 = joined(w4, swap(w4, 2))
+    p4 = joined(p2, pack_swap(p2, 1))
+    xa = joined(x2, swap(x2, ORDER_EVEN[1], ORDER_ODD[1]))
+    xa, w8 = lax.optimization_barrier((xa, w8))
+
+    xb = swap(xa, ORDER_EVEN[2], ORDER_ODD[2])
+    xa_other = swap(xa, 1)
     w_other = swap(w8, 1)
-    x = jnp.concatenate([x, x3], axis=0)
-    x_other = swap(x, 1)
-    p3 = swap(pack, ORDER_EVEN[2], ORDER_ODD[2])
-    pack = jnp.concatenate([pack, p3], axis=0)
-    pack_other = swap(pack, 1)
+    pa = joined(p4, pack_swap(p4, 2))
+    xb, xa_other, w_other = lax.optimization_barrier((xb, xa_other, w_other))
+    xb_other = swap(xb, 1)
+    pb = pack_swap(pa, 3)
+    pa_other = swap(pa, 1)
 
     wide = rows + 2 * EDGE
     w_masks = block_masks((8, 4, 2))
-    any_spec = pl.BlockSpec(memory_space=pl.ANY)
-    smem = pl.BlockSpec(memory_space=pltpu.SMEM)
-    vmem = pl.BlockSpec(memory_space=pltpu.VMEM)
     contexts = pl.pallas_call(
         functools.partial(
             attention_kernel, rows=rows, even=even, odd=odd, w_masks=w_masks, count=count
         ),
         name="attention",
         out_shape=[jax.ShapeDtypeStruct((wide, HD), jnp.bfloat16)] * 4,
-        in_specs=[smem] + [any_spec] * 4,
+        in_specs=[smem] + [any_spec] * 6,
         out_specs=[vmem] * 4,
         scratch_shapes=[
             pltpu.VMEM((count + 2 * EDGE, width), jnp.bfloat16),
@@ -307,23 +388,25 @@
         ],
         compiler_params=pltpu.CompilerParams(vmem_limit_bytes=40 << 20),
         cost_estimate=pl.CostEstimate(
-            flops=4_000_000_000, bytes_accessed=8 << 20, transcendentals=4 * wide * count
+            flops=5_000_000_000, bytes_accessed=8 << 20, transcendentals=4 * wide * count
         ),
-    )(scalars, x, x_other, w8, w_other)
+    )(scalars, xa, xb, xa_other, xb_other, w8, w_other)
+    pb, contexts = lax.optimization_barrier((pb, contexts))
+    pb_other = swap(pb, 1)
     mine = [contexts[0]] + [swap(part, mask) for part, mask in zip(contexts[1:], ALONG_Z[1:])]
 
     feats = jnp.concatenate([ahead, features, behind], axis=0)
     return pl.pallas_call(
-        functools.partial(tail_kernel, rows=rows, even=even, odd=odd, parts=parts),
+        functools.partial(tail_kernel, rows=rows),
         name="tail",
         out_shape=jax.ShapeDtypeStruct((rows, width), jnp.bfloat16),
-        in_specs=[smem] + [vmem] * 9 + [any_spec] * 2,
+        in_specs=[smem] + [vmem] * 9 + [any_spec] * 4,
         out_specs=vmem,
         scratch_shapes=[
-            pltpu.VMEM((16 * parts[0], width), jnp.bfloat16),
-            pltpu.VMEM((16 * depth, width), jnp.bfloat16),
-            pltpu.VMEM((16 * depth, width), jnp.bfloat16),
-            pltpu.VMEM((16 * depth, width), jnp.bfloat16),
+            pltpu.VMEM(pa.shape, jnp.bfloat16),
+            pltpu.VMEM(pa.shape, jnp.bfloat16),
+            pltpu.VMEM(pa.shape, jnp.bfloat16),
+            pltpu.VMEM(pa.shape, jnp.bfloat16),
             pltpu.VMEM((wide, width), jnp.float32),
             pltpu.SemaphoreType.DMA((4,)),
         ],
@@ -339,8 +422,10 @@
         w_dw,
         bn_scale.reshape(1, -1),
         bn_shift.reshape(1, -1),
-        pack,
-        pack_other,
+        pa,
+        pb,
+        pa_other,
+        pb_other,
     )
 
 
@@ -359,7 +444,7 @@
         P("frames", None),
     )
     return jax.shard_map(
-        per_device if mesh.shape["frames"] == 16 else per_device_general,
+        per_device if (mesh.shape["groups"], mesh.shape["frames"]) == (2, 16) else per_device_general,
         mesh=mesh,
         in_specs=placed,
         out_specs=P(("groups", "frames"), None),

time: 153 us -> 108 us (0.71)
  waiting for transfers between devices: 101 us -> 45.8 us
  starting transfers between devices: 26.2 us -> 40.7 us
  local copies, waits for them, and re-layouts: 9.63 us -> 5.29 us
    ppermute x16 -> x15, waiting for transfers between devices: 101 us -> 34.4 us  [swap(): return lax.ppermute(array, 'frames', pairs)]
    ppermute x0 -> x4, waiting for transfers between devices: none -> 11.4 us  [swap(): return lax.ppermute(array, ('groups', 'frames'), pairs)]
    ppermute x0 -> x4, starting transfers between devices: none -> 8.03 us  [swap(): return lax.ppermute(array, ('groups', 'frames'), pairs)]
    ppermute x16 -> x15, starting transfers between devices: 22.5 us -> 29.8 us  [swap(): return lax.ppermute(array, 'frames', pairs)]
    concatenate x3 -> x0, local copies, waits for them, and re-layouts: 2.66 us -> none  [the longest x1 1.39 us: per_device(): pack = jnp.concatenate([pack, p3], axis=0)]
    pallas_call x1 -> x2, Pallas kernels: 5.64 us -> 7.63 us  [the longest x1 6.5 us: per_device(): pl.pallas_call(functools.partial(tail_kernel, rows=rows), name='tail', ou...]
    unnamed x28 -> x22, local copies, waits for them, and re-layouts: 6.61 us -> 5.29 us
  transfers between devices with their start and end apart: 18 -> 21, of which waited for: 11 -> 11; matrix products, arithmetic and copies ran while one was open for 3% -> 0% of each run, Pallas kernels for 5% -> 6%
where the time goes in v2:
time: 108 us; the launch traced here: 107 us
  waiting for transfers between devices  45.8 us (42%)
  starting transfers between devices  40.7 us (38%)
  Pallas kernels  14.1 us (13%)
  local copies, waits for them, and re-layouts  5.29 us (5%)
    ppermute x15, waiting for transfers between devices, swap(): return lax.ppermute(array, 'frames', pairs)  34.4 us
    ppermute x15, starting transfers between devices, swap(): return lax.ppermute(array, 'frames', pairs)  29.8 us
    ppermute x4, waiting for transfers between devices, swap(): return lax.ppermute(array, ('groups', 'frames'), pairs)  11.4 us
    ppermute x4, starting transfers between devices, swap(): return lax.ppermute(array, ('groups', 'frames'), pairs)  8.03 us
    pallas_call x1, Pallas kernels, per_device(): pl.pallas_call(functools.partial(tail_kernel, rows=rows), name='tail', ou...  6.5 us
    pallas_call x1, Pallas kernels, per_device(): pl.pallas_call(functools.partial(attention_kernel, rows=rows, even=even,...  6.43 us
    unnamed x22, local copies, waits for them, and re-layouts  5.29 us
  transfers between devices with their start and end apart: 21, of which 11 were waited for; matrix products, arithmetic and copies ran while one was open for 0% of the time, Pallas kernels for 6%

profile of v2, /device:TPU:0, one launch (start us, length us, event | category | flops | bytes accessed | tf_op | source)
XLA Modules:
  0.0 107.2 jit_solution(14310013635771788630)
XLA Ops:
  0.7 0.9 copy-done
  1.7 0.9 copy-done.2
  2.6 0.9 copy-done.3
  3.6 0.9 copy-done.4
  6.0 1.1 %prepare.1 = (bf16[128,1024]{1,0:T(8,128)(2,1)S(1)}, bf16[64,384]{1,0:T(8,128)(2,1)S(1)}, bf16[64,384]{1,0:T(8,128)(2,1)S(1)}, bf16[64,384]{1,0:T(8,128)(2,1)S(1...) custom-call(s32[4]{0:T(128)S(1)} %pad_add_fusion.scalars, bf16[128,1024]{1,0:T(8,128)(2,1)S(1)} %copy-done, ...), custom_call_target="tpu_custom_call" | custom-call | tf_op jit(solution)/shard_map/prepare/pallas_call | solution.py:328
  7.1 4.1 %collective-permute-start = (bf16[32,3584]{1,0:T(8,128)(2,1)S(1)}, bf16[32,3584]{1,0:T(8,128)(2,1)S(1)}, u32[]{:S(2)}, u32[]{:S(2)}) collective-permute-start(bf16[32,3584]{1,0:T(8,128)(2,1)S(1)} %get-tuple-element.29), channel_id=1, source_target_pairs={{0,8},{1,9},{2,10},{3,11},{4,12},{5,13},{6,14},{7,15},{8,0},{9,1},... | collective-permute-start | bytes 688136 | tf_op jit(solution)/shard_map/ppermute | solution.py:119
  11.2 10.5 %collective-permute-done = bf16[32,3584]{1,0:T(8,128)(2,1)S(1)} collective-permute-done((bf16[32,3584]{1,0:T(8,128)(2,1)S(1)}, bf16[32,3584]{1,0:T(8,128)(2,1)S(1)}, u32[]{:S(2)}, u32[]{:S(2)}) %collective-permute-start) | collective-permute-done | bytes 229408 | tf_op jit(solution)/shard_map/ppermute | solution.py:119
  22.6 3.4 %collective-permute-start.5 = (bf16[64,384]{1,0:T(8,128)(2,1)S(1)}, bf16[64,384]{1,0:T(8,128)(2,1)S(1)}, u32[]{:S(2)}, u32[]{:S(2)}) collective-permute-start(bf16[64,384]{1,0:T(8,128)(2,1)S(1)} %get-tuple-element.32), channel_id=1, source_target_pairs={{0,8},{1,9},{2,10},{3,11},{4,12},{5,13},{6,14},{7,15},{8,0},{9,1},... | collective-permute-start | bytes 147464 | tf_op jit(solution)/shard_map/ppermute | solution.py:117
  26.0 1.4 %collective-permute-start.7 = (bf16[64,384]{1,0:T(8,128)(2,1)S(1)}, bf16[64,384]{1,0:T(8,128)(2,1)S(1)}, u32[]{:S(2)}, u32[]{:S(2)}) collective-permute-start(bf16[64,384]{1,0:T(8,128)(2,1)S(1)} %get-tuple-element.34), channel_id=1, source_target_pairs={{0,12},{1,13},{2,14},{3,15},{4,8},{5,9},{6,10},{7,11},{8,4},{9,5},... | collective-permute-start | bytes 147464 | tf_op jit(solution)/shard_map/ppermute | solution.py:117
  27.4 1.3 %collective-permute-start.9 = (bf16[16,1024]{1,0:T(8,128)(2,1)S(1)}, bf16[16,1024]{1,0:T(8,128)(2,1)S(1)}, u32[]{:S(2)}, u32[]{:S(2)}) collective-permute-start(bf16[16,1024]{1,0:T(8,128)(2,1)S(1)} %get-tuple-element.53), channel_id=1, source_target_pairs={{1,0},{2,1},{3,2},{4,3},{5,4},{6,5},{7,6},{8,7},{9,8},{10,9},{11,1... | collective-permute-start | bytes 98312 | tf_op jit(solution)/shard_map/ppermute | solution.py:350
  28.7 1.4 %collective-permute-done.5 = bf16[64,384]{1,0:T(8,128)(2,1)S(1)} collective-permute-done((bf16[64,384]{1,0:T(8,128)(2,1)S(1)}, bf16[64,384]{1,0:T(8,128)(2,1)S(1)}, u32[]{:S(2)}, u32[]{:S(2)}) %collective-permute-start.5) | collective-permute-done | bytes 49184 | tf_op jit(solution)/shard_map/ppermute | solution.py:117
  30.1 1.6 %collective-permute-start.8 = (bf16[16,1024]{1,0:T(8,128)(2,1)S(1)}, bf16[16,1024]{1,0:T(8,128)(2,1)S(1)}, u32[]{:S(2)}, u32[]{:S(2)}) collective-permute-start(bf16[16,1024]{1,0:T(8,128)(2,1)S(1)} %get-tuple-element.54), channel_id=1, source_target_pairs={{0,1},{1,2},{2,3},{3,4},{4,5},{5,6},{6,7},{7,8},{8,9},{9,10},{10,1... | collective-permute-start | bytes 98312 | tf_op jit(solution)/shard_map/ppermute | solution.py:349
  31.8 1.2 %collective-permute-done.6 = bf16[64,384]{1,0:T(8,128)(2,1)S(1)} collective-permute-done((bf16[64,384]{1,0:T(8,128)(2,1)S(1)}, bf16[64,384]{1,0:T(8,128)(2,1)S(1)}, u32[]{:S(2)}, u32[]{:S(2)}) %collective-permute-start.6) | collective-permute-done | bytes 49184 | tf_op jit(solution)/shard_map/ppermute | solution.py:117
  33.0 2.6 %collective-permute-start.4 = (bf16[128,1024]{1,0:T(8,128)(2,1)S(1)}, bf16[128,1024]{1,0:T(8,128)(2,1)S(1)}, u32[]{:S(2)}, u32[]{:S(2)}) collective-permute-start(bf16[128,1024]{1,0:T(8,128)(2,1)S(1)} %get-tuple-element.30), channel_id=1, source_target_pairs={{0,8},{1,3},{2,10},{3,1},{4,12},{5,7},{6,14},{7,5},{8,0},{9,11},{1... | collective-permute-start | bytes 786440 | tf_op jit(solution)/shard_map/ppermute | solution.py:117
  35.6 1.6 %collective-permute-start.2 = (bf16[128,3584]{1,0:T(8,128)(2,1)S(1)}, bf16[128,3584]{1,0:T(8,128)(2,1)S(1)}, u32[]{:S(2)}, u32[]{:S(2)}) collective-permute-start(bf16[128,3584]{1,0:T(8,128)(2,1)S(1)} %pad_maximum_fusion.2), channel_id=1, source_target_pairs={{0,2},{1,17},{2,0},{3,19},{4,6},{5,21},{6,4},{7,23},{8,10},{9,25},... | collective-permute-start | bytes 2752520 | tf_op jit(solution)/shard_map/ppermute | solution.py:119
  37.2 3.0 %collective-permute-done.4 = bf16[128,1024]{1,0:T(8,128)(2,1)S(1)} collective-permute-done((bf16[128,1024]{1,0:T(8,128)(2,1)S(1)}, bf16[128,1024]{1,0:T(8,128)(2,1)S(1)}, u32[]{:S(2)}, u32[]{:S(2)}) %collective-permute-start.4) | collective-permute-done | bytes 262176 | tf_op jit(solution)/shard_map/ppermute | solution.py:117
  40.3 3.6 %collective-permute-start.10 = (bf16[256,1024]{1,0:T(8,128)(2,1)S(1)}, bf16[256,1024]{1,0:T(8,128)(2,1)S(1)}, u32[]{:S(2)}, u32[]{:S(2)}) collective-permute-start(bf16[256,1024]{1,0:T(8,128)(2,1)S(1)} %pad_maximum_fusion.3), channel_id=1, source_target_pairs={{0,4},{1,9},{2,6},{3,11},{4,0},{5,13},{6,2},{7,15},{8,12},{9,1},{1... | collective-permute-start | bytes 1572872 | tf_op jit(solution)/shard_map/ppermute | solution.py:117
  43.9 1.4 %collective-permute-start.11 = (bf16[256,384]{1,0:T(8,128)(2,1)S(1)}, bf16[256,384]{1,0:T(8,128)(2,1)S(1)}, u32[]{:S(2)}, u32[]{:S(2)}) collective-permute-start(bf16[256,384]{1,0:T(8,128)(2,1)S(1)} %pad_maximum_fusion.7), channel_id=1, source_target_pairs={{0,2},{1,3},{2,0},{3,1},{4,6},{5,7},{6,4},{7,5},{8,10},{9,11},{10,... | collective-permute-start | bytes 589832 | tf_op jit(solution)/shard_map/ppermute | solution.py:117
  45.3 10.5 %collective-permute-done.11 = bf16[256,384]{1,0:T(8,128)(2,1)S(1)} collective-permute-done((bf16[256,384]{1,0:T(8,128)(2,1)S(1)}, bf16[256,384]{1,0:T(8,128)(2,1)S(1)}, u32[]{:S(2)}, u32[]{:S(2)}) %collective-permute-start.11) | collective-permute-done | bytes 196640 | tf_op jit(solution)/shard_map/ppermute | solution.py:117
  55.9 2.5 %collective-permute-start.13 = (bf16[512,1024]{1,0:T(8,128)(2,1)S(1)}, bf16[512,1024]{1,0:T(8,128)(2,1)S(1)}, u32[]{:S(2)}, u32[]{:S(2)}) collective-permute-start(bf16[512,1024]{1,0:T(8,128)(2,1)S(1)} %pad_maximum_fusion.1.xa), channel_id=1, source_target_pairs={{0,1},{1,0},{2,3},{3,2},{4,5},{5,4},{6,7},{7,6},{8,9},{9,8},{10,11... | collective-permute-start | bytes 3145736 | tf_op jit(solution)/shard_map/ppermute | solution.py:117
  58.4 1.1 %collective-permute-start.12 = (bf16[512,1024]{1,0:T(8,128)(2,1)S(1)}, bf16[512,1024]{1,0:T(8,128)(2,1)S(1)}, u32[]{:S(2)}, u32[]{:S(2)}) collective-permute-start(bf16[512,1024]{1,0:T(8,128)(2,1)S(1)} %pad_maximum_fusion.1.xa), channel_id=1, source_target_pairs={{0,2},{1,5},{2,0},{3,7},{4,6},{5,1},{6,4},{7,3},{8,10},{9,13},{10,... | collective-permute-start | bytes 3145736 | tf_op jit(solution)/shard_map/ppermute | solution.py:117
  59.9 1.6 %collective-permute-start.3 = (bf16[256,3584]{1,0:T(8,128)(2,1)S(1)}, bf16[256,3584]{1,0:T(8,128)(2,1)S(1)}, u32[]{:S(2)}, u32[]{:S(2)}) collective-permute-start(bf16[256,3584]{1,0:T(8,128)(2,1)S(1)} %pad_maximum_fusion.pa), channel_id=1, source_target_pairs={{0,16},{1,5},{2,18},{3,7},{4,20},{5,1},{6,22},{7,3},{8,24},{9,13},... | collective-permute-start | bytes 5505032 | tf_op jit(solution)/shard_map/ppermute | solution.py:119
  61.5 11.8 %collective-permute-done.12.xb = bf16[512,1024]{1,0:T(8,128)(2,1)S(1)} collective-permute-done((bf16[512,1024]{1,0:T(8,128)(2,1)S(1)}, bf16[512,1024]{1,0:T(8,128)(2,1)S(1)}, u32[]{:S(2)}, u32[]{:S(2)}) %collective-permute-start.12) | collective-permute-done | bytes 1048608 | tf_op jit(solution)/shard_map/ppermute | solution.py:117
  73.7 2.1 %collective-permute-done.15.xb_other = bf16[512,1024]{1,0:T(8,128)(2,1)S(1)} collective-permute-done((bf16[512,1024]{1,0:T(8,128)(2,1)S(1)}, bf16[512,1024]{1,0:T(8,128)(2,1)S(1)}, u32[]{:S(2)}, u32[]{:S(2)}) %collective-permute-start.15) | collective-permute-done | bytes 1048608 | tf_op jit(solution)/shard_map/ppermute | solution.py:117
  75.9 6.4 %attention.1 = (bf16[160,128]{1,0:T(8,128)(2,1)S(1)}, bf16[160,128]{1,0:T(8,128)(2,1)S(1)}, bf16[160,128]{1,0:T(8,128)(2,1)S(1)}, bf16[160,128]{1,0:T(8,128)(2,1)S(1)}) custom-call(s32[4]{0:T(128)S(1)} %pad_add_fusion.scalars, bf16[512,1024]{1,0:T(8,128)(2,1)S(1)} %pad_maximum_fusion.1.xa, bf16[512,1024]{1,0:T(8,128)(2,1)S(1)} %collective-permute-done.12.xb, ...), custom_call_target="tpu_custom_call" | custom-call | flops 5000000000 | bytes 8388608 | tf_op jit(solution)/shard_map/attention/pallas_call | solution.py:374
  83.2 8.6 %collective-permute-start.20 = (bf16[256,3584]{1,0:T(8,128)(2,1)S(1)}, bf16[256,3584]{1,0:T(8,128)(2,1)S(1)}, u32[]{:S(2)}, u32[]{:S(2)}) collective-permute-start(bf16[256,3584]{1,0:T(8,128)(2,1)S(1)} %collective-permute-done.3.pb), channel_id=1, source_target_pairs={{0,1},{1,0},{2,3},{3,2},{4,5},{5,4},{6,7},{7,6},{8,9},{9,8},{10,11... | collective-permute-start | bytes 5505032 | tf_op jit(solution)/shard_map/ppermute | solution.py:117
  91.8 1.6 %collective-permute-start.16 = (bf16[160,128]{1,0:T(8,128)(2,1)S(1)}, bf16[160,128]{1,0:T(8,128)(2,1)S(1)}, u32[]{:S(2)}, u32[]{:S(2)}) collective-permute-start(bf16[160,128]{1,0:T(8,128)(2,1)S(1)} %get-tuple-element.47), channel_id=1, source_target_pairs={{0,8},{1,9},{2,10},{3,11},{4,12},{5,13},{6,14},{7,15},{8,0},{9,1},... | collective-permute-start | bytes 122888 | tf_op jit(solution)/shard_map/ppermute | solution.py:117
  93.5 1.4 %collective-permute-start.17 = (bf16[160,128]{1,0:T(8,128)(2,1)S(1)}, bf16[160,128]{1,0:T(8,128)(2,1)S(1)}, u32[]{:S(2)}, u32[]{:S(2)}) collective-permute-start(bf16[160,128]{1,0:T(8,128)(2,1)S(1)} %get-tuple-element.48), channel_id=1, source_target_pairs={{0,4},{1,5},{2,6},{3,7},{4,0},{5,1},{6,2},{7,3},{8,12},{9,13},{10,... | collective-permute-start | bytes 122888 | tf_op jit(solution)/shard_map/ppermute | solution.py:117
  94.9 1.4 %collective-permute-start.18 = (bf16[160,128]{1,0:T(8,128)(2,1)S(1)}, bf16[160,128]{1,0:T(8,128)(2,1)S(1)}, u32[]{:S(2)}, u32[]{:S(2)}) collective-permute-start(bf16[160,128]{1,0:T(8,128)(2,1)S(1)} %get-tuple-element.49), channel_id=1, source_target_pairs={{0,12},{1,13},{2,14},{3,15},{4,8},{5,9},{6,10},{7,11},{8,4},{9,5},... | collective-permute-start | bytes 122888 | tf_op jit(solution)/shard_map/ppermute | solution.py:117
  96.3 1.1 collective-permute-done.16.c1
  97.6 3.1 %collective-permute-done.18.c3 = bf16[160,128]{1,0:T(8,128)(2,1)S(1)} collective-permute-done((bf16[160,128]{1,0:T(8,128)(2,1)S(1)}, bf16[160,128]{1,0:T(8,128)(2,1)S(1)}, u32[]{:S(2)}, u32[]{:S(2)}) %collective-permute-start.18) | collective-permute-done | bytes 40992 | tf_op jit(solution)/shard_map/ppermute | solution.py:117
  100.7 6.5 %tail.1 = bf16[128,1024]{1,0:T(8,128)(2,1)} custom-call(s32[4]{0:T(128)S(1)} %pad_add_fusion.scalars, bf16[160,128]{1,0:T(8,128)(2,1)S(1)} %get-tuple-element.46.c0, bf16[160,128]{1,0:T(8,128)(2,1)S(1)} %collective-permute-done.16.c1, bf16[160,128]{1,0:T(8,128)(2,1)S(1)} %collective-permute-done.17.c2, bf16[160,128]{1,0:T(8,128)(2,1)S(1)} %collective-permute-done.18.c3, ...), custom_call_target="tpu_custom_call" | custom-call | flops 1200000000 | bytes 8388608 | tf_op jit(solution)/shard_map/tail/pallas_call | solution.py:399
  (45 shorter events, 4.8 us)
Async XLA Ops:
  0.7 1.0 copy-start
  1.7 0.9 copy-start.2
  2.6 0.9 copy-start.3
  3.6 0.9 copy-start.4
  4.5 0.8 copy-start.6
  5.3 0.7 copy-start.7
  7.1 14.6 %collective-permute-start = (bf16[32,3584]{1,0:T(8,128)(2,1)S(1)}, bf16[32,3584]{1,0:T(8,128)(2,1)S(1)}, u32[]{:S(2)}, u32[]{:S(2)}) collective-permute-start(bf16[32,3584]{1,0:T(8,128)(2,1)S(1)} %get-tuple-element.29), channel_id=1, source_target_pairs={{0,8},{1,9},{2,10},{3,11},{4,12},{5,13},{6,14},{7,15},{8,0},{9,1},... | collective-permute-start | bytes 688136 | tf_op jit(solution)/shard_map/ppermute | solution.py:119
  21.8 13.8 %collective-permute-start.1 = (bf16[64,3584]{1,0:T(8,128)(2,1)S(1)}, bf16[64,3584]{1,0:T(8,128)(2,1)S(1)}, u32[]{:S(2)}, u32[]{:S(2)}) collective-permute-start(bf16[64,3584]{1,0:T(8,128)(2,1)S(1)} %pad_maximum_fusion.4), channel_id=1, source_target_pairs={{0,4},{1,3},{2,6},{3,1},{4,0},{5,7},{6,2},{7,5},{8,12},{9,11},{10,... | collective-permute-start | bytes 1376264 | tf_op jit(solution)/shard_map/ppermute | solution.py:119
  22.6 7.6 %collective-permute-start.5 = (bf16[64,384]{1,0:T(8,128)(2,1)S(1)}, bf16[64,384]{1,0:T(8,128)(2,1)S(1)}, u32[]{:S(2)}, u32[]{:S(2)}) collective-permute-start(bf16[64,384]{1,0:T(8,128)(2,1)S(1)} %get-tuple-element.32), channel_id=1, source_target_pairs={{0,8},{1,9},{2,10},{3,11},{4,12},{5,13},{6,14},{7,15},{8,0},{9,1},... | collective-permute-start | bytes 147464 | tf_op jit(solution)/shard_map/ppermute | solution.py:117
  26.0 7.0 %collective-permute-start.6 = (bf16[64,384]{1,0:T(8,128)(2,1)S(1)}, bf16[64,384]{1,0:T(8,128)(2,1)S(1)}, u32[]{:S(2)}, u32[]{:S(2)}) collective-permute-start(bf16[64,384]{1,0:T(8,128)(2,1)S(1)} %get-tuple-element.33), channel_id=1, source_target_pairs={{0,4},{1,5},{2,6},{3,7},{4,0},{5,1},{6,2},{7,3},{8,12},{9,13},{10,... | collective-permute-start | bytes 147464 | tf_op jit(solution)/shard_map/ppermute | solution.py:117
  26.0 9.5 %collective-permute-start.7 = (bf16[64,384]{1,0:T(8,128)(2,1)S(1)}, bf16[64,384]{1,0:T(8,128)(2,1)S(1)}, u32[]{:S(2)}, u32[]{:S(2)}) collective-permute-start(bf16[64,384]{1,0:T(8,128)(2,1)S(1)} %get-tuple-element.34), channel_id=1, source_target_pairs={{0,12},{1,13},{2,14},{3,15},{4,8},{5,9},{6,10},{7,11},{8,4},{9,5},... | collective-permute-start | bytes 147464 | tf_op jit(solution)/shard_map/ppermute | solution.py:117
  27.4 12.9 %collective-permute-start.9 = (bf16[16,1024]{1,0:T(8,128)(2,1)S(1)}, bf16[16,1024]{1,0:T(8,128)(2,1)S(1)}, u32[]{:S(2)}, u32[]{:S(2)}) collective-permute-start(bf16[16,1024]{1,0:T(8,128)(2,1)S(1)} %get-tuple-element.53), channel_id=1, source_target_pairs={{1,0},{2,1},{3,2},{4,3},{5,4},{6,5},{7,6},{8,7},{9,8},{10,9},{11,1... | collective-permute-start | bytes 98312 | tf_op jit(solution)/shard_map/ppermute | solution.py:350
  30.1 10.1 %collective-permute-start.8 = (bf16[16,1024]{1,0:T(8,128)(2,1)S(1)}, bf16[16,1024]{1,0:T(8,128)(2,1)S(1)}, u32[]{:S(2)}, u32[]{:S(2)}) collective-permute-start(bf16[16,1024]{1,0:T(8,128)(2,1)S(1)} %get-tuple-element.54), channel_id=1, source_target_pairs={{0,1},{1,2},{2,3},{3,4},{4,5},{5,6},{6,7},{7,8},{8,9},{9,10},{10,1... | collective-permute-start | bytes 98312 | tf_op jit(solution)/shard_map/ppermute | solution.py:349
  33.0 7.3 %collective-permute-start.4 = (bf16[128,1024]{1,0:T(8,128)(2,1)S(1)}, bf16[128,1024]{1,0:T(8,128)(2,1)S(1)}, u32[]{:S(2)}, u32[]{:S(2)}) collective-permute-start(bf16[128,1024]{1,0:T(8,128)(2,1)S(1)} %get-tuple-element.30), channel_id=1, source_target_pairs={{0,8},{1,3},{2,10},{3,1},{4,12},{5,7},{6,14},{7,5},{8,0},{9,11},{1... | collective-permute-start | bytes 786440 | tf_op jit(solution)/shard_map/ppermute | solution.py:117
  35.6 24.1 %collective-permute-start.2 = (bf16[128,3584]{1,0:T(8,128)(2,1)S(1)}, bf16[128,3584]{1,0:T(8,128)(2,1)S(1)}, u32[]{:S(2)}, u32[]{:S(2)}) collective-permute-start(bf16[128,3584]{1,0:T(8,128)(2,1)S(1)} %pad_maximum_fusion.2), channel_id=1, source_target_pairs={{0,2},{1,17},{2,0},{3,19},{4,6},{5,21},{6,4},{7,23},{8,10},{9,25},... | collective-permute-start | bytes 2752520 | tf_op jit(solution)/shard_map/ppermute | solution.py:119
  40.3 15.5 %collective-permute-start.10 = (bf16[256,1024]{1,0:T(8,128)(2,1)S(1)}, bf16[256,1024]{1,0:T(8,128)(2,1)S(1)}, u32[]{:S(2)}, u32[]{:S(2)}) collective-permute-start(bf16[256,1024]{1,0:T(8,128)(2,1)S(1)} %pad_maximum_fusion.3), channel_id=1, source_target_pairs={{0,4},{1,9},{2,6},{3,11},{4,0},{5,13},{6,2},{7,15},{8,12},{9,1},{1... | collective-permute-start | bytes 1572872 | tf_op jit(solution)/shard_map/ppermute | solution.py:117
  43.9 11.9 %collective-permute-start.11 = (bf16[256,384]{1,0:T(8,128)(2,1)S(1)}, bf16[256,384]{1,0:T(8,128)(2,1)S(1)}, u32[]{:S(2)}, u32[]{:S(2)}) collective-permute-start(bf16[256,384]{1,0:T(8,128)(2,1)S(1)} %pad_maximum_fusion.7), channel_id=1, source_target_pairs={{0,2},{1,3},{2,0},{3,1},{4,6},{5,7},{6,4},{7,5},{8,10},{9,11},{10,... | collective-permute-start | bytes 589832 | tf_op jit(solution)/shard_map/ppermute | solution.py:117
  55.9 5.6 %collective-permute-start.13 = (bf16[512,1024]{1,0:T(8,128)(2,1)S(1)}, bf16[512,1024]{1,0:T(8,128)(2,1)S(1)}, u32[]{:S(2)}, u32[]{:S(2)}) collective-permute-start(bf16[512,1024]{1,0:T(8,128)(2,1)S(1)} %pad_maximum_fusion.1.xa), channel_id=1, source_target_pairs={{0,1},{1,0},{2,3},{3,2},{4,5},{5,4},{6,7},{7,6},{8,9},{9,8},{10,11... | collective-permute-start | bytes 3145736 | tf_op jit(solution)/shard_map/ppermute | solution.py:117
  58.4 14.8 %collective-permute-start.12 = (bf16[512,1024]{1,0:T(8,128)(2,1)S(1)}, bf16[512,1024]{1,0:T(8,128)(2,1)S(1)}, u32[]{:S(2)}, u32[]{:S(2)}) collective-permute-start(bf16[512,1024]{1,0:T(8,128)(2,1)S(1)} %pad_maximum_fusion.1.xa), channel_id=1, source_target_pairs={{0,2},{1,5},{2,0},{3,7},{4,6},{5,1},{6,4},{7,3},{8,10},{9,13},{10,... | collective-permute-start | bytes 3145736 | tf_op jit(solution)/shard_map/ppermute | solution.py:117
  59.5 1.9 %collective-permute-start.14 = (bf16[512,384]{1,0:T(8,128)(2,1)S(1)}, bf16[512,384]{1,0:T(8,128)(2,1)S(1)}, u32[]{:S(2)}, u32[]{:S(2)}) collective-permute-start(bf16[512,384]{1,0:T(8,128)(2,1)S(1)} %pad_maximum_fusion.5.own_w), channel_id=1, source_target_pairs={{0,1},{1,0},{2,3},{3,2},{4,5},{5,4},{6,7},{7,6},{8,9},{9,8},{10,11... | collective-permute-start | bytes 1179656 | tf_op jit(solution)/shard_map/ppermute | solution.py:117
  59.9 36.4 %copy-start.1 = (bf16[128,1024]{1,0:T(8,128)(2,1)S(1)}, bf16[128,1024]{1,0:T(8,128)(2,1)}, u32[]{:S(2)}) copy-start(bf16[128,1024]{1,0:T(8,128)(2,1)} %feats_in.1) | copy-start | bytes 786436
  59.9 40.8 %copy-start.5 = (f32[9,1024]{1,0:T(8,128)S(1)}, f32[9,1024]{1,0:T(8,128)}, u32[]{:S(2)}) copy-start(f32[9,1024]{1,0:T(8,128)} %taps.1) | copy-start | bytes 110596
  59.9 40.8 %copy-start.8 = (f32[1024]{0:T(1024)S(1)}, f32[1024]{0:T(1024)}, u32[]{:S(2)}) copy-start(f32[1024]{0:T(1024)} %param.16) | copy-start | bytes 12292
  59.9 40.8 %copy-start.9 = (f32[1024]{0:T(1024)S(1)}, f32[1024]{0:T(1024)}, u32[]{:S(2)}) copy-start(f32[1024]{0:T(1024)} %param.19) | copy-start | bytes 12292
  59.9 40.8 %copy-start.10 = (f32[1024]{0:T(1024)S(1)}, f32[1024]{0:T(1024)}, u32[]{:S(2)}) copy-start(f32[1024]{0:T(1024)} %param.20) | copy-start | bytes 12292
  59.9 23.3 %collective-permute-start.3 = (bf16[256,3584]{1,0:T(8,128)(2,1)S(1)}, bf16[256,3584]{1,0:T(8,128)(2,1)S(1)}, u32[]{:S(2)}, u32[]{:S(2)}) collective-permute-start(bf16[256,3584]{1,0:T(8,128)(2,1)S(1)} %pad_maximum_fusion.pa), channel_id=1, source_target_pairs={{0,16},{1,5},{2,18},{3,7},{4,20},{5,1},{6,22},{7,3},{8,24},{9,13},... | collective-permute-start | bytes 5505032 | tf_op jit(solution)/shard_map/ppermute | solution.py:119
  73.2 2.7 %collective-permute-start.15 = (bf16[512,1024]{1,0:T(8,128)(2,1)S(1)}, bf16[512,1024]{1,0:T(8,128)(2,1)S(1)}, u32[]{:S(2)}, u32[]{:S(2)}) collective-permute-start(bf16[512,1024]{1,0:T(8,128)(2,1)S(1)} %collective-permute-done.12.xb), channel_id=1, source_target_pairs={{0,1},{1,0},{2,3},{3,2},{4,5},{5,4},{6,7},{7,6},{8,9},{9,8},{10,11... | collective-permute-start | bytes 3145736 | tf_op jit(solution)/shard_map/ppermute | solution.py:117
  73.2 23.0 %collective-permute-start.19 = (bf16[256,3584]{1,0:T(8,128)(2,1)S(1)}, bf16[256,3584]{1,0:T(8,128)(2,1)S(1)}, u32[]{:S(2)}, u32[]{:S(2)}) collective-permute-start(bf16[256,3584]{1,0:T(8,128)(2,1)S(1)} %pad_maximum_fusion.pa), channel_id=1, source_target_pairs={{0,1},{1,0},{2,3},{3,2},{4,5},{5,4},{6,7},{7,6},{8,9},{9,8},{10,11... | collective-permute-start | bytes 5505032 | tf_op jit(solution)/shard_map/ppermute | solution.py:117
  83.2 17.5 %collective-permute-start.20 = (bf16[256,3584]{1,0:T(8,128)(2,1)S(1)}, bf16[256,3584]{1,0:T(8,128)(2,1)S(1)}, u32[]{:S(2)}, u32[]{:S(2)}) collective-permute-start(bf16[256,3584]{1,0:T(8,128)(2,1)S(1)} %collective-permute-done.3.pb), channel_id=1, source_target_pairs={{0,1},{1,0},{2,3},{3,2},{4,5},{5,4},{6,7},{7,6},{8,9},{9,8},{10,11... | collective-permute-start | bytes 5505032 | tf_op jit(solution)/shard_map/ppermute | solution.py:117
  91.8 5.5 %collective-permute-start.16 = (bf16[160,128]{1,0:T(8,128)(2,1)S(1)}, bf16[160,128]{1,0:T(8,128)(2,1)S(1)}, u32[]{:S(2)}, u32[]{:S(2)}) collective-permute-start(bf16[160,128]{1,0:T(8,128)(2,1)S(1)} %get-tuple-element.47), channel_id=1, source_target_pairs={{0,8},{1,9},{2,10},{3,11},{4,12},{5,13},{6,14},{7,15},{8,0},{9,1},... | collective-permute-start | bytes 122888 | tf_op jit(solution)/shard_map/ppermute | solution.py:117
  93.5 4.1 %collective-permute-start.17 = (bf16[160,128]{1,0:T(8,128)(2,1)S(1)}, bf16[160,128]{1,0:T(8,128)(2,1)S(1)}, u32[]{:S(2)}, u32[]{:S(2)}) collective-permute-start(bf16[160,128]{1,0:T(8,128)(2,1)S(1)} %get-tuple-element.48), channel_id=1, source_target_pairs={{0,4},{1,5},{2,6},{3,7},{4,0},{5,1},{6,2},{7,3},{8,12},{9,13},{10,... | collective-permute-start | bytes 122888 | tf_op jit(solution)/shard_map/ppermute | solution.py:117
  94.9 5.8 %collective-permute-start.18 = (bf16[160,128]{1,0:T(8,128)(2,1)S(1)}, bf16[160,128]{1,0:T(8,128)(2,1)S(1)}, u32[]{:S(2)}, u32[]{:S(2)}) collective-permute-start(bf16[160,128]{1,0:T(8,128)(2,1)S(1)} %get-tuple-element.49), channel_id=1, source_target_pairs={{0,12},{1,13},{2,14},{3,15},{4,8},{5,9},{6,10},{7,11},{8,4},{9,5},... | collective-permute-start | bytes 122888 | tf_op jit(solution)/shard_map/ppermute | solution.py:117

commit v3 on v2

--- a/solution.py
+++ b/solution.py
@@ -337,7 +337,7 @@
             pltpu.VMEM((rows, width), jnp.bfloat16),
             pltpu.SemaphoreType.DMA((16,)),
         ],
-        compiler_params=pltpu.CompilerParams(vmem_limit_bytes=16 << 20),
+        compiler_params=pltpu.CompilerParams(vmem_limit_bytes=60 << 20),
     )(scalars, features, ln1_gain.reshape(1, -1), w_qkv, w_out, w_pw1, w_pw2)
 
     def joined(*arrays):
@@ -353,18 +353,18 @@
     p2 = joined(pack, pack_swap(pack, 0))
     x2 = joined(normed1, x1)
     w4 = joined(w_mine, *w_z)
-    x2, w4, ahead, behind = lax.optimization_barrier((x2, w4, ahead, behind))
-
     w8 = joined(w4, swap(w4, 2))
+    p2, w8, x2, ahead, behind = lax.optimization_barrier((p2, w8, x2, ahead, behind))
+
     p4 = joined(p2, pack_swap(p2, 1))
     xa = joined(x2, swap(x2, ORDER_EVEN[1], ORDER_ODD[1]))
-    xa, w8 = lax.optimization_barrier((xa, w8))
+    w_other = swap(w8, 1)
+    xa, w_other = lax.optimization_barrier((xa, w_other))
 
     xb = swap(xa, ORDER_EVEN[2], ORDER_ODD[2])
     xa_other = swap(xa, 1)
-    w_other = swap(w8, 1)
     pa = joined(p4, pack_swap(p4, 2))
-    xb, xa_other, w_other = lax.optimization_barrier((xb, xa_other, w_other))
+    xb, xa_other = lax.optimization_barrier((xb, xa_other))
     xb_other = swap(xb, 1)
     pb = pack_swap(pa, 3)
     pa_other = swap(pa, 1)
@@ -391,9 +391,9 @@
             flops=5_000_000_000, bytes_accessed=8 << 20, transcendentals=4 * wide * count
         ),
     )(scalars, xa, xb, xa_other, xb_other, w8, w_other)
-    pb, contexts = lax.optimization_barrier((pb, contexts))
+    mine = [contexts[0]] + [swap(part, mask) for part, mask in zip(contexts[1:], ALONG_Z[1:])]
+    pb, _ = lax.optimization_barrier((pb, mine))
     pb_other = swap(pb, 1)
-    mine = [contexts[0]] + [swap(part, mask) for part, mask in zip(contexts[1:], ALONG_Z[1:])]
 
     feats = jnp.concatenate([ahead, features, behind], axis=0)
     return pl.pallas_call(

time: 108 us -> 97.8 us (0.906)
  starting transfers between devices: 40.7 us -> 23.5 us
  waiting for transfers between devices: 45.8 us -> 53.6 us
  local copies, waits for them, and re-layouts: 5.29 us -> 0.82 us
  other arithmetic: 0.48 us -> 2.79 us
  Pallas kernels: 14.1 us -> 15.8 us
    ppermute x4, waiting for transfers between devices: 11.4 us -> 25.8 us  [swap(): return lax.ppermute(array, ('groups', 'frames'), pairs)]
    ppermute x15, starting transfers between devices: 29.8 us -> 15.6 us  [swap(): return lax.ppermute(array, 'frames', pairs)]
    ppermute x15, waiting for transfers between devices: 34.4 us -> 27.8 us  [swap(): return lax.ppermute(array, 'frames', pairs)]
    unnamed x22 -> x14, local copies, waits for them, and re-layouts: 5.29 us -> 0.04 us
    ppermute x4, starting transfers between devices: 8.03 us -> 3.61 us  [swap(): return lax.ppermute(array, ('groups', 'frames'), pairs)]
    pallas_call x1, Pallas kernels: 1.12 us -> 2.9 us  [per_device(): pl.pallas_call(prepare_kernel, name='prepare', out_shape=[jax.ShapeDtypeS...]
    concatenate x7, other arithmetic: 0.38 us -> 2.11 us  [joined(): return lax.optimization_barrier(jnp.concatenate(arrays, axis=0))]
    ppermute x1, starting transfers between devices: 1.61 us -> 3.03 us  [per_device(): lax.ppermute(features[-EDGE:], 'frames', [(i, i + 1) for i in range(15)])]
  transfers between devices with their start and end apart: 21 -> 21, of which waited for: 11 -> 12; matrix products, arithmetic and copies ran while one was open for 0% -> 3% of each run, Pallas kernels for 6% -> 7%
where the time goes in v3:
time: 97.8 us; the launch traced here: 97.4 us
  waiting for transfers between devices  53.6 us (55%)
  starting transfers between devices  23.5 us (24%)
  Pallas kernels  15.8 us (16%)
  other arithmetic  2.79 us (3%)
    ppermute x15, waiting for transfers between devices, swap(): return lax.ppermute(array, 'frames', pairs)  27.8 us
    ppermute x4, waiting for transfers between devices, swap(): return lax.ppermute(array, ('groups', 'frames'), pairs)  25.8 us
    ppermute x15, starting transfers between devices, swap(): return lax.ppermute(array, 'frames', pairs)  15.6 us
    pallas_call x1, Pallas kernels, per_device(): pl.pallas_call(functools.partial(tail_kernel, rows=rows), name='tail', ou...  6.5 us
    pallas_call x1, Pallas kernels, per_device(): pl.pallas_call(functools.partial(attention_kernel, rows=rows, even=even,...  6.43 us
    ppermute x4, starting transfers between devices, swap(): return lax.ppermute(array, ('groups', 'frames'), pairs)  3.61 us
    ppermute x1, starting transfers between devices, per_device(): lax.ppermute(features[-EDGE:], 'frames', [(i, i + 1) for i in range(15)])  3.03 us
    pallas_call x1, Pallas kernels, per_device(): pl.pallas_call(prepare_kernel, name='prepare', out_shape=[jax.ShapeDtypeS...  2.9 us
  transfers between devices with their start and end apart: 21, of which 12 were waited for; matrix products, arithmetic and copies ran while one was open for 3% of the time, Pallas kernels for 7%

profile of v3, /device:TPU:0, one launch (start us, length us, event | category | flops | bytes accessed | tf_op | source)
XLA Modules:
  0.0 97.4 jit_solution(10175230054827821091)
XLA Ops:
  0.7 0.7 pad_add_fusion.scalars
  1.3 2.9 %prepare.1 = (bf16[128,1024]{1,0:T(8,128)(2,1)}, bf16[64,384]{1,0:T(8,128)(2,1)}, bf16[64,384]{1,0:T(8,128)(2,1)}, bf16[64,384]{1,0:T(8,128)(2,1)}, bf16[64,384]{1,0:T(8,128)(2,1)}, /*index=5*/bf16[32,3584]{1,0:T(8,128)(2,1)}) custom-call(s32[4]{0:T(128)} %pad_add_fusion.scalars, bf16[128,1024]{1,0:T(8,128)(2,1)} %feats_in.1, f32[1,1024]{1,0:T(1,128)} %bitcast.10, ...), custom_call_target="tpu_custom_call" | custom-call | tf_op jit(solution)/shard_map/prepare/pallas_call | solution.py:328
  4.2 4.1 %collective-permute-start.1 = (bf16[64,384]{1,0:T(8,128)(2,1)}, bf16[64,384]{1,0:T(8,128)(2,1)S(1)}, u32[]{:S(2)}, u32[]{:S(2)}) collective-permute-start(bf16[64,384]{1,0:T(8,128)(2,1)} %get-tuple-element.27), channel_id=1, source_target_pairs={{0,8},{1,9},{2,10},{3,11},{4,12},{5,13},{6,14},{7,15},{8,0},{9,1},... | collective-permute-start | bytes 147464 | tf_op jit(solution)/shard_map/ppermute | solution.py:117
  8.3 1.6 %collective-permute-start.2 = (bf16[64,384]{1,0:T(8,128)(2,1)}, bf16[64,384]{1,0:T(8,128)(2,1)S(1)}, u32[]{:S(2)}, u32[]{:S(2)}) collective-permute-start(bf16[64,384]{1,0:T(8,128)(2,1)} %get-tuple-element.28), channel_id=1, source_target_pairs={{0,4},{1,5},{2,6},{3,7},{4,0},{5,1},{6,2},{7,3},{8,12},{9,13},{10,... | collective-permute-start | bytes 147464 | tf_op jit(solution)/shard_map/ppermute | solution.py:117
  9.9 1.9 %collective-permute-start = (bf16[32,3584]{1,0:T(8,128)(2,1)}, bf16[32,3584]{1,0:T(8,128)(2,1)S(1)}, u32[]{:S(2)}, u32[]{:S(2)}) collective-permute-start(bf16[32,3584]{1,0:T(8,128)(2,1)} %get-tuple-element.25), channel_id=1, source_target_pairs={{0,8},{1,9},{2,10},{3,11},{4,12},{5,13},{6,14},{7,15},{8,0},{9,1},... | collective-permute-start | bytes 688136 | tf_op jit(solution)/shard_map/ppermute | solution.py:119
  11.8 0.8 fusion
  12.6 1.3 %collective-permute-start.7 = (bf16[16,1024]{1,0:T(8,128)(2,1)S(1)}, bf16[16,1024]{1,0:T(8,128)(2,1)S(1)}, u32[]{:S(2)}, u32[]{:S(2)}) collective-permute-start(bf16[16,1024]{1,0:T(8,128)(2,1)S(1)} %get-tuple-element.45), channel_id=1, source_target_pairs={{1,0},{2,1},{3,2},{4,3},{5,4},{6,5},{7,6},{8,7},{9,8},{10,9},{11,1... | collective-permute-start | bytes 98312 | tf_op jit(solution)/shard_map/ppermute | solution.py:350
  13.9 3.0 %collective-permute-start.6 = (bf16[16,1024]{1,0:T(8,128)(2,1)S(1)}, bf16[16,1024]{1,0:T(8,128)(2,1)S(1)}, u32[]{:S(2)}, u32[]{:S(2)}) collective-permute-start(bf16[16,1024]{1,0:T(8,128)(2,1)S(1)} %get-tuple-element.46), channel_id=1, source_target_pairs={{0,1},{1,2},{2,3},{3,4},{4,5},{5,6},{6,7},{7,8},{8,9},{9,10},{10,1... | collective-permute-start | bytes 98312 | tf_op jit(solution)/shard_map/ppermute | solution.py:349
  16.9 2.8 %collective-permute-start.5 = (bf16[128,1024]{1,0:T(8,128)(2,1)}, bf16[128,1024]{1,0:T(8,128)(2,1)S(1)}, u32[]{:S(2)}, u32[]{:S(2)}) collective-permute-start(bf16[128,1024]{1,0:T(8,128)(2,1)} %get-tuple-element.30), channel_id=1, source_target_pairs={{0,8},{1,3},{2,10},{3,1},{4,12},{5,7},{6,14},{7,5},{8,0},{9,11},{1... | collective-permute-start | bytes 786440 | tf_op jit(solution)/shard_map/ppermute | solution.py:117
  19.7 0.8 pad_maximum_fusion.7
  20.6 0.1 collective-permute-start.4
  20.7 6.4 %collective-permute-done = bf16[32,3584]{1,0:T(8,128)(2,1)S(1)} collective-permute-done((bf16[32,3584]{1,0:T(8,128)(2,1)}, bf16[32,3584]{1,0:T(8,128)(2,1)S(1)}, u32[]{:S(2)}, u32[]{:S(2)}) %collective-permute-start) | collective-permute-done | bytes 229408 | tf_op jit(solution)/shard_map/ppermute | solution.py:119
  27.1 1.0 pad_maximum_fusion.4
  28.1 0.4 collective-permute-done.4
  28.5 1.8 %collective-permute-done.5 = bf16[128,1024]{1,0:T(8,128)(2,1)S(1)} collective-permute-done((bf16[128,1024]{1,0:T(8,128)(2,1)}, bf16[128,1024]{1,0:T(8,128)(2,1)S(1)}, u32[]{:S(2)}, u32[]{:S(2)}) %collective-permute-start.5) | collective-permute-done | bytes 262176 | tf_op jit(solution)/shard_map/ppermute | solution.py:117
  30.4 2.0 %collective-permute-start.8 = (bf16[256,1024]{1,0:T(8,128)(2,1)S(1)}, bf16[256,1024]{1,0:T(8,128)(2,1)S(1)}, u32[]{:S(2)}, u32[]{:S(2)}) collective-permute-start(bf16[256,1024]{1,0:T(8,128)(2,1)S(1)} %pad_maximum_fusion.3), channel_id=1, source_target_pairs={{0,4},{1,9},{2,6},{3,11},{4,0},{5,13},{6,2},{7,15},{8,12},{9,1},{1... | collective-permute-start | bytes 1572872 | tf_op jit(solution)/shard_map/ppermute | solution.py:117
  32.4 12.0 %collective-permute-done.16 = bf16[64,3584]{1,0:T(8,128)(2,1)S(1)} collective-permute-done((bf16[64,3584]{1,0:T(8,128)(2,1)S(1)}, bf16[64,3584]{1,0:T(8,128)(2,1)S(1)}, u32[]{:S(2)}, u32[]{:S(2)}) %collective-permute-start.16) | collective-permute-done | bytes 458784 | tf_op jit(solution)/shard_map/ppermute | solution.py:119
  44.7 5.4 %collective-permute-done.8 = bf16[256,1024]{1,0:T(8,128)(2,1)S(1)} collective-permute-done((bf16[256,1024]{1,0:T(8,128)(2,1)S(1)}, bf16[256,1024]{1,0:T(8,128)(2,1)S(1)}, u32[]{:S(2)}, u32[]{:S(2)}) %collective-permute-start.8) | collective-permute-done | bytes 524320 | tf_op jit(solution)/shard_map/ppermute | solution.py:117
  50.2 0.4 collective-permute-start.10
  50.7 7.3 %collective-permute-done.17 = bf16[128,3584]{1,0:T(8,128)(2,1)S(1)} collective-permute-done((bf16[128,3584]{1,0:T(8,128)(2,1)S(1)}, bf16[128,3584]{1,0:T(8,128)(2,1)S(1)}, u32[]{:S(2)}, u32[]{:S(2)}) %collective-permute-start.17) | collective-permute-done | bytes 917536 | tf_op jit(solution)/shard_map/ppermute | solution.py:119
  58.0 0.1 pad_maximum_fusion.pa
  58.2 1.6 %collective-permute-start.18 = (bf16[256,3584]{1,0:T(8,128)(2,1)S(1)}, bf16[256,3584]{1,0:T(8,128)(2,1)S(1)}, u32[]{:S(2)}, u32[]{:S(2)}) collective-permute-start(bf16[256,3584]{1,0:T(8,128)(2,1)S(1)} %pad_maximum_fusion.pa), channel_id=1, source_target_pairs={{0,16},{1,5},{2,18},{3,7},{4,20},{5,1},{6,22},{7,3},{8,24},{9,13},... | collective-permute-start | bytes 5505032 | tf_op jit(solution)/shard_map/ppermute | solution.py:119
  59.7 9.5 %collective-permute-done.10.xb = bf16[512,1024]{1,0:T(8,128)(2,1)S(1)} collective-permute-done((bf16[512,1024]{1,0:T(8,128)(2,1)S(1)}, bf16[512,1024]{1,0:T(8,128)(2,1)S(1)}, u32[]{:S(2)}, u32[]{:S(2)}) %collective-permute-start.10) | collective-permute-done | bytes 1048608 | tf_op jit(solution)/shard_map/ppermute | solution.py:117
  69.2 2.7 %collective-permute-done.12.xb_other = bf16[512,1024]{1,0:T(8,128)(2,1)S(1)} collective-permute-done((bf16[512,1024]{1,0:T(8,128)(2,1)S(1)}, bf16[512,1024]{1,0:T(8,128)(2,1)S(1)}, u32[]{:S(2)}, u32[]{:S(2)}) %collective-permute-start.12) | collective-permute-done | bytes 1048608 | tf_op jit(solution)/shard_map/ppermute | solution.py:117
  71.9 6.4 %attention.1 = (bf16[160,128]{1,0:T(8,128)(2,1)S(1)}, bf16[160,128]{1,0:T(8,128)(2,1)S(1)}, bf16[160,128]{1,0:T(8,128)(2,1)S(1)}, bf16[160,128]{1,0:T(8,128)(2,1)S(1)}) custom-call(s32[4]{0:T(128)S(1)} %copy-done.1, bf16[512,1024]{1,0:T(8,128)(2,1)S(1)} %pad_maximum_fusion.1.xa, bf16[512,1024]{1,0:T(8,128)(2,1)S(1)} %collective-permute-done.10.xb, ...), custom_call_target="tpu_custom_call" | custom-call | flops 5000000000 | bytes 8388608 | tf_op jit(solution)/shard_map/attention/pallas_call | solution.py:374
  78.4 2.5 %collective-permute-start.14 = (bf16[160,128]{1,0:T(8,128)(2,1)S(1)}, bf16[160,128]{1,0:T(8,128)(2,1)S(1)}, u32[]{:S(2)}, u32[]{:S(2)}) collective-permute-start(bf16[160,128]{1,0:T(8,128)(2,1)S(1)} %get-tuple-element.39), channel_id=1, source_target_pairs={{0,4},{1,5},{2,6},{3,7},{4,0},{5,1},{6,2},{7,3},{8,12},{9,13},{10,... | collective-permute-start | bytes 122888 | tf_op jit(solution)/shard_map/ppermute | solution.py:117
  80.9 1.8 %collective-permute-start.15 = (bf16[160,128]{1,0:T(8,128)(2,1)S(1)}, bf16[160,128]{1,0:T(8,128)(2,1)S(1)}, u32[]{:S(2)}, u32[]{:S(2)}) collective-permute-start(bf16[160,128]{1,0:T(8,128)(2,1)S(1)} %get-tuple-element.40), channel_id=1, source_target_pairs={{0,12},{1,13},{2,14},{3,15},{4,8},{5,9},{6,10},{7,11},{8,4},{9,5},... | collective-permute-start | bytes 122888 | tf_op jit(solution)/shard_map/ppermute | solution.py:117
  82.8 0.9 collective-permute-done.13.c1
  83.7 0.4 collective-permute-done.14.c2
  84.1 3.1 %collective-permute-done.15.c3 = bf16[160,128]{1,0:T(8,128)(2,1)S(1)} collective-permute-done((bf16[160,128]{1,0:T(8,128)(2,1)S(1)}, bf16[160,128]{1,0:T(8,128)(2,1)S(1)}, u32[]{:S(2)}, u32[]{:S(2)}) %collective-permute-start.15) | collective-permute-done | bytes 40992 | tf_op jit(solution)/shard_map/ppermute | solution.py:117
  87.2 3.7 %collective-permute-done.20.pb_other = bf16[256,3584]{1,0:T(8,128)(2,1)S(1)} collective-permute-done((bf16[256,3584]{1,0:T(8,128)(2,1)S(1)}, bf16[256,3584]{1,0:T(8,128)(2,1)S(1)}, u32[]{:S(2)}, u32[]{:S(2)}) %collective-permute-start.20) | collective-permute-done | bytes 1835040 | tf_op jit(solution)/shard_map/ppermute | solution.py:117
  90.9 6.5 %tail.1 = bf16[128,1024]{1,0:T(8,128)(2,1)} custom-call(s32[4]{0:T(128)S(1)} %copy-done.1, bf16[160,128]{1,0:T(8,128)(2,1)S(1)} %get-tuple-element.37.c0, bf16[160,128]{1,0:T(8,128)(2,1)S(1)} %collective-permute-done.13.c1, bf16[160,128]{1,0:T(8,128)(2,1)S(1)} %collective-permute-done.14.c2, bf16[160,128]{1,0:T(8,128)(2,1)S(1)} %collective-permute-done.15.c3, ...), custom_call_target="tpu_custom_call" | custom-call | flops 1200000000 | bytes 8388608 | tf_op jit(solution)/shard_map/tail/pallas_call | solution.py:399
  (37 shorter events, 0.7 us)
Async XLA Ops:
  4.2 26.1 %copy-start.6 = (bf16[128,1024]{1,0:T(8,128)(2,1)S(1)}, bf16[128,1024]{1,0:T(8,128)(2,1)}, u32[]{:S(2)}) copy-start(bf16[128,1024]{1,0:T(8,128)(2,1)} %get-tuple-element.30) | copy-start | bytes 786436
  4.2 9.7 %collective-permute-start.1 = (bf16[64,384]{1,0:T(8,128)(2,1)}, bf16[64,384]{1,0:T(8,128)(2,1)S(1)}, u32[]{:S(2)}, u32[]{:S(2)}) collective-permute-start(bf16[64,384]{1,0:T(8,128)(2,1)} %get-tuple-element.27), channel_id=1, source_target_pairs={{0,8},{1,9},{2,10},{3,11},{4,12},{5,13},{6,14},{7,15},{8,0},{9,1},... | collective-permute-start | bytes 147464 | tf_op jit(solution)/shard_map/ppermute | solution.py:117
  8.3 8.6 %collective-permute-start.2 = (bf16[64,384]{1,0:T(8,128)(2,1)}, bf16[64,384]{1,0:T(8,128)(2,1)S(1)}, u32[]{:S(2)}, u32[]{:S(2)}) collective-permute-start(bf16[64,384]{1,0:T(8,128)(2,1)} %get-tuple-element.28), channel_id=1, source_target_pairs={{0,4},{1,5},{2,6},{3,7},{4,0},{5,1},{6,2},{7,3},{8,12},{9,13},{10,... | collective-permute-start | bytes 147464 | tf_op jit(solution)/shard_map/ppermute | solution.py:117
  9.9 9.8 %collective-permute-start.3 = (bf16[64,384]{1,0:T(8,128)(2,1)}, bf16[64,384]{1,0:T(8,128)(2,1)S(1)}, u32[]{:S(2)}, u32[]{:S(2)}) collective-permute-start(bf16[64,384]{1,0:T(8,128)(2,1)} %get-tuple-element.29), channel_id=1, source_target_pairs={{0,12},{1,13},{2,14},{3,15},{4,8},{5,9},{6,10},{7,11},{8,4},{9,5},... | collective-permute-start | bytes 147464 | tf_op jit(solution)/shard_map/ppermute | solution.py:117
  9.9 17.2 %collective-permute-start = (bf16[32,3584]{1,0:T(8,128)(2,1)}, bf16[32,3584]{1,0:T(8,128)(2,1)S(1)}, u32[]{:S(2)}, u32[]{:S(2)}) collective-permute-start(bf16[32,3584]{1,0:T(8,128)(2,1)} %get-tuple-element.25), channel_id=1, source_target_pairs={{0,8},{1,9},{2,10},{3,11},{4,12},{5,13},{6,14},{7,15},{8,0},{9,1},... | collective-permute-start | bytes 688136 | tf_op jit(solution)/shard_map/ppermute | solution.py:119
  12.6 17.7 %collective-permute-start.7 = (bf16[16,1024]{1,0:T(8,128)(2,1)S(1)}, bf16[16,1024]{1,0:T(8,128)(2,1)S(1)}, u32[]{:S(2)}, u32[]{:S(2)}) collective-permute-start(bf16[16,1024]{1,0:T(8,128)(2,1)S(1)} %get-tuple-element.45), channel_id=1, source_target_pairs={{1,0},{2,1},{3,2},{4,3},{5,4},{6,5},{7,6},{8,7},{9,8},{10,9},{11,1... | collective-permute-start | bytes 98312 | tf_op jit(solution)/shard_map/ppermute | solution.py:350
  13.9 16.4 %collective-permute-start.6 = (bf16[16,1024]{1,0:T(8,128)(2,1)S(1)}, bf16[16,1024]{1,0:T(8,128)(2,1)S(1)}, u32[]{:S(2)}, u32[]{:S(2)}) collective-permute-start(bf16[16,1024]{1,0:T(8,128)(2,1)S(1)} %get-tuple-element.46), channel_id=1, source_target_pairs={{0,1},{1,2},{2,3},{3,4},{4,5},{5,6},{6,7},{7,8},{8,9},{9,10},{10,1... | collective-permute-start | bytes 98312 | tf_op jit(solution)/shard_map/ppermute | solution.py:349
  16.9 13.3 %collective-permute-start.5 = (bf16[128,1024]{1,0:T(8,128)(2,1)}, bf16[128,1024]{1,0:T(8,128)(2,1)S(1)}, u32[]{:S(2)}, u32[]{:S(2)}) collective-permute-start(bf16[128,1024]{1,0:T(8,128)(2,1)} %get-tuple-element.30), channel_id=1, source_target_pairs={{0,8},{1,3},{2,10},{3,1},{4,12},{5,7},{6,14},{7,5},{8,0},{9,11},{1... | collective-permute-start | bytes 786440 | tf_op jit(solution)/shard_map/ppermute | solution.py:117
  20.6 7.9 %collective-permute-start.4 = (bf16[256,384]{1,0:T(8,128)(2,1)S(1)}, bf16[256,384]{1,0:T(8,128)(2,1)S(1)}, u32[]{:S(2)}, u32[]{:S(2)}) collective-permute-start(bf16[256,384]{1,0:T(8,128)(2,1)S(1)} %pad_maximum_fusion.7), channel_id=1, source_target_pairs={{0,2},{1,3},{2,0},{3,1},{4,6},{5,7},{6,4},{7,5},{8,10},{9,11},{10,... | collective-permute-start | bytes 589832 | tf_op jit(solution)/shard_map/ppermute | solution.py:117
  30.3 14.1 %collective-permute-start.16 = (bf16[64,3584]{1,0:T(8,128)(2,1)S(1)}, bf16[64,3584]{1,0:T(8,128)(2,1)S(1)}, u32[]{:S(2)}, u32[]{:S(2)}) collective-permute-start(bf16[64,3584]{1,0:T(8,128)(2,1)S(1)} %pad_maximum_fusion.4), channel_id=1, source_target_pairs={{0,4},{1,3},{2,6},{3,1},{4,0},{5,7},{6,2},{7,5},{8,12},{9,11},{10,... | collective-permute-start | bytes 1376264 | tf_op jit(solution)/shard_map/ppermute | solution.py:119
  30.4 19.7 %collective-permute-start.8 = (bf16[256,1024]{1,0:T(8,128)(2,1)S(1)}, bf16[256,1024]{1,0:T(8,128)(2,1)S(1)}, u32[]{:S(2)}, u32[]{:S(2)}) collective-permute-start(bf16[256,1024]{1,0:T(8,128)(2,1)S(1)} %pad_maximum_fusion.3), channel_id=1, source_target_pairs={{0,4},{1,9},{2,6},{3,11},{4,0},{5,13},{6,2},{7,15},{8,12},{9,1},{1... | collective-permute-start | bytes 1572872 | tf_op jit(solution)/shard_map/ppermute | solution.py:117
  44.5 13.5 %collective-permute-start.17 = (bf16[128,3584]{1,0:T(8,128)(2,1)S(1)}, bf16[128,3584]{1,0:T(8,128)(2,1)S(1)}, u32[]{:S(2)}, u32[]{:S(2)}) collective-permute-start(bf16[128,3584]{1,0:T(8,128)(2,1)S(1)} %pad_maximum_fusion.2), channel_id=1, source_target_pairs={{0,2},{1,17},{2,0},{3,19},{4,6},{5,21},{6,4},{7,23},{8,10},{9,25},... | collective-permute-start | bytes 2752520 | tf_op jit(solution)/shard_map/ppermute | solution.py:119
  44.6 5.6 %collective-permute-start.9 = (bf16[512,384]{1,0:T(8,128)(2,1)S(1)}, bf16[512,384]{1,0:T(8,128)(2,1)S(1)}, u32[]{:S(2)}, u32[]{:S(2)}) collective-permute-start(bf16[512,384]{1,0:T(8,128)(2,1)S(1)} %pad_maximum_fusion.5.own_w), channel_id=1, source_target_pairs={{0,1},{1,0},{2,3},{3,2},{4,5},{5,4},{6,7},{7,6},{8,9},{9,8},{10,11... | collective-permute-start | bytes 1179656 | tf_op jit(solution)/shard_map/ppermute | solution.py:117
  50.1 21.7 %copy-start.1 = (s32[4]{0:T(128)S(1)}, s32[4]{0:T(128)}, u32[]{:S(2)}) copy-start(s32[4]{0:T(128)} %pad_add_fusion.scalars) | copy-start | bytes 52
  50.2 9.6 %collective-permute-start.11 = (bf16[512,1024]{1,0:T(8,128)(2,1)S(1)}, bf16[512,1024]{1,0:T(8,128)(2,1)S(1)}, u32[]{:S(2)}, u32[]{:S(2)}) collective-permute-start(bf16[512,1024]{1,0:T(8,128)(2,1)S(1)} %pad_maximum_fusion.1.xa), channel_id=1, source_target_pairs={{0,1},{1,0},{2,3},{3,2},{4,5},{5,4},{6,7},{7,6},{8,9},{9,8},{10,11... | collective-permute-start | bytes 3145736 | tf_op jit(solution)/shard_map/ppermute | solution.py:117
  50.2 19.0 %collective-permute-start.10 = (bf16[512,1024]{1,0:T(8,128)(2,1)S(1)}, bf16[512,1024]{1,0:T(8,128)(2,1)S(1)}, u32[]{:S(2)}, u32[]{:S(2)}) collective-permute-start(bf16[512,1024]{1,0:T(8,128)(2,1)S(1)} %pad_maximum_fusion.1.xa), channel_id=1, source_target_pairs={{0,2},{1,5},{2,0},{3,7},{4,6},{5,1},{6,4},{7,3},{8,10},{9,13},{10,... | collective-permute-start | bytes 3145736 | tf_op jit(solution)/shard_map/ppermute | solution.py:117
  58.1 29.0 %copy-start.5 = (bf16[128,1024]{1,0:T(8,128)(2,1)S(1)}, bf16[128,1024]{1,0:T(8,128)(2,1)}, u32[]{:S(2)}) copy-start(bf16[128,1024]{1,0:T(8,128)(2,1)} %feats_in.1) | copy-start | bytes 786436
  58.1 32.8 %copy-start = (f32[9,1024]{1,0:T(8,128)S(1)}, f32[9,1024]{1,0:T(8,128)}, u32[]{:S(2)}) copy-start(f32[9,1024]{1,0:T(8,128)} %taps.1) | copy-start | bytes 110596
  58.1 32.8 %copy-start.2 = (f32[1024]{0:T(1024)S(1)}, f32[1024]{0:T(1024)}, u32[]{:S(2)}) copy-start(f32[1024]{0:T(1024)} %param.16) | copy-start | bytes 12292
  58.1 32.8 %copy-start.3 = (f32[1024]{0:T(1024)S(1)}, f32[1024]{0:T(1024)}, u32[]{:S(2)}) copy-start(f32[1024]{0:T(1024)} %param.19) | copy-start | bytes 12292
  58.1 32.8 %copy-start.4 = (f32[1024]{0:T(1024)S(1)}, f32[1024]{0:T(1024)}, u32[]{:S(2)}) copy-start(f32[1024]{0:T(1024)} %param.20) | copy-start | bytes 12292
  58.2 29.0 %collective-permute-start.18 = (bf16[256,3584]{1,0:T(8,128)(2,1)S(1)}, bf16[256,3584]{1,0:T(8,128)(2,1)S(1)}, u32[]{:S(2)}, u32[]{:S(2)}) collective-permute-start(bf16[256,3584]{1,0:T(8,128)(2,1)S(1)} %pad_maximum_fusion.pa), channel_id=1, source_target_pairs={{0,16},{1,5},{2,18},{3,7},{4,20},{5,1},{6,22},{7,3},{8,24},{9,13},... | collective-permute-start | bytes 5505032 | tf_op jit(solution)/shard_map/ppermute | solution.py:119
  69.2 2.7 %collective-permute-start.12 = (bf16[512,1024]{1,0:T(8,128)(2,1)S(1)}, bf16[512,1024]{1,0:T(8,128)(2,1)S(1)}, u32[]{:S(2)}, u32[]{:S(2)}) collective-permute-start(bf16[512,1024]{1,0:T(8,128)(2,1)S(1)} %collective-permute-done.10.xb), channel_id=1, source_target_pairs={{0,1},{1,0},{2,3},{3,2},{4,5},{5,4},{6,7},{7,6},{8,9},{9,8},{10,11... | collective-permute-start | bytes 3145736 | tf_op jit(solution)/shard_map/ppermute | solution.py:117
  78.3 5.4 %collective-permute-start.13 = (bf16[160,128]{1,0:T(8,128)(2,1)S(1)}, bf16[160,128]{1,0:T(8,128)(2,1)S(1)}, u32[]{:S(2)}, u32[]{:S(2)}) collective-permute-start(bf16[160,128]{1,0:T(8,128)(2,1)S(1)} %get-tuple-element.38), channel_id=1, source_target_pairs={{0,8},{1,9},{2,10},{3,11},{4,12},{5,13},{6,14},{7,15},{8,0},{9,1},... | collective-permute-start | bytes 122888 | tf_op jit(solution)/shard_map/ppermute | solution.py:117
  78.4 5.7 %collective-permute-start.14 = (bf16[160,128]{1,0:T(8,128)(2,1)S(1)}, bf16[160,128]{1,0:T(8,128)(2,1)S(1)}, u32[]{:S(2)}, u32[]{:S(2)}) collective-permute-start(bf16[160,128]{1,0:T(8,128)(2,1)S(1)} %get-tuple-element.39), channel_id=1, source_target_pairs={{0,4},{1,5},{2,6},{3,7},{4,0},{5,1},{6,2},{7,3},{8,12},{9,13},{10,... | collective-permute-start | bytes 122888 | tf_op jit(solution)/shard_map/ppermute | solution.py:117
  80.9 6.2 %collective-permute-start.15 = (bf16[160,128]{1,0:T(8,128)(2,1)S(1)}, bf16[160,128]{1,0:T(8,128)(2,1)S(1)}, u32[]{:S(2)}, u32[]{:S(2)}) collective-permute-start(bf16[160,128]{1,0:T(8,128)(2,1)S(1)} %get-tuple-element.40), channel_id=1, source_target_pairs={{0,12},{1,13},{2,14},{3,15},{4,8},{5,9},{6,10},{7,11},{8,4},{9,5},... | collective-permute-start | bytes 122888 | tf_op jit(solution)/shard_map/ppermute | solution.py:117
  82.8 4.4 %collective-permute-start.19 = (bf16[256,3584]{1,0:T(8,128)(2,1)S(1)}, bf16[256,3584]{1,0:T(8,128)(2,1)S(1)}, u32[]{:S(2)}, u32[]{:S(2)}) collective-permute-start(bf16[256,3584]{1,0:T(8,128)(2,1)S(1)} %pad_maximum_fusion.pa), channel_id=1, source_target_pairs={{0,1},{1,0},{2,3},{3,2},{4,5},{5,4},{6,7},{7,6},{8,9},{9,8},{10,11... | collective-permute-start | bytes 5505032 | tf_op jit(solution)/shard_map/ppermute | solution.py:117
  87.1 3.8 %collective-permute-start.20 = (bf16[256,3584]{1,0:T(8,128)(2,1)S(1)}, bf16[256,3584]{1,0:T(8,128)(2,1)S(1)}, u32[]{:S(2)}, u32[]{:S(2)}) collective-permute-start(bf16[256,3584]{1,0:T(8,128)(2,1)S(1)} %collective-permute-done.18.pb), channel_id=1, source_target_pairs={{0,1},{1,0},{2,3},{3,2},{4,5},{5,4},{6,7},{7,6},{8,9},{9,8},{10,11... | collective-permute-start | bytes 5505032 | tf_op jit(solution)/shard_map/ppermute | solution.py:117

commit v4 on v3

--- a/solution.py
+++ b/solution.py
@@ -19,7 +19,7 @@
 ORDER_ODD = (2, 8, 4)
 PACK_EVEN = (8, 4, 2, 16)
 PACK_ODD = (8, 2, 16, 4)
-ALONG_Z = (0, 8, 4, 12)
+ALONG_Z = (0, 12, 4, 8)
 
 
 def extended(cells, sides, width):
@@ -135,7 +135,7 @@
 def prepare_kernel(
     scalars, feats_in, gain, w_qkv, w_out, w_pw1, w_pw2, normed, head0, head1, head2, head3, pack, feats, sems
 ):
-    me, group = scalars[0], scalars[3]
+    me, group = lax.axis_index("frames"), lax.axis_index("groups")
     load = pltpu.make_async_copy(feats_in, feats, sems.at[0])
     load.start()
     att = w_qkv.shape[1] // 3
@@ -169,7 +169,7 @@
     scalars, xa, xb, xa_other, xb_other, own_w, other_w, *refs, rows, even, odd, w_masks, count
 ):
     outs, (x_all, w_all, keys, values, sems) = refs[:4], refs[4:]
-    me, limit = scalars[0], scalars[1]
+    me, limit = lax.axis_index("frames"), scalars[0]
     depth = w_all.shape[0] // 16
     for other_core, (xs, ws) in enumerate((((xa, xb), own_w), ((xa_other, xb_other), other_w))):
         for j in range(8):
@@ -238,20 +238,15 @@
 
 def tail_kernel(
     scalars, c0, c1, c2, c3, feats, gain, taps, bn_scale, bn_shift, pa, pb, pa_other, pb_other, out,
-    v0, v1, v2, v3, wide_gated, sems, *, rows
+    wide_gated, *, rows
 ):
-    me, limit, place = scalars[0], scalars[1], scalars[2]
-    held = (v0, v1, v2, v3)
-    copies = [
-        pltpu.make_async_copy(a, b, sems.at[i])
-        for i, (a, b) in enumerate(zip((pa, pa_other, pb, pb_other), (v0, v2, v1, v3)))
-    ]
-    for copy in copies:
-        copy.start()
+    me, limit = lax.axis_index("frames"), scalars[0]
+    place = lax.axis_index("groups") * 16 + me
+    held = (pa, pb, pa_other, pb_other)
     wide = rows + 2 * EDGE
     width = out.shape[1]
     quarter = width // 4
-    step = v0.shape[0] // 8
+    step = pa.shape[0] // 8
     lanes = lax.broadcasted_iota(jnp.int32, (1, width), 1)
     source = lane_sources(place, lanes, step)
     index = (source & 15) * (2 * step) + (source // 16) * step + lanes % step
@@ -282,8 +277,6 @@
         for h in range(2):
             by = jnp.where((small + head * HD == row_out) & (side == h), 1.0, 0.0).astype(jnp.bfloat16)
             spreads[h] = spreads[h] + jnp.dot(part[...], by, preferred_element_type=jnp.float32)
-    for copy in copies:
-        copy.wait()
     for h in range(2):
         halves.append(times(spreads[h].astype(jnp.bfloat16), 3 * width, 3 * width + width // 2))
     attended = feats[...].astype(jnp.float32) + jnp.concatenate(halves, axis=1)
@@ -315,17 +308,15 @@
     rows, width = features.shape
     count = rows * 16
     depth = w_qkv.shape[0]
-    me = lax.axis_index("frames")
-    group = lax.axis_index("groups")
     groups = lax.axis_size("groups")
-    scalars = jnp.stack([me, valid_length[0], 16 * group + me, group]).astype(jnp.int32)
+    scalars = valid_length
     even, odd = block_masks(ORDER_EVEN), block_masks(ORDER_ODD)
     any_spec = pl.BlockSpec(memory_space=pl.ANY)
     hbm = pl.BlockSpec(memory_space=pltpu.HBM)
     smem = pl.BlockSpec(memory_space=pltpu.SMEM)
     vmem = pl.BlockSpec(memory_space=pltpu.VMEM)
 
-    normed1, w_mine, w_8, w_4, w_12, pack = pl.pallas_call(
+    normed1, w_mine, w_12, w_4, w_8, pack = pl.pallas_call(
         prepare_kernel,
         name="prepare",
         out_shape=[jax.ShapeDtypeStruct((rows, width), jnp.bfloat16)]
@@ -349,7 +340,7 @@
     ahead = lax.ppermute(features[-EDGE:], "frames", [(i, i + 1) for i in range(15)])
     behind = lax.ppermute(features[:EDGE], "frames", [(i + 1, i) for i in range(15)])
     x1 = swap(normed1, ORDER_EVEN[0], ORDER_ODD[0])
-    w_z = [swap(part, mask) for part, mask in zip((w_8, w_4, w_12), ALONG_Z[1:])]
+    w_z = [swap(part, mask) for part, mask in zip((w_12, w_4, w_8), ALONG_Z[1:])]
     p2 = joined(pack, pack_swap(pack, 0))
     x2 = joined(normed1, x1)
     w4 = joined(w_mine, *w_z)
@@ -370,7 +361,7 @@
     pa_other = swap(pa, 1)
 
     wide = rows + 2 * EDGE
-    w_masks = block_masks((8, 4, 2))
+    w_masks = list(ALONG_Z) + [mask ^ 2 for mask in ALONG_Z]
     contexts = pl.pallas_call(
         functools.partial(
             attention_kernel, rows=rows, even=even, odd=odd, w_masks=w_masks, count=count
@@ -400,15 +391,10 @@
         functools.partial(tail_kernel, rows=rows),
         name="tail",
         out_shape=jax.ShapeDtypeStruct((rows, width), jnp.bfloat16),
-        in_specs=[smem] + [vmem] * 9 + [any_spec] * 4,
+        in_specs=[smem] + [vmem] * 13,
         out_specs=vmem,
         scratch_shapes=[
-            pltpu.VMEM(pa.shape, jnp.bfloat16),
-            pltpu.VMEM(pa.shape, jnp.bfloat16),
-            pltpu.VMEM(pa.shape, jnp.bfloat16),
-            pltpu.VMEM(pa.shape, jnp.bfloat16),
             pltpu.VMEM((wide, width), jnp.float32),
-            pltpu.SemaphoreType.DMA((4,)),
         ],
         compiler_params=pltpu.CompilerParams(vmem_limit_bytes=40 << 20),
         cost_estimate=pl.CostEstimate(

time: 97.8 us -> 94.1 us (0.962)
  waiting for transfers between devices: 53.6 us -> 49.9 us
  starting transfers between devices: 23.5 us -> 26.3 us
  Pallas kernels: 15.8 us -> 13.9 us
    ppermute x4, waiting for transfers between devices: 25.8 us -> 22.2 us  [swap(): return lax.ppermute(array, ('groups', 'frames'), pairs)]
    ppermute x15, starting transfers between devices: 15.6 us -> 17.5 us  [swap(): return lax.ppermute(array, 'frames', pairs)]
    pallas_call x1, Pallas kernels: 6.5 us -> 5.11 us  [per_device(): pl.pallas_call(functools.partial(tail_kernel, rows=rows), name='tail', ou...]
  transfers between devices with their start and end apart: 21 -> 21, of which waited for: 12 -> 12; matrix products, arithmetic and copies ran while one was open for 3% -> 3% of each run, Pallas kernels for 7% -> 6%
where the time goes in v4:
time: 94.1 us; the launch traced here: 93.8 us
  waiting for transfers between devices  49.9 us (53%)
  starting transfers between devices  26.3 us (28%)
  Pallas kernels  13.9 us (15%)
  other arithmetic  2.14 us (2%)
    ppermute x15, waiting for transfers between devices, swap(): return lax.ppermute(array, 'frames', pairs)  27.7 us
    ppermute x4, waiting for transfers between devices, swap(): return lax.ppermute(array, ('groups', 'frames'), pairs)  22.2 us
    ppermute x15, starting transfers between devices, swap(): return lax.ppermute(array, 'frames', pairs)  17.5 us
    pallas_call x1, Pallas kernels, per_device(): pl.pallas_call(functools.partial(attention_kernel, rows=rows, even=even,...  5.86 us
    pallas_call x1, Pallas kernels, per_device(): pl.pallas_call(functools.partial(tail_kernel, rows=rows), name='tail', ou...  5.11 us
    ppermute x4, starting transfers between devices, swap(): return lax.ppermute(array, ('groups', 'frames'), pairs)  4.46 us
    ppermute x1, starting transfers between devices, per_device(): lax.ppermute(features[-EDGE:], 'frames', [(i, i + 1) for i in range(15)])  3.03 us
    pallas_call x1, Pallas kernels, per_device(): pl.pallas_call(prepare_kernel, name='prepare', out_shape=[jax.ShapeDtypeS...  2.89 us
  transfers between devices with their start and end apart: 21, of which 12 were waited for; matrix products, arithmetic and copies ran while one was open for 3% of the time, Pallas kernels for 6%

profile of v4, /device:TPU:0, one launch (start us, length us, event | category | flops | bytes accessed | tf_op | source)
XLA Modules:
  0.0 93.8 jit_solution(2561865139408923385)
XLA Ops:
  0.7 2.9 %prepare.1 = (bf16[128,1024]{1,0:T(8,128)(2,1)}, bf16[64,384]{1,0:T(8,128)(2,1)}, bf16[64,384]{1,0:T(8,128)(2,1)}, bf16[64,384]{1,0:T(8,128)(2,1)}, bf16[64,384]{1,0:T(8,128)(2,1)}, /*index=5*/bf16[32,3584]{1,0:T(8,128)(2,1)}) custom-call(s32[1]{0:T(128)S(6)} %copy.12.scalars, bf16[128,1024]{1,0:T(8,128)(2,1)} %feats_in.1, f32[1,1024]{1,0:T(1,128)} %bitcast.7, ...), custom_call_target="tpu_custom_call" | custom-call | tf_op jit(solution)/shard_map/prepare/pallas_call | solution.py:319
  3.6 5.1 %collective-permute-start.1 = (bf16[64,384]{1,0:T(8,128)(2,1)}, bf16[64,384]{1,0:T(8,128)(2,1)S(1)}, u32[]{:S(2)}, u32[]{:S(2)}) collective-permute-start(bf16[64,384]{1,0:T(8,128)(2,1)} %get-tuple-element.27), channel_id=1, source_target_pairs={{0,12},{1,13},{2,14},{3,15},{4,8},{5,9},{6,10},{7,11},{8,4},{9,5},... | collective-permute-start | bytes 147464 | tf_op jit(solution)/shard_map/ppermute | solution.py:117
  8.7 0.6 collective-permute-start.3
  9.3 2.3 %collective-permute-start = (bf16[32,3584]{1,0:T(8,128)(2,1)}, bf16[32,3584]{1,0:T(8,128)(2,1)S(1)}, u32[]{:S(2)}, u32[]{:S(2)}) collective-permute-start(bf16[32,3584]{1,0:T(8,128)(2,1)} %get-tuple-element.25), channel_id=1, source_target_pairs={{0,8},{1,9},{2,10},{3,11},{4,12},{5,13},{6,14},{7,15},{8,0},{9,1},... | collective-permute-start | bytes 688136 | tf_op jit(solution)/shard_map/ppermute | solution.py:119
  11.6 0.8 fusion
  12.4 1.3 %collective-permute-start.7 = (bf16[16,1024]{1,0:T(8,128)(2,1)S(1)}, bf16[16,1024]{1,0:T(8,128)(2,1)S(1)}, u32[]{:S(2)}, u32[]{:S(2)}) collective-permute-start(bf16[16,1024]{1,0:T(8,128)(2,1)S(1)} %get-tuple-element.45), channel_id=1, source_target_pairs={{1,0},{2,1},{3,2},{4,3},{5,4},{6,5},{7,6},{8,7},{9,8},{10,9},{11,1... | collective-permute-start | bytes 98312 | tf_op jit(solution)/shard_map/ppermute | solution.py:341
  13.7 3.0 %collective-permute-start.6 = (bf16[16,1024]{1,0:T(8,128)(2,1)S(1)}, bf16[16,1024]{1,0:T(8,128)(2,1)S(1)}, u32[]{:S(2)}, u32[]{:S(2)}) collective-permute-start(bf16[16,1024]{1,0:T(8,128)(2,1)S(1)} %get-tuple-element.46), channel_id=1, source_target_pairs={{0,1},{1,2},{2,3},{3,4},{4,5},{5,6},{6,7},{7,8},{8,9},{9,10},{10,1... | collective-permute-start | bytes 98312 | tf_op jit(solution)/shard_map/ppermute | solution.py:340
  16.7 2.3 %collective-permute-start.5 = (bf16[128,1024]{1,0:T(8,128)(2,1)}, bf16[128,1024]{1,0:T(8,128)(2,1)S(1)}, u32[]{:S(2)}, u32[]{:S(2)}) collective-permute-start(bf16[128,1024]{1,0:T(8,128)(2,1)} %get-tuple-element.30), channel_id=1, source_target_pairs={{0,8},{1,3},{2,10},{3,1},{4,12},{5,7},{6,14},{7,5},{8,0},{9,11},{1... | collective-permute-start | bytes 786440 | tf_op jit(solution)/shard_map/ppermute | solution.py:117
  19.1 1.2 %collective-permute-done.3 = bf16[64,384]{1,0:T(8,128)(2,1)S(1)} collective-permute-done((bf16[64,384]{1,0:T(8,128)(2,1)}, bf16[64,384]{1,0:T(8,128)(2,1)S(1)}, u32[]{:S(2)}, u32[]{:S(2)}) %collective-permute-start.3) | collective-permute-done | bytes 49184 | tf_op jit(solution)/shard_map/ppermute | solution.py:117
  20.3 0.8 pad_maximum_fusion.7
  21.1 1.6 %collective-permute-start.4 = (bf16[256,384]{1,0:T(8,128)(2,1)S(1)}, bf16[256,384]{1,0:T(8,128)(2,1)S(1)}, u32[]{:S(2)}, u32[]{:S(2)}) collective-permute-start(bf16[256,384]{1,0:T(8,128)(2,1)S(1)} %pad_maximum_fusion.7), channel_id=1, source_target_pairs={{0,2},{1,3},{2,0},{3,1},{4,6},{5,7},{6,4},{7,5},{8,10},{9,11},{10,... | collective-permute-start | bytes 589832 | tf_op jit(solution)/shard_map/ppermute | solution.py:117
  22.7 4.0 %collective-permute-done = bf16[32,3584]{1,0:T(8,128)(2,1)S(1)} collective-permute-done((bf16[32,3584]{1,0:T(8,128)(2,1)}, bf16[32,3584]{1,0:T(8,128)(2,1)S(1)}, u32[]{:S(2)}, u32[]{:S(2)}) %collective-permute-start) | collective-permute-done | bytes 229408 | tf_op jit(solution)/shard_map/ppermute | solution.py:119
  26.7 1.0 %pad_maximum_fusion.4 = bf16[64,3584]{1,0:T(8,128)(2,1)S(1)} fusion(bf16[32,3584]{1,0:T(8,128)(2,1)S(1)} %collective-permute-done, bf16[32,3584]{1,0:T(8,128)(2,1)} %get-tuple-element.25), kind=kLoop, calls=%fused_computation.4 | loop fusion | flops 917504 | bytes 917504 | tf_op jit(solution)/shard_map/concatenate | solution.py:335
  27.7 0.3 collective-permute-done.4
  28.0 1.8 %collective-permute-done.5 = bf16[128,1024]{1,0:T(8,128)(2,1)S(1)} collective-permute-done((bf16[128,1024]{1,0:T(8,128)(2,1)}, bf16[128,1024]{1,0:T(8,128)(2,1)S(1)}, u32[]{:S(2)}, u32[]{:S(2)}) %collective-permute-start.5) | collective-permute-done | bytes 262176 | tf_op jit(solution)/shard_map/ppermute | solution.py:117
  30.0 2.0 %collective-permute-start.8 = (bf16[256,1024]{1,0:T(8,128)(2,1)S(1)}, bf16[256,1024]{1,0:T(8,128)(2,1)S(1)}, u32[]{:S(2)}, u32[]{:S(2)}) collective-permute-start(bf16[256,1024]{1,0:T(8,128)(2,1)S(1)} %pad_maximum_fusion.3), channel_id=1, source_target_pairs={{0,4},{1,9},{2,6},{3,11},{4,0},{5,13},{6,2},{7,15},{8,12},{9,1},{1... | collective-permute-start | bytes 1572872 | tf_op jit(solution)/shard_map/ppermute | solution.py:117
  32.0 11.0 %collective-permute-done.16 = bf16[64,3584]{1,0:T(8,128)(2,1)S(1)} collective-permute-done((bf16[64,3584]{1,0:T(8,128)(2,1)S(1)}, bf16[64,3584]{1,0:T(8,128)(2,1)S(1)}, u32[]{:S(2)}, u32[]{:S(2)}) %collective-permute-start.16) | collective-permute-done | bytes 458784 | tf_op jit(solution)/shard_map/ppermute | solution.py:119
  43.1 0.5 collective-permute-start.17
  43.6 5.0 %collective-permute-done.8 = bf16[256,1024]{1,0:T(8,128)(2,1)S(1)} collective-permute-done((bf16[256,1024]{1,0:T(8,128)(2,1)S(1)}, bf16[256,1024]{1,0:T(8,128)(2,1)S(1)}, u32[]{:S(2)}, u32[]{:S(2)}) %collective-permute-start.8) | collective-permute-done | bytes 524320 | tf_op jit(solution)/shard_map/ppermute | solution.py:117
  48.8 0.5 collective-permute-start.10
  49.3 7.2 %collective-permute-done.17 = bf16[128,3584]{1,0:T(8,128)(2,1)S(1)} collective-permute-done((bf16[128,3584]{1,0:T(8,128)(2,1)S(1)}, bf16[128,3584]{1,0:T(8,128)(2,1)S(1)}, u32[]{:S(2)}, u32[]{:S(2)}) %collective-permute-start.17) | collective-permute-done | bytes 917536 | tf_op jit(solution)/shard_map/ppermute | solution.py:119
  56.7 1.6 %collective-permute-start.18 = (bf16[256,3584]{1,0:T(8,128)(2,1)S(1)}, bf16[256,3584]{1,0:T(8,128)(2,1)S(1)}, u32[]{:S(2)}, u32[]{:S(2)}) collective-permute-start(bf16[256,3584]{1,0:T(8,128)(2,1)S(1)} %pad_maximum_fusion.pa), channel_id=1, source_target_pairs={{0,16},{1,5},{2,18},{3,7},{4,20},{5,1},{6,22},{7,3},{8,24},{9,13},... | collective-permute-start | bytes 5505032 | tf_op jit(solution)/shard_map/ppermute | solution.py:119
  58.3 9.5 %collective-permute-done.10.xb = bf16[512,1024]{1,0:T(8,128)(2,1)S(1)} collective-permute-done((bf16[512,1024]{1,0:T(8,128)(2,1)S(1)}, bf16[512,1024]{1,0:T(8,128)(2,1)S(1)}, u32[]{:S(2)}, u32[]{:S(2)}) %collective-permute-start.10) | collective-permute-done | bytes 1048608 | tf_op jit(solution)/shard_map/ppermute | solution.py:117
  67.8 2.7 %collective-permute-done.12.xb_other = bf16[512,1024]{1,0:T(8,128)(2,1)S(1)} collective-permute-done((bf16[512,1024]{1,0:T(8,128)(2,1)S(1)}, bf16[512,1024]{1,0:T(8,128)(2,1)S(1)}, u32[]{:S(2)}, u32[]{:S(2)}) %collective-permute-start.12) | collective-permute-done | bytes 1048608 | tf_op jit(solution)/shard_map/ppermute | solution.py:117
  70.4 5.9 %attention.1 = (bf16[160,128]{1,0:T(8,128)(2,1)S(1)}, bf16[160,128]{1,0:T(8,128)(2,1)S(1)}, bf16[160,128]{1,0:T(8,128)(2,1)S(1)}, bf16[160,128]{1,0:T(8,128)(2,1)S(1)}) custom-call(s32[1]{0:T(128)S(6)} %copy.12.scalars, bf16[512,1024]{1,0:T(8,128)(2,1)S(1)} %pad_maximum_fusion.1.xa, bf16[512,1024]{1,0:T(8,128)(2,1)S(1)} %collective-permute-done.10.xb, ...), custom_call_target="tpu_custom_call" | custom-call | flops 5000000000 | bytes 8388608 | tf_op jit(solution)/shard_map/attention/pallas_call | solution.py:365
  76.3 3.0 %collective-permute-start.13 = (bf16[160,128]{1,0:T(8,128)(2,1)S(1)}, bf16[160,128]{1,0:T(8,128)(2,1)S(1)}, u32[]{:S(2)}, u32[]{:S(2)}) collective-permute-start(bf16[160,128]{1,0:T(8,128)(2,1)S(1)} %get-tuple-element.38), channel_id=1, source_target_pairs={{0,12},{1,13},{2,14},{3,15},{4,8},{5,9},{6,10},{7,11},{8,4},{9,5},... | collective-permute-start | bytes 122888 | tf_op jit(solution)/shard_map/ppermute | solution.py:117
  79.3 1.5 %collective-permute-start.15 = (bf16[160,128]{1,0:T(8,128)(2,1)S(1)}, bf16[160,128]{1,0:T(8,128)(2,1)S(1)}, u32[]{:S(2)}, u32[]{:S(2)}) collective-permute-start(bf16[160,128]{1,0:T(8,128)(2,1)S(1)} %get-tuple-element.40), channel_id=1, source_target_pairs={{0,8},{1,9},{2,10},{3,11},{4,12},{5,13},{6,14},{7,15},{8,0},{9,1},... | collective-permute-start | bytes 122888 | tf_op jit(solution)/shard_map/ppermute | solution.py:117
  80.7 2.0 %collective-permute-done.13.c1 = bf16[160,128]{1,0:T(8,128)(2,1)S(1)} collective-permute-done((bf16[160,128]{1,0:T(8,128)(2,1)S(1)}, bf16[160,128]{1,0:T(8,128)(2,1)S(1)}, u32[]{:S(2)}, u32[]{:S(2)}) %collective-permute-start.13) | collective-permute-done | bytes 40992 | tf_op jit(solution)/shard_map/ppermute | solution.py:117
  82.7 1.8 %collective-permute-done.14.c2 = bf16[160,128]{1,0:T(8,128)(2,1)S(1)} collective-permute-done((bf16[160,128]{1,0:T(8,128)(2,1)S(1)}, bf16[160,128]{1,0:T(8,128)(2,1)S(1)}, u32[]{:S(2)}, u32[]{:S(2)}) %collective-permute-start.14) | collective-permute-done | bytes 40992 | tf_op jit(solution)/shard_map/ppermute | solution.py:117
  84.5 0.7 collective-permute-start.20
  85.3 3.4 %collective-permute-done.20.pb_other = bf16[256,3584]{1,0:T(8,128)(2,1)S(1)} collective-permute-done((bf16[256,3584]{1,0:T(8,128)(2,1)S(1)}, bf16[256,3584]{1,0:T(8,128)(2,1)S(1)}, u32[]{:S(2)}, u32[]{:S(2)}) %collective-permute-start.20) | collective-permute-done | bytes 1835040 | tf_op jit(solution)/shard_map/ppermute | solution.py:117
  88.7 5.1 %tail.1 = bf16[128,1024]{1,0:T(8,128)(2,1)} custom-call(s32[1]{0:T(128)S(6)} %copy.12.scalars, bf16[160,128]{1,0:T(8,128)(2,1)S(1)} %get-tuple-element.37.c0, bf16[160,128]{1,0:T(8,128)(2,1)S(1)} %collective-permute-done.13.c1, bf16[160,128]{1,0:T(8,128)(2,1)S(1)} %collective-permute-done.14.c2, bf16[160,128]{1,0:T(8,128)(2,1)S(1)} %collective-permute-done.15.c3, ...), custom_call_target="tpu_custom_call" | custom-call | flops 1200000000 | bytes 8388608 | tf_op jit(solution)/shard_map/tail/pallas_call | solution.py:390
  (34 shorter events, 0.6 us)
Async XLA Ops:
  3.5 26.3 %copy-start.5 = (bf16[128,1024]{1,0:T(8,128)(2,1)S(1)}, bf16[128,1024]{1,0:T(8,128)(2,1)}, u32[]{:S(2)}) copy-start(bf16[128,1024]{1,0:T(8,128)(2,1)} %get-tuple-element.30) | copy-start | bytes 786436
  3.6 10.1 %collective-permute-start.1 = (bf16[64,384]{1,0:T(8,128)(2,1)}, bf16[64,384]{1,0:T(8,128)(2,1)S(1)}, u32[]{:S(2)}, u32[]{:S(2)}) collective-permute-start(bf16[64,384]{1,0:T(8,128)(2,1)} %get-tuple-element.27), channel_id=1, source_target_pairs={{0,12},{1,13},{2,14},{3,15},{4,8},{5,9},{6,10},{7,11},{8,4},{9,5},... | collective-permute-start | bytes 147464 | tf_op jit(solution)/shard_map/ppermute | solution.py:117
  8.7 8.0 %collective-permute-start.2 = (bf16[64,384]{1,0:T(8,128)(2,1)}, bf16[64,384]{1,0:T(8,128)(2,1)S(1)}, u32[]{:S(2)}, u32[]{:S(2)}) collective-permute-start(bf16[64,384]{1,0:T(8,128)(2,1)} %get-tuple-element.28), channel_id=1, source_target_pairs={{0,4},{1,5},{2,6},{3,7},{4,0},{5,1},{6,2},{7,3},{8,12},{9,13},{10,... | collective-permute-start | bytes 147464 | tf_op jit(solution)/shard_map/ppermute | solution.py:117
  8.7 11.6 %collective-permute-start.3 = (bf16[64,384]{1,0:T(8,128)(2,1)}, bf16[64,384]{1,0:T(8,128)(2,1)S(1)}, u32[]{:S(2)}, u32[]{:S(2)}) collective-permute-start(bf16[64,384]{1,0:T(8,128)(2,1)} %get-tuple-element.29), channel_id=1, source_target_pairs={{0,8},{1,9},{2,10},{3,11},{4,12},{5,13},{6,14},{7,15},{8,0},{9,1},... | collective-permute-start | bytes 147464 | tf_op jit(solution)/shard_map/ppermute | solution.py:117
  9.3 17.4 %collective-permute-start = (bf16[32,3584]{1,0:T(8,128)(2,1)}, bf16[32,3584]{1,0:T(8,128)(2,1)S(1)}, u32[]{:S(2)}, u32[]{:S(2)}) collective-permute-start(bf16[32,3584]{1,0:T(8,128)(2,1)} %get-tuple-element.25), channel_id=1, source_target_pairs={{0,8},{1,9},{2,10},{3,11},{4,12},{5,13},{6,14},{7,15},{8,0},{9,1},... | collective-permute-start | bytes 688136 | tf_op jit(solution)/shard_map/ppermute | solution.py:119
  12.4 17.5 %collective-permute-start.7 = (bf16[16,1024]{1,0:T(8,128)(2,1)S(1)}, bf16[16,1024]{1,0:T(8,128)(2,1)S(1)}, u32[]{:S(2)}, u32[]{:S(2)}) collective-permute-start(bf16[16,1024]{1,0:T(8,128)(2,1)S(1)} %get-tuple-element.45), channel_id=1, source_target_pairs={{1,0},{2,1},{3,2},{4,3},{5,4},{6,5},{7,6},{8,7},{9,8},{10,9},{11,1... | collective-permute-start | bytes 98312 | tf_op jit(solution)/shard_map/ppermute | solution.py:341
  13.7 16.2 %collective-permute-start.6 = (bf16[16,1024]{1,0:T(8,128)(2,1)S(1)}, bf16[16,1024]{1,0:T(8,128)(2,1)S(1)}, u32[]{:S(2)}, u32[]{:S(2)}) collective-permute-start(bf16[16,1024]{1,0:T(8,128)(2,1)S(1)} %get-tuple-element.46), channel_id=1, source_target_pairs={{0,1},{1,2},{2,3},{3,4},{4,5},{5,6},{6,7},{7,8},{8,9},{9,10},{10,1... | collective-permute-start | bytes 98312 | tf_op jit(solution)/shard_map/ppermute | solution.py:340
  16.7 13.1 %collective-permute-start.5 = (bf16[128,1024]{1,0:T(8,128)(2,1)}, bf16[128,1024]{1,0:T(8,128)(2,1)S(1)}, u32[]{:S(2)}, u32[]{:S(2)}) collective-permute-start(bf16[128,1024]{1,0:T(8,128)(2,1)} %get-tuple-element.30), channel_id=1, source_target_pairs={{0,8},{1,3},{2,10},{3,1},{4,12},{5,7},{6,14},{7,5},{8,0},{9,11},{1... | collective-permute-start | bytes 786440 | tf_op jit(solution)/shard_map/ppermute | solution.py:117
  21.1 6.9 %collective-permute-start.4 = (bf16[256,384]{1,0:T(8,128)(2,1)S(1)}, bf16[256,384]{1,0:T(8,128)(2,1)S(1)}, u32[]{:S(2)}, u32[]{:S(2)}) collective-permute-start(bf16[256,384]{1,0:T(8,128)(2,1)S(1)} %pad_maximum_fusion.7), channel_id=1, source_target_pairs={{0,2},{1,3},{2,0},{3,1},{4,6},{5,7},{6,4},{7,5},{8,10},{9,11},{10,... | collective-permute-start | bytes 589832 | tf_op jit(solution)/shard_map/ppermute | solution.py:117
  29.9 13.1 %collective-permute-start.16 = (bf16[64,3584]{1,0:T(8,128)(2,1)S(1)}, bf16[64,3584]{1,0:T(8,128)(2,1)S(1)}, u32[]{:S(2)}, u32[]{:S(2)}) collective-permute-start(bf16[64,3584]{1,0:T(8,128)(2,1)S(1)} %pad_maximum_fusion.4), channel_id=1, source_target_pairs={{0,4},{1,3},{2,6},{3,1},{4,0},{5,7},{6,2},{7,5},{8,12},{9,11},{10,... | collective-permute-start | bytes 1376264 | tf_op jit(solution)/shard_map/ppermute | solution.py:119
  30.0 18.6 %collective-permute-start.8 = (bf16[256,1024]{1,0:T(8,128)(2,1)S(1)}, bf16[256,1024]{1,0:T(8,128)(2,1)S(1)}, u32[]{:S(2)}, u32[]{:S(2)}) collective-permute-start(bf16[256,1024]{1,0:T(8,128)(2,1)S(1)} %pad_maximum_fusion.3), channel_id=1, source_target_pairs={{0,4},{1,9},{2,6},{3,11},{4,0},{5,13},{6,2},{7,15},{8,12},{9,1},{1... | collective-permute-start | bytes 1572872 | tf_op jit(solution)/shard_map/ppermute | solution.py:117
  43.1 13.5 %collective-permute-start.17 = (bf16[128,3584]{1,0:T(8,128)(2,1)S(1)}, bf16[128,3584]{1,0:T(8,128)(2,1)S(1)}, u32[]{:S(2)}, u32[]{:S(2)}) collective-permute-start(bf16[128,3584]{1,0:T(8,128)(2,1)S(1)} %pad_maximum_fusion.2), channel_id=1, source_target_pairs={{0,2},{1,17},{2,0},{3,19},{4,6},{5,21},{6,4},{7,23},{8,10},{9,25},... | collective-permute-start | bytes 2752520 | tf_op jit(solution)/shard_map/ppermute | solution.py:119
  43.6 5.1 %collective-permute-start.9 = (bf16[512,384]{1,0:T(8,128)(2,1)S(1)}, bf16[512,384]{1,0:T(8,128)(2,1)S(1)}, u32[]{:S(2)}, u32[]{:S(2)}) collective-permute-start(bf16[512,384]{1,0:T(8,128)(2,1)S(1)} %pad_maximum_fusion.5.own_w), channel_id=1, source_target_pairs={{0,1},{1,0},{2,3},{3,2},{4,5},{5,4},{6,7},{7,6},{8,9},{9,8},{10,11... | collective-permute-start | bytes 1179656 | tf_op jit(solution)/shard_map/ppermute | solution.py:117
  48.7 9.6 %collective-permute-start.11 = (bf16[512,1024]{1,0:T(8,128)(2,1)S(1)}, bf16[512,1024]{1,0:T(8,128)(2,1)S(1)}, u32[]{:S(2)}, u32[]{:S(2)}) collective-permute-start(bf16[512,1024]{1,0:T(8,128)(2,1)S(1)} %pad_maximum_fusion.1.xa), channel_id=1, source_target_pairs={{0,1},{1,0},{2,3},{3,2},{4,5},{5,4},{6,7},{7,6},{8,9},{9,8},{10,11... | collective-permute-start | bytes 3145736 | tf_op jit(solution)/shard_map/ppermute | solution.py:117
  48.8 19.0 %collective-permute-start.10 = (bf16[512,1024]{1,0:T(8,128)(2,1)S(1)}, bf16[512,1024]{1,0:T(8,128)(2,1)S(1)}, u32[]{:S(2)}, u32[]{:S(2)}) collective-permute-start(bf16[512,1024]{1,0:T(8,128)(2,1)S(1)} %pad_maximum_fusion.1.xa), channel_id=1, source_target_pairs={{0,2},{1,5},{2,0},{3,7},{4,6},{5,1},{6,4},{7,3},{8,10},{9,13},{10,... | collective-permute-start | bytes 3145736 | tf_op jit(solution)/shard_map/ppermute | solution.py:117
  56.6 28.6 %copy-start.4 = (bf16[128,1024]{1,0:T(8,128)(2,1)S(1)}, bf16[128,1024]{1,0:T(8,128)(2,1)}, u32[]{:S(2)}) copy-start(bf16[128,1024]{1,0:T(8,128)(2,1)} %feats_in.1) | copy-start | bytes 786436
  56.6 32.0 %copy-start = (f32[9,1024]{1,0:T(8,128)S(1)}, f32[9,1024]{1,0:T(8,128)}, u32[]{:S(2)}) copy-start(f32[9,1024]{1,0:T(8,128)} %taps.1) | copy-start | bytes 110596
  56.7 32.0 %copy-start.1 = (f32[1024]{0:T(1024)S(1)}, f32[1024]{0:T(1024)}, u32[]{:S(2)}) copy-start(f32[1024]{0:T(1024)} %param.16) | copy-start | bytes 12292
  56.7 32.0 %copy-start.2 = (f32[1024]{0:T(1024)S(1)}, f32[1024]{0:T(1024)}, u32[]{:S(2)}) copy-start(f32[1024]{0:T(1024)} %param.19) | copy-start | bytes 12292
  56.7 32.0 %copy-start.3 = (f32[1024]{0:T(1024)S(1)}, f32[1024]{0:T(1024)}, u32[]{:S(2)}) copy-start(f32[1024]{0:T(1024)} %param.20) | copy-start | bytes 12292
  56.7 27.8 %collective-permute-start.18 = (bf16[256,3584]{1,0:T(8,128)(2,1)S(1)}, bf16[256,3584]{1,0:T(8,128)(2,1)S(1)}, u32[]{:S(2)}, u32[]{:S(2)}) collective-permute-start(bf16[256,3584]{1,0:T(8,128)(2,1)S(1)} %pad_maximum_fusion.pa), channel_id=1, source_target_pairs={{0,16},{1,5},{2,18},{3,7},{4,20},{5,1},{6,22},{7,3},{8,24},{9,13},... | collective-permute-start | bytes 5505032 | tf_op jit(solution)/shard_map/ppermute | solution.py:119
  67.7 2.7 %collective-permute-start.12 = (bf16[512,1024]{1,0:T(8,128)(2,1)S(1)}, bf16[512,1024]{1,0:T(8,128)(2,1)S(1)}, u32[]{:S(2)}, u32[]{:S(2)}) collective-permute-start(bf16[512,1024]{1,0:T(8,128)(2,1)S(1)} %collective-permute-done.10.xb), channel_id=1, source_target_pairs={{0,1},{1,0},{2,3},{3,2},{4,5},{5,4},{6,7},{7,6},{8,9},{9,8},{10,11... | collective-permute-start | bytes 3145736 | tf_op jit(solution)/shard_map/ppermute | solution.py:117
  76.3 6.5 %collective-permute-start.13 = (bf16[160,128]{1,0:T(8,128)(2,1)S(1)}, bf16[160,128]{1,0:T(8,128)(2,1)S(1)}, u32[]{:S(2)}, u32[]{:S(2)}) collective-permute-start(bf16[160,128]{1,0:T(8,128)(2,1)S(1)} %get-tuple-element.38), channel_id=1, source_target_pairs={{0,12},{1,13},{2,14},{3,15},{4,8},{5,9},{6,10},{7,11},{8,4},{9,5},... | collective-permute-start | bytes 122888 | tf_op jit(solution)/shard_map/ppermute | solution.py:117
  79.2 5.3 %collective-permute-start.14 = (bf16[160,128]{1,0:T(8,128)(2,1)S(1)}, bf16[160,128]{1,0:T(8,128)(2,1)S(1)}, u32[]{:S(2)}, u32[]{:S(2)}) collective-permute-start(bf16[160,128]{1,0:T(8,128)(2,1)S(1)} %get-tuple-element.39), channel_id=1, source_target_pairs={{0,4},{1,5},{2,6},{3,7},{4,0},{5,1},{6,2},{7,3},{8,12},{9,13},{10,... | collective-permute-start | bytes 122888 | tf_op jit(solution)/shard_map/ppermute | solution.py:117
  79.3 5.3 %collective-permute-start.15 = (bf16[160,128]{1,0:T(8,128)(2,1)S(1)}, bf16[160,128]{1,0:T(8,128)(2,1)S(1)}, u32[]{:S(2)}, u32[]{:S(2)}) collective-permute-start(bf16[160,128]{1,0:T(8,128)(2,1)S(1)} %get-tuple-element.40), channel_id=1, source_target_pairs={{0,8},{1,9},{2,10},{3,11},{4,12},{5,13},{6,14},{7,15},{8,0},{9,1},... | collective-permute-start | bytes 122888 | tf_op jit(solution)/shard_map/ppermute | solution.py:117
  80.7 4.6 %collective-permute-start.19 = (bf16[256,3584]{1,0:T(8,128)(2,1)S(1)}, bf16[256,3584]{1,0:T(8,128)(2,1)S(1)}, u32[]{:S(2)}, u32[]{:S(2)}) collective-permute-start(bf16[256,3584]{1,0:T(8,128)(2,1)S(1)} %pad_maximum_fusion.pa), channel_id=1, source_target_pairs={{0,1},{1,0},{2,3},{3,2},{4,5},{5,4},{6,7},{7,6},{8,9},{9,8},{10,11... | collective-permute-start | bytes 5505032 | tf_op jit(solution)/shard_map/ppermute | solution.py:117
  84.5 4.1 %collective-permute-start.20 = (bf16[256,3584]{1,0:T(8,128)(2,1)S(1)}, bf16[256,3584]{1,0:T(8,128)(2,1)S(1)}, u32[]{:S(2)}, u32[]{:S(2)}) collective-permute-start(bf16[256,3584]{1,0:T(8,128)(2,1)S(1)} %collective-permute-done.18.pb), channel_id=1, source_target_pairs={{0,1},{1,0},{2,3},{3,2},{4,5},{5,4},{6,7},{7,6},{8,9},{9,8},{10,11... | collective-permute-start | bytes 5505032 | tf_op jit(solution)/shard_map/ppermute | solution.py:117

commit v5 on v4

--- a/solution.py
+++ b/solution.py
@@ -17,8 +17,8 @@
 
 ORDER_EVEN = (8, 4, 2)
 ORDER_ODD = (2, 8, 4)
-PACK_EVEN = (8, 4, 2, 16)
-PACK_ODD = (8, 2, 16, 4)
+PACK_EVEN = (8, 2, 16, 4)
+PACK_ODD = (8, 4, 16, 2)
 ALONG_Z = (0, 12, 4, 8)
 
 
@@ -168,39 +168,28 @@
 def attention_kernel(
     scalars, xa, xb, xa_other, xb_other, own_w, other_w, *refs, rows, even, odd, w_masks, count
 ):
-    outs, (x_all, w_all, keys, values, sems) = refs[:4], refs[4:]
+    outs, (x_all, w_all, keys, values) = refs[:4], refs[4:]
     me, limit = lax.axis_index("frames"), scalars[0]
     depth = w_all.shape[0] // 16
-    for other_core, (xs, ws) in enumerate((((xa, xb), own_w), ((xa_other, xb_other), other_w))):
-        for j in range(8):
-            src = source_of(me, j, w_masks, w_masks, other_core)
-            pltpu.make_async_copy(
-                ws.at[pl.ds(j * depth, depth)],
-                w_all.at[pl.ds(pl.multiple_of(src * depth, depth), depth)],
-                sems.at[0],
-            ).start()
-        for j in range(8):
-            src = source_of(me, j, even, odd, other_core)
-            pltpu.make_async_copy(
-                xs[j // 4].at[pl.ds((j % 4) * rows, rows)],
-                x_all.at[pl.ds(pl.multiple_of(EDGE + src * rows, EDGE), rows)],
-                sems.at[1],
-            ).start()
     width = x_all.shape[1]
     x_all[0:EDGE, :] = jnp.zeros((EDGE, width), jnp.bfloat16)
     x_all[EDGE + count : 2 * EDGE + count, :] = jnp.zeros((EDGE, width), jnp.bfloat16)
-    pltpu.make_async_copy(w_all, w_all, sems.at[0]).wait()
-    inner = x_all.at[pl.ds(EDGE, count)]
-    pltpu.make_async_copy(inner, inner, sems.at[1]).wait()
-    step = 512
-    for r in range(count // step):
+    for other_core, ws in enumerate((own_w, other_w)):
+        for j in range(8):
+            src = source_of(me, j, w_masks, w_masks, other_core)
+            row = pl.multiple_of(src * depth, depth)
+            w_all[pl.ds(row, depth), :] = ws[j * depth : (j + 1) * depth, :]
+    for part, xs in enumerate((xa, xb, xa_other, xb_other)):
         both = jnp.dot(
-            x_all[EDGE + r * step : EDGE + (r + 1) * step, :],
-            w_all[:, HD:],
-            preferred_element_type=jnp.float32,
+            xs[...], w_all[:, HD:], preferred_element_type=jnp.float32
         ).astype(jnp.bfloat16)
-        keys[r * step : (r + 1) * step, :] = both[:, :HD]
-        values[r * step : (r + 1) * step, :] = both[:, HD:]
+        for i in range(4):
+            src = source_of(me, 4 * (part % 2) + i, even, odd, part // 2)
+            row = pl.multiple_of(src * rows, rows)
+            here = slice(i * rows, (i + 1) * rows)
+            keys[pl.ds(row, rows), :] = both[here, :HD]
+            values[pl.ds(row, rows), :] = both[here, HD:]
+            x_all[pl.ds(pl.multiple_of(row + EDGE, EDGE), rows), :] = xs[here, :]
     wide = rows + 2 * EDGE
     position = lax.broadcasted_iota(jnp.int32, (1, count), 1)
     valid = position < limit
@@ -311,7 +300,6 @@
     groups = lax.axis_size("groups")
     scalars = valid_length
     even, odd = block_masks(ORDER_EVEN), block_masks(ORDER_ODD)
-    any_spec = pl.BlockSpec(memory_space=pl.ANY)
     hbm = pl.BlockSpec(memory_space=pltpu.HBM)
     smem = pl.BlockSpec(memory_space=pltpu.SMEM)
     vmem = pl.BlockSpec(memory_space=pltpu.VMEM)
@@ -355,7 +343,6 @@
     xb = swap(xa, ORDER_EVEN[2], ORDER_ODD[2])
     xa_other = swap(xa, 1)
     pa = joined(p4, pack_swap(p4, 2))
-    xb, xa_other = lax.optimization_barrier((xb, xa_other))
     xb_other = swap(xb, 1)
     pb = pack_swap(pa, 3)
     pa_other = swap(pa, 1)
@@ -368,14 +355,13 @@
         ),
         name="attention",
         out_shape=[jax.ShapeDtypeStruct((wide, HD), jnp.bfloat16)] * 4,
-        in_specs=[smem] + [any_spec] * 6,
+        in_specs=[smem] + [vmem] * 6,
         out_specs=[vmem] * 4,
         scratch_shapes=[
             pltpu.VMEM((count + 2 * EDGE, width), jnp.bfloat16),
             pltpu.VMEM((16 * depth, 3 * HD), jnp.bfloat16),
             pltpu.VMEM((count, HD), jnp.bfloat16),
             pltpu.VMEM((count, HD), jnp.bfloat16),
-            pltpu.SemaphoreType.DMA((2,)),
         ],
         compiler_params=pltpu.CompilerParams(vmem_limit_bytes=40 << 20),
         cost_estimate=pl.CostEstimate(

time: 94.1 us -> 93.5 us (level)
  starting transfers between devices: 26.3 us -> 35.7 us
  waiting for transfers between devices: 49.9 us -> 40.9 us
  Pallas kernels: 13.9 us -> 12.8 us
    ppermute x15, starting transfers between devices: 17.5 us -> 26.2 us  [swap(): return lax.ppermute(array, 'frames', pairs)]
    ppermute x15, waiting for transfers between devices: 27.7 us -> 20.6 us  [swap(): return lax.ppermute(array, 'frames', pairs)]
    ppermute x4, waiting for transfers between devices: 22.2 us -> 20.2 us  [swap(): return lax.ppermute(array, ('groups', 'frames'), pairs)]
    pallas_call x1, Pallas kernels: 5.86 us -> 4.78 us  [per_device(): pl.pallas_call(functools.partial(attention_kernel, rows=rows, even=even,...]
  transfers between devices with their start and end apart: 21 -> 21, of which waited for: 12 -> 11; matrix products, arithmetic and copies ran while one was open for 3% -> 3% of each run, Pallas kernels for 6% -> 5%
where the time goes in v5:
time: 93.5 us; the launch traced here: 93.1 us
  waiting for transfers between devices  40.9 us (44%)
  starting transfers between devices  35.7 us (38%)
  Pallas kernels  12.8 us (14%)
  other arithmetic  2.13 us (2%)
    ppermute x15, starting transfers between devices, swap(): return lax.ppermute(array, 'frames', pairs)  26.2 us
    ppermute x15, waiting for transfers between devices, swap(): return lax.ppermute(array, 'frames', pairs)  20.6 us
    ppermute x4, waiting for transfers between devices, swap(): return lax.ppermute(array, ('groups', 'frames'), pairs)  20.2 us
    ppermute x4, starting transfers between devices, swap(): return lax.ppermute(array, ('groups', 'frames'), pairs)  5.15 us
    pallas_call x1, Pallas kernels, per_device(): pl.pallas_call(functools.partial(tail_kernel, rows=rows), name='tail', ou...  5.11 us
    pallas_call x1, Pallas kernels, per_device(): pl.pallas_call(functools.partial(attention_kernel, rows=rows, even=even,...  4.78 us
    ppermute x1, starting transfers between devices, per_device(): lax.ppermute(features[-EDGE:], 'frames', [(i, i + 1) for i in range(15)])  3.03 us
    pallas_call x1, Pallas kernels, per_device(): pl.pallas_call(prepare_kernel, name='prepare', out_shape=[jax.ShapeDtypeS...  2.89 us
  transfers between devices with their start and end apart: 21, of which 11 were waited for; matrix products, arithmetic and copies ran while one was open for 3% of the time, Pallas kernels for 5%

profile of v5, /device:TPU:0, one launch (start us, length us, event | category | flops | bytes accessed | tf_op | source)
XLA Modules:
  0.0 93.1 jit_solution(10464464172247269008)
XLA Ops:
  0.7 2.9 %prepare.1 = (bf16[128,1024]{1,0:T(8,128)(2,1)}, bf16[64,384]{1,0:T(8,128)(2,1)}, bf16[64,384]{1,0:T(8,128)(2,1)}, bf16[64,384]{1,0:T(8,128)(2,1)}, bf16[64,384]{1,0:T(8,128)(2,1)}, /*index=5*/bf16[32,3584]{1,0:T(8,128)(2,1)}) custom-call(s32[1]{0:T(128)S(6)} %copy.12.scalars, bf16[128,1024]{1,0:T(8,128)(2,1)} %feats_in.1, f32[1,1024]{1,0:T(1,128)} %bitcast.7, ...), custom_call_target="tpu_custom_call" | custom-call | tf_op jit(solution)/shard_map/prepare/pallas_call | solution.py:307
  3.6 5.1 %collective-permute-start.1 = (bf16[64,384]{1,0:T(8,128)(2,1)}, bf16[64,384]{1,0:T(8,128)(2,1)S(1)}, u32[]{:S(2)}, u32[]{:S(2)}) collective-permute-start(bf16[64,384]{1,0:T(8,128)(2,1)} %get-tuple-element.25), channel_id=1, source_target_pairs={{0,12},{1,13},{2,14},{3,15},{4,8},{5,9},{6,10},{7,11},{8,4},{9,5},... | collective-permute-start | bytes 147464 | tf_op jit(solution)/shard_map/ppermute | solution.py:117
  8.7 0.6 collective-permute-start.3
  9.3 2.3 %collective-permute-start = (bf16[32,3584]{1,0:T(8,128)(2,1)}, bf16[32,3584]{1,0:T(8,128)(2,1)S(1)}, u32[]{:S(2)}, u32[]{:S(2)}) collective-permute-start(bf16[32,3584]{1,0:T(8,128)(2,1)} %get-tuple-element.23), channel_id=1, source_target_pairs={{0,8},{1,9},{2,10},{3,11},{4,12},{5,13},{6,14},{7,15},{8,0},{9,1},... | collective-permute-start | bytes 688136 | tf_op jit(solution)/shard_map/ppermute | solution.py:119
  11.6 0.8 fusion
  12.4 1.3 %collective-permute-start.7 = (bf16[16,1024]{1,0:T(8,128)(2,1)S(1)}, bf16[16,1024]{1,0:T(8,128)(2,1)S(1)}, u32[]{:S(2)}, u32[]{:S(2)}) collective-permute-start(bf16[16,1024]{1,0:T(8,128)(2,1)S(1)} %get-tuple-element.41), channel_id=1, source_target_pairs={{1,0},{2,1},{3,2},{4,3},{5,4},{6,5},{7,6},{8,7},{9,8},{10,9},{11,1... | collective-permute-start | bytes 98312 | tf_op jit(solution)/shard_map/ppermute | solution.py:329
  13.7 3.0 %collective-permute-start.6 = (bf16[16,1024]{1,0:T(8,128)(2,1)S(1)}, bf16[16,1024]{1,0:T(8,128)(2,1)S(1)}, u32[]{:S(2)}, u32[]{:S(2)}) collective-permute-start(bf16[16,1024]{1,0:T(8,128)(2,1)S(1)} %get-tuple-element.42), channel_id=1, source_target_pairs={{0,1},{1,2},{2,3},{3,4},{4,5},{5,6},{6,7},{7,8},{8,9},{9,10},{10,1... | collective-permute-start | bytes 98312 | tf_op jit(solution)/shard_map/ppermute | solution.py:328
  16.7 2.3 %collective-permute-start.5 = (bf16[128,1024]{1,0:T(8,128)(2,1)}, bf16[128,1024]{1,0:T(8,128)(2,1)S(1)}, u32[]{:S(2)}, u32[]{:S(2)}) collective-permute-start(bf16[128,1024]{1,0:T(8,128)(2,1)} %get-tuple-element.28), channel_id=1, source_target_pairs={{0,8},{1,3},{2,10},{3,1},{4,12},{5,7},{6,14},{7,5},{8,0},{9,11},{1... | collective-permute-start | bytes 786440 | tf_op jit(solution)/shard_map/ppermute | solution.py:117
  19.1 1.2 %collective-permute-done.3 = bf16[64,384]{1,0:T(8,128)(2,1)S(1)} collective-permute-done((bf16[64,384]{1,0:T(8,128)(2,1)}, bf16[64,384]{1,0:T(8,128)(2,1)S(1)}, u32[]{:S(2)}, u32[]{:S(2)}) %collective-permute-start.3) | collective-permute-done | bytes 49184 | tf_op jit(solution)/shard_map/ppermute | solution.py:117
  20.3 0.8 pad_maximum_fusion.7
  21.1 1.6 %collective-permute-start.4 = (bf16[256,384]{1,0:T(8,128)(2,1)S(1)}, bf16[256,384]{1,0:T(8,128)(2,1)S(1)}, u32[]{:S(2)}, u32[]{:S(2)}) collective-permute-start(bf16[256,384]{1,0:T(8,128)(2,1)S(1)} %pad_maximum_fusion.7), channel_id=1, source_target_pairs={{0,2},{1,3},{2,0},{3,1},{4,6},{5,7},{6,4},{7,5},{8,10},{9,11},{10,... | collective-permute-start | bytes 589832 | tf_op jit(solution)/shard_map/ppermute | solution.py:117
  22.7 4.0 %collective-permute-done = bf16[32,3584]{1,0:T(8,128)(2,1)S(1)} collective-permute-done((bf16[32,3584]{1,0:T(8,128)(2,1)}, bf16[32,3584]{1,0:T(8,128)(2,1)S(1)}, u32[]{:S(2)}, u32[]{:S(2)}) %collective-permute-start) | collective-permute-done | bytes 229408 | tf_op jit(solution)/shard_map/ppermute | solution.py:119
  26.7 1.0 %pad_maximum_fusion.4 = bf16[64,3584]{1,0:T(8,128)(2,1)S(1)} fusion(bf16[32,3584]{1,0:T(8,128)(2,1)S(1)} %collective-permute-done, bf16[32,3584]{1,0:T(8,128)(2,1)} %get-tuple-element.23), kind=kLoop, calls=%fused_computation.4 | loop fusion | flops 917504 | bytes 917504 | tf_op jit(solution)/shard_map/concatenate | solution.py:323
  27.7 0.3 collective-permute-done.4
  28.0 1.8 %collective-permute-done.5 = bf16[128,1024]{1,0:T(8,128)(2,1)S(1)} collective-permute-done((bf16[128,1024]{1,0:T(8,128)(2,1)}, bf16[128,1024]{1,0:T(8,128)(2,1)S(1)}, u32[]{:S(2)}, u32[]{:S(2)}) %collective-permute-start.5) | collective-permute-done | bytes 262176 | tf_op jit(solution)/shard_map/ppermute | solution.py:117
  29.9 1.2 %collective-permute-start.16 = (bf16[64,3584]{1,0:T(8,128)(2,1)S(1)}, bf16[64,3584]{1,0:T(8,128)(2,1)S(1)}, u32[]{:S(2)}, u32[]{:S(2)}) collective-permute-start(bf16[64,3584]{1,0:T(8,128)(2,1)S(1)} %pad_maximum_fusion.4), channel_id=1, source_target_pairs={{0,2},{1,5},{2,0},{3,7},{4,6},{5,1},{6,4},{7,3},{8,10},{9,13},{10,... | collective-permute-start | bytes 1376264 | tf_op jit(solution)/shard_map/ppermute | solution.py:119
  31.1 7.3 %collective-permute-done.16 = bf16[64,3584]{1,0:T(8,128)(2,1)S(1)} collective-permute-done((bf16[64,3584]{1,0:T(8,128)(2,1)S(1)}, bf16[64,3584]{1,0:T(8,128)(2,1)S(1)}, u32[]{:S(2)}, u32[]{:S(2)}) %collective-permute-start.16) | collective-permute-done | bytes 458784 | tf_op jit(solution)/shard_map/ppermute | solution.py:119
  38.5 1.6 %collective-permute-start.17 = (bf16[128,3584]{1,0:T(8,128)(2,1)S(1)}, bf16[128,3584]{1,0:T(8,128)(2,1)S(1)}, u32[]{:S(2)}, u32[]{:S(2)}) collective-permute-start(bf16[128,3584]{1,0:T(8,128)(2,1)S(1)} %pad_maximum_fusion.2), channel_id=1, source_target_pairs={{0,16},{1,17},{2,18},{3,19},{4,20},{5,21},{6,22},{7,23},{8,24},{9,... | collective-permute-start | bytes 2752520 | tf_op jit(solution)/shard_map/ppermute | solution.py:119
  40.1 5.0 %collective-permute-start.9 = (bf16[512,384]{1,0:T(8,128)(2,1)S(1)}, bf16[512,384]{1,0:T(8,128)(2,1)S(1)}, u32[]{:S(2)}, u32[]{:S(2)}) collective-permute-start(bf16[512,384]{1,0:T(8,128)(2,1)S(1)} %pad_maximum_fusion.5.own_w), channel_id=1, source_target_pairs={{0,1},{1,0},{2,3},{3,2},{4,5},{5,4},{6,7},{7,6},{8,9},{9,8},{10,11... | collective-permute-start | bytes 1179656 | tf_op jit(solution)/shard_map/ppermute | solution.py:117
  45.0 1.8 %collective-permute-done.8 = bf16[256,1024]{1,0:T(8,128)(2,1)S(1)} collective-permute-done((bf16[256,1024]{1,0:T(8,128)(2,1)S(1)}, bf16[256,1024]{1,0:T(8,128)(2,1)S(1)}, u32[]{:S(2)}, u32[]{:S(2)}) %collective-permute-start.8) | collective-permute-done | bytes 524320 | tf_op jit(solution)/shard_map/ppermute | solution.py:117
  46.9 1.6 %collective-permute-start.10 = (bf16[512,1024]{1,0:T(8,128)(2,1)S(1)}, bf16[512,1024]{1,0:T(8,128)(2,1)S(1)}, u32[]{:S(2)}, u32[]{:S(2)}) collective-permute-start(bf16[512,1024]{1,0:T(8,128)(2,1)S(1)} %pad_maximum_fusion.1.xa), channel_id=1, source_target_pairs={{0,2},{1,5},{2,0},{3,7},{4,6},{5,1},{6,4},{7,3},{8,10},{9,13},{10,... | collective-permute-start | bytes 3145736 | tf_op jit(solution)/shard_map/ppermute | solution.py:117
  48.5 8.9 %collective-permute-done.17 = bf16[128,3584]{1,0:T(8,128)(2,1)S(1)} collective-permute-done((bf16[128,3584]{1,0:T(8,128)(2,1)S(1)}, bf16[128,3584]{1,0:T(8,128)(2,1)S(1)}, u32[]{:S(2)}, u32[]{:S(2)}) %collective-permute-start.17) | collective-permute-done | bytes 917536 | tf_op jit(solution)/shard_map/ppermute | solution.py:119
  57.7 5.3 %collective-permute-start.11 = (bf16[512,1024]{1,0:T(8,128)(2,1)S(1)}, bf16[512,1024]{1,0:T(8,128)(2,1)S(1)}, u32[]{:S(2)}, u32[]{:S(2)}) collective-permute-start(bf16[512,1024]{1,0:T(8,128)(2,1)S(1)} %pad_maximum_fusion.1.xa), channel_id=1, source_target_pairs={{0,1},{1,0},{2,3},{3,2},{4,5},{5,4},{6,7},{7,6},{8,9},{9,8},{10,11... | collective-permute-start | bytes 3145736 | tf_op jit(solution)/shard_map/ppermute | solution.py:117
  63.1 2.3 %collective-permute-done.11.xa_other = bf16[512,1024]{1,0:T(8,128)(2,1)S(1)} collective-permute-done((bf16[512,1024]{1,0:T(8,128)(2,1)S(1)}, bf16[512,1024]{1,0:T(8,128)(2,1)S(1)}, u32[]{:S(2)}, u32[]{:S(2)}) %collective-permute-start.11) | collective-permute-done | bytes 1048608 | tf_op jit(solution)/shard_map/ppermute | solution.py:117
  65.3 1.5 %collective-permute-done.12.xb_other = bf16[512,1024]{1,0:T(8,128)(2,1)S(1)} collective-permute-done((bf16[512,1024]{1,0:T(8,128)(2,1)S(1)}, bf16[512,1024]{1,0:T(8,128)(2,1)S(1)}, u32[]{:S(2)}, u32[]{:S(2)}) %collective-permute-start.12) | collective-permute-done | bytes 1048608 | tf_op jit(solution)/shard_map/ppermute | solution.py:117
  66.8 4.8 %attention.1 = (bf16[160,128]{1,0:T(8,128)(2,1)S(1)}, bf16[160,128]{1,0:T(8,128)(2,1)S(1)}, bf16[160,128]{1,0:T(8,128)(2,1)S(1)}, bf16[160,128]{1,0:T(8,128)(2,1)S(1)}) custom-call(s32[1]{0:T(128)S(6)} %copy.12.scalars, bf16[512,1024]{1,0:T(8,128)(2,1)S(1)} %pad_maximum_fusion.1.xa, bf16[512,1024]{1,0:T(8,128)(2,1)S(1)} %collective-permute-done.10.xb, ...), custom_call_target="tpu_custom_call" | custom-call | flops 5000000000 | bytes 8388608 | tf_op jit(solution)/shard_map/attention/pallas_call | solution.py:352
  71.6 2.7 %collective-permute-start.13 = (bf16[160,128]{1,0:T(8,128)(2,1)S(1)}, bf16[160,128]{1,0:T(8,128)(2,1)S(1)}, u32[]{:S(2)}, u32[]{:S(2)}) collective-permute-start(bf16[160,128]{1,0:T(8,128)(2,1)S(1)} %get-tuple-element.34), channel_id=1, source_target_pairs={{0,12},{1,13},{2,14},{3,15},{4,8},{5,9},{6,10},{7,11},{8,4},{9,5},... | collective-permute-start | bytes 122888 | tf_op jit(solution)/shard_map/ppermute | solution.py:117
  74.3 1.8 %collective-permute-start.15 = (bf16[160,128]{1,0:T(8,128)(2,1)S(1)}, bf16[160,128]{1,0:T(8,128)(2,1)S(1)}, u32[]{:S(2)}, u32[]{:S(2)}) collective-permute-start(bf16[160,128]{1,0:T(8,128)(2,1)S(1)} %get-tuple-element.36), channel_id=1, source_target_pairs={{0,8},{1,9},{2,10},{3,11},{4,12},{5,13},{6,14},{7,15},{8,0},{9,1},... | collective-permute-start | bytes 122888 | tf_op jit(solution)/shard_map/ppermute | solution.py:117
  76.1 8.0 %collective-permute-done.13.c1 = bf16[160,128]{1,0:T(8,128)(2,1)S(1)} collective-permute-done((bf16[160,128]{1,0:T(8,128)(2,1)S(1)}, bf16[160,128]{1,0:T(8,128)(2,1)S(1)}, u32[]{:S(2)}, u32[]{:S(2)}) %collective-permute-start.13) | collective-permute-done | bytes 40992 | tf_op jit(solution)/shard_map/ppermute | solution.py:117
  84.1 0.1 collective-permute-start.20
  84.3 3.7 %collective-permute-done.20.pb_other = bf16[256,3584]{1,0:T(8,128)(2,1)S(1)} collective-permute-done((bf16[256,3584]{1,0:T(8,128)(2,1)S(1)}, bf16[256,3584]{1,0:T(8,128)(2,1)S(1)}, u32[]{:S(2)}, u32[]{:S(2)}) %collective-permute-start.20) | collective-permute-done | bytes 1835040 | tf_op jit(solution)/shard_map/ppermute | solution.py:117
  88.0 5.1 %tail.1 = bf16[128,1024]{1,0:T(8,128)(2,1)} custom-call(s32[1]{0:T(128)S(6)} %copy.12.scalars, bf16[160,128]{1,0:T(8,128)(2,1)S(1)} %get-tuple-element.33.c0, bf16[160,128]{1,0:T(8,128)(2,1)S(1)} %collective-permute-done.13.c1, bf16[160,128]{1,0:T(8,128)(2,1)S(1)} %collective-permute-done.14.c2, bf16[160,128]{1,0:T(8,128)(2,1)S(1)} %collective-permute-done.15.c3, ...), custom_call_target="tpu_custom_call" | custom-call | flops 1200000000 | bytes 8388608 | tf_op jit(solution)/shard_map/tail/pallas_call | solution.py:376
  (34 shorter events, 0.5 us)
Async XLA Ops:
  3.5 26.3 %copy-start.5 = (bf16[128,1024]{1,0:T(8,128)(2,1)S(1)}, bf16[128,1024]{1,0:T(8,128)(2,1)}, u32[]{:S(2)}) copy-start(bf16[128,1024]{1,0:T(8,128)(2,1)} %get-tuple-element.28) | copy-start | bytes 786436
  3.6 10.1 %collective-permute-start.1 = (bf16[64,384]{1,0:T(8,128)(2,1)}, bf16[64,384]{1,0:T(8,128)(2,1)S(1)}, u32[]{:S(2)}, u32[]{:S(2)}) collective-permute-start(bf16[64,384]{1,0:T(8,128)(2,1)} %get-tuple-element.25), channel_id=1, source_target_pairs={{0,12},{1,13},{2,14},{3,15},{4,8},{5,9},{6,10},{7,11},{8,4},{9,5},... | collective-permute-start | bytes 147464 | tf_op jit(solution)/shard_map/ppermute | solution.py:117
  8.7 8.0 %collective-permute-start.2 = (bf16[64,384]{1,0:T(8,128)(2,1)}, bf16[64,384]{1,0:T(8,128)(2,1)S(1)}, u32[]{:S(2)}, u32[]{:S(2)}) collective-permute-start(bf16[64,384]{1,0:T(8,128)(2,1)} %get-tuple-element.26), channel_id=1, source_target_pairs={{0,4},{1,5},{2,6},{3,7},{4,0},{5,1},{6,2},{7,3},{8,12},{9,13},{10,... | collective-permute-start | bytes 147464 | tf_op jit(solution)/shard_map/ppermute | solution.py:117
  8.7 11.6 %collective-permute-start.3 = (bf16[64,384]{1,0:T(8,128)(2,1)}, bf16[64,384]{1,0:T(8,128)(2,1)S(1)}, u32[]{:S(2)}, u32[]{:S(2)}) collective-permute-start(bf16[64,384]{1,0:T(8,128)(2,1)} %get-tuple-element.27), channel_id=1, source_target_pairs={{0,8},{1,9},{2,10},{3,11},{4,12},{5,13},{6,14},{7,15},{8,0},{9,1},... | collective-permute-start | bytes 147464 | tf_op jit(solution)/shard_map/ppermute | solution.py:117
  9.3 17.4 %collective-permute-start = (bf16[32,3584]{1,0:T(8,128)(2,1)}, bf16[32,3584]{1,0:T(8,128)(2,1)S(1)}, u32[]{:S(2)}, u32[]{:S(2)}) collective-permute-start(bf16[32,3584]{1,0:T(8,128)(2,1)} %get-tuple-element.23), channel_id=1, source_target_pairs={{0,8},{1,9},{2,10},{3,11},{4,12},{5,13},{6,14},{7,15},{8,0},{9,1},... | collective-permute-start | bytes 688136 | tf_op jit(solution)/shard_map/ppermute | solution.py:119
  12.4 17.5 %collective-permute-start.7 = (bf16[16,1024]{1,0:T(8,128)(2,1)S(1)}, bf16[16,1024]{1,0:T(8,128)(2,1)S(1)}, u32[]{:S(2)}, u32[]{:S(2)}) collective-permute-start(bf16[16,1024]{1,0:T(8,128)(2,1)S(1)} %get-tuple-element.41), channel_id=1, source_target_pairs={{1,0},{2,1},{3,2},{4,3},{5,4},{6,5},{7,6},{8,7},{9,8},{10,9},{11,1... | collective-permute-start | bytes 98312 | tf_op jit(solution)/shard_map/ppermute | solution.py:329
  13.7 16.2 %collective-permute-start.6 = (bf16[16,1024]{1,0:T(8,128)(2,1)S(1)}, bf16[16,1024]{1,0:T(8,128)(2,1)S(1)}, u32[]{:S(2)}, u32[]{:S(2)}) collective-permute-start(bf16[16,1024]{1,0:T(8,128)(2,1)S(1)} %get-tuple-element.42), channel_id=1, source_target_pairs={{0,1},{1,2},{2,3},{3,4},{4,5},{5,6},{6,7},{7,8},{8,9},{9,10},{10,1... | collective-permute-start | bytes 98312 | tf_op jit(solution)/shard_map/ppermute | solution.py:328
  16.7 13.1 %collective-permute-start.5 = (bf16[128,1024]{1,0:T(8,128)(2,1)}, bf16[128,1024]{1,0:T(8,128)(2,1)S(1)}, u32[]{:S(2)}, u32[]{:S(2)}) collective-permute-start(bf16[128,1024]{1,0:T(8,128)(2,1)} %get-tuple-element.28), channel_id=1, source_target_pairs={{0,8},{1,3},{2,10},{3,1},{4,12},{5,7},{6,14},{7,5},{8,0},{9,11},{1... | collective-permute-start | bytes 786440 | tf_op jit(solution)/shard_map/ppermute | solution.py:117
  21.1 6.9 %collective-permute-start.4 = (bf16[256,384]{1,0:T(8,128)(2,1)S(1)}, bf16[256,384]{1,0:T(8,128)(2,1)S(1)}, u32[]{:S(2)}, u32[]{:S(2)}) collective-permute-start(bf16[256,384]{1,0:T(8,128)(2,1)S(1)} %pad_maximum_fusion.7), channel_id=1, source_target_pairs={{0,2},{1,3},{2,0},{3,1},{4,6},{5,7},{6,4},{7,5},{8,10},{9,11},{10,... | collective-permute-start | bytes 589832 | tf_op jit(solution)/shard_map/ppermute | solution.py:117
  29.9 8.5 %collective-permute-start.16 = (bf16[64,3584]{1,0:T(8,128)(2,1)S(1)}, bf16[64,3584]{1,0:T(8,128)(2,1)S(1)}, u32[]{:S(2)}, u32[]{:S(2)}) collective-permute-start(bf16[64,3584]{1,0:T(8,128)(2,1)S(1)} %pad_maximum_fusion.4), channel_id=1, source_target_pairs={{0,2},{1,5},{2,0},{3,7},{4,6},{5,1},{6,4},{7,3},{8,10},{9,13},{10,... | collective-permute-start | bytes 1376264 | tf_op jit(solution)/shard_map/ppermute | solution.py:119
  31.1 15.7 %collective-permute-start.8 = (bf16[256,1024]{1,0:T(8,128)(2,1)S(1)}, bf16[256,1024]{1,0:T(8,128)(2,1)S(1)}, u32[]{:S(2)}, u32[]{:S(2)}) collective-permute-start(bf16[256,1024]{1,0:T(8,128)(2,1)S(1)} %pad_maximum_fusion.3), channel_id=1, source_target_pairs={{0,4},{1,9},{2,6},{3,11},{4,0},{5,13},{6,2},{7,15},{8,12},{9,1},{1... | collective-permute-start | bytes 1572872 | tf_op jit(solution)/shard_map/ppermute | solution.py:117
  38.5 19.0 %collective-permute-start.17 = (bf16[128,3584]{1,0:T(8,128)(2,1)S(1)}, bf16[128,3584]{1,0:T(8,128)(2,1)S(1)}, u32[]{:S(2)}, u32[]{:S(2)}) collective-permute-start(bf16[128,3584]{1,0:T(8,128)(2,1)S(1)} %pad_maximum_fusion.2), channel_id=1, source_target_pairs={{0,16},{1,17},{2,18},{3,19},{4,20},{5,21},{6,22},{7,23},{8,24},{9,... | collective-permute-start | bytes 2752520 | tf_op jit(solution)/shard_map/ppermute | solution.py:119
  40.1 6.8 %collective-permute-start.9 = (bf16[512,384]{1,0:T(8,128)(2,1)S(1)}, bf16[512,384]{1,0:T(8,128)(2,1)S(1)}, u32[]{:S(2)}, u32[]{:S(2)}) collective-permute-start(bf16[512,384]{1,0:T(8,128)(2,1)S(1)} %pad_maximum_fusion.5.own_w), channel_id=1, source_target_pairs={{0,1},{1,0},{2,3},{3,2},{4,5},{5,4},{6,7},{7,6},{8,9},{9,8},{10,11... | collective-permute-start | bytes 1179656 | tf_op jit(solution)/shard_map/ppermute | solution.py:117
  46.9 16.2 %collective-permute-start.10 = (bf16[512,1024]{1,0:T(8,128)(2,1)S(1)}, bf16[512,1024]{1,0:T(8,128)(2,1)S(1)}, u32[]{:S(2)}, u32[]{:S(2)}) collective-permute-start(bf16[512,1024]{1,0:T(8,128)(2,1)S(1)} %pad_maximum_fusion.1.xa), channel_id=1, source_target_pairs={{0,2},{1,5},{2,0},{3,7},{4,6},{5,1},{6,4},{7,3},{8,10},{9,13},{10,... | collective-permute-start | bytes 3145736 | tf_op jit(solution)/shard_map/ppermute | solution.py:117
  57.6 26.7 %copy-start.4 = (bf16[128,1024]{1,0:T(8,128)(2,1)S(1)}, bf16[128,1024]{1,0:T(8,128)(2,1)}, u32[]{:S(2)}) copy-start(bf16[128,1024]{1,0:T(8,128)(2,1)} %feats_in.1) | copy-start | bytes 786436
  57.6 30.4 %copy-start = (f32[9,1024]{1,0:T(8,128)S(1)}, f32[9,1024]{1,0:T(8,128)}, u32[]{:S(2)}) copy-start(f32[9,1024]{1,0:T(8,128)} %taps.1) | copy-start | bytes 110596
  57.6 30.4 %copy-start.1 = (f32[1024]{0:T(1024)S(1)}, f32[1024]{0:T(1024)}, u32[]{:S(2)}) copy-start(f32[1024]{0:T(1024)} %param.16) | copy-start | bytes 12292
  57.6 30.3 %copy-start.2 = (f32[1024]{0:T(1024)S(1)}, f32[1024]{0:T(1024)}, u32[]{:S(2)}) copy-start(f32[1024]{0:T(1024)} %param.19) | copy-start | bytes 12292
  57.6 30.3 %copy-start.3 = (f32[1024]{0:T(1024)S(1)}, f32[1024]{0:T(1024)}, u32[]{:S(2)}) copy-start(f32[1024]{0:T(1024)} %param.20) | copy-start | bytes 12292
  57.7 26.5 %collective-permute-start.18 = (bf16[256,3584]{1,0:T(8,128)(2,1)S(1)}, bf16[256,3584]{1,0:T(8,128)(2,1)S(1)}, u32[]{:S(2)}, u32[]{:S(2)}) collective-permute-start(bf16[256,3584]{1,0:T(8,128)(2,1)S(1)} %pad_maximum_fusion.pa), channel_id=1, source_target_pairs={{0,4},{1,3},{2,6},{3,1},{4,0},{5,7},{6,2},{7,5},{8,12},{9,11},{10,... | collective-permute-start | bytes 5505032 | tf_op jit(solution)/shard_map/ppermute | solution.py:119
  57.7 7.6 %collective-permute-start.11 = (bf16[512,1024]{1,0:T(8,128)(2,1)S(1)}, bf16[512,1024]{1,0:T(8,128)(2,1)S(1)}, u32[]{:S(2)}, u32[]{:S(2)}) collective-permute-start(bf16[512,1024]{1,0:T(8,128)(2,1)S(1)} %pad_maximum_fusion.1.xa), channel_id=1, source_target_pairs={{0,1},{1,0},{2,3},{3,2},{4,5},{5,4},{6,7},{7,6},{8,9},{9,8},{10,11... | collective-permute-start | bytes 3145736 | tf_op jit(solution)/shard_map/ppermute | solution.py:117
  63.1 3.8 %collective-permute-start.12 = (bf16[512,1024]{1,0:T(8,128)(2,1)S(1)}, bf16[512,1024]{1,0:T(8,128)(2,1)S(1)}, u32[]{:S(2)}, u32[]{:S(2)}) collective-permute-start(bf16[512,1024]{1,0:T(8,128)(2,1)S(1)} %collective-permute-done.10.xb), channel_id=1, source_target_pairs={{0,1},{1,0},{2,3},{3,2},{4,5},{5,4},{6,7},{7,6},{8,9},{9,8},{10,11... | collective-permute-start | bytes 3145736 | tf_op jit(solution)/shard_map/ppermute | solution.py:117
  71.6 12.5 %collective-permute-start.13 = (bf16[160,128]{1,0:T(8,128)(2,1)S(1)}, bf16[160,128]{1,0:T(8,128)(2,1)S(1)}, u32[]{:S(2)}, u32[]{:S(2)}) collective-permute-start(bf16[160,128]{1,0:T(8,128)(2,1)S(1)} %get-tuple-element.34), channel_id=1, source_target_pairs={{0,12},{1,13},{2,14},{3,15},{4,8},{5,9},{6,10},{7,11},{8,4},{9,5},... | collective-permute-start | bytes 122888 | tf_op jit(solution)/shard_map/ppermute | solution.py:117
  74.3 9.8 %collective-permute-start.14 = (bf16[160,128]{1,0:T(8,128)(2,1)S(1)}, bf16[160,128]{1,0:T(8,128)(2,1)S(1)}, u32[]{:S(2)}, u32[]{:S(2)}) collective-permute-start(bf16[160,128]{1,0:T(8,128)(2,1)S(1)} %get-tuple-element.35), channel_id=1, source_target_pairs={{0,4},{1,5},{2,6},{3,7},{4,0},{5,1},{6,2},{7,3},{8,12},{9,13},{10,... | collective-permute-start | bytes 122888 | tf_op jit(solution)/shard_map/ppermute | solution.py:117
  74.3 9.8 %collective-permute-start.15 = (bf16[160,128]{1,0:T(8,128)(2,1)S(1)}, bf16[160,128]{1,0:T(8,128)(2,1)S(1)}, u32[]{:S(2)}, u32[]{:S(2)}) collective-permute-start(bf16[160,128]{1,0:T(8,128)(2,1)S(1)} %get-tuple-element.36), channel_id=1, source_target_pairs={{0,8},{1,9},{2,10},{3,11},{4,12},{5,13},{6,14},{7,15},{8,0},{9,1},... | collective-permute-start | bytes 122888 | tf_op jit(solution)/shard_map/ppermute | solution.py:117
  76.1 8.2 %collective-permute-start.19 = (bf16[256,3584]{1,0:T(8,128)(2,1)S(1)}, bf16[256,3584]{1,0:T(8,128)(2,1)S(1)}, u32[]{:S(2)}, u32[]{:S(2)}) collective-permute-start(bf16[256,3584]{1,0:T(8,128)(2,1)S(1)} %pad_maximum_fusion.pa), channel_id=1, source_target_pairs={{0,1},{1,0},{2,3},{3,2},{4,5},{5,4},{6,7},{7,6},{8,9},{9,8},{10,11... | collective-permute-start | bytes 5505032 | tf_op jit(solution)/shard_map/ppermute | solution.py:117
  84.1 3.9 %collective-permute-start.20 = (bf16[256,3584]{1,0:T(8,128)(2,1)S(1)}, bf16[256,3584]{1,0:T(8,128)(2,1)S(1)}, u32[]{:S(2)}, u32[]{:S(2)}) collective-permute-start(bf16[256,3584]{1,0:T(8,128)(2,1)S(1)} %collective-permute-done.18.pb), channel_id=1, source_target_pairs={{0,1},{1,0},{2,3},{3,2},{4,5},{5,4},{6,7},{7,6},{8,9},{9,8},{10,11... | collective-permute-start | bytes 5505032 | tf_op jit(solution)/shard_map/ppermute | solution.py:117

commit v6 on v5

--- a/solution.py
+++ b/solution.py
@@ -259,15 +259,17 @@
     row_out = (source & 15) * step + lanes % step
     side = source // 16
     heads = [((me ^ mask) // 4) for mask in ALONG_Z]
-    halves = []
-    spreads = [0.0, 0.0]
+    spread = 0.0
     small = lax.broadcasted_iota(jnp.int32, (HD, width), 0)
     for head, part in zip(heads, (c0, c1, c2, c3)):
-        for h in range(2):
-            by = jnp.where((small + head * HD == row_out) & (side == h), 1.0, 0.0).astype(jnp.bfloat16)
-            spreads[h] = spreads[h] + jnp.dot(part[...], by, preferred_element_type=jnp.float32)
-    for h in range(2):
-        halves.append(times(spreads[h].astype(jnp.bfloat16), 3 * width, 3 * width + width // 2))
+        by = jnp.where(small + head * HD == row_out, 1.0, 0.0).astype(jnp.bfloat16)
+        spread = spread + jnp.dot(part[...], by, preferred_element_type=jnp.float32)
+    halves = [
+        times(
+            jnp.where(side == h, spread, 0.0).astype(jnp.bfloat16), 3 * width, 3 * width + width // 2
+        )
+        for h in range(2)
+    ]
     attended = feats[...].astype(jnp.float32) + jnp.concatenate(halves, axis=1)
     mean = jnp.mean(attended, axis=-1, keepdims=True)
     centred = attended - mean
@@ -365,7 +367,7 @@
         ],
         compiler_params=pltpu.CompilerParams(vmem_limit_bytes=40 << 20),
         cost_estimate=pl.CostEstimate(
-            flops=5_000_000_000, bytes_accessed=8 << 20, transcendentals=4 * wide * count
+            flops=6_000_000_000, bytes_accessed=8 << 20, transcendentals=4 * wide * count
         ),
     )(scalars, xa, xb, xa_other, xb_other, w8, w_other)
     mine = [contexts[0]] + [swap(part, mask) for part, mask in zip(contexts[1:], ALONG_Z[1:])]

time: 93.5 us -> 93.1 us (level)
  no operation moved by 1% of the time
where the time goes in v6:
time: 93.1 us; the launch traced here: 92.8 us
  waiting for transfers between devices  40.9 us (44%)
  starting transfers between devices  35.7 us (38%)
  Pallas kernels  12.5 us (13%)
  other arithmetic  2.13 us (2%)
    ppermute x15, starting transfers between devices, swap(): return lax.ppermute(array, 'frames', pairs)  26.2 us
    ppermute x15, waiting for transfers between devices, swap(): return lax.ppermute(array, 'frames', pairs)  20.6 us
    ppermute x4, waiting for transfers between devices, swap(): return lax.ppermute(array, ('groups', 'frames'), pairs)  20.2 us
    ppermute x4, starting transfers between devices, swap(): return lax.ppermute(array, ('groups', 'frames'), pairs)  5.15 us
    pallas_call x1, Pallas kernels, per_device(): pl.pallas_call(functools.partial(tail_kernel, rows=rows), name='tail', ou...  4.79 us
    pallas_call x1, Pallas kernels, per_device(): pl.pallas_call(functools.partial(attention_kernel, rows=rows, even=even,...  4.78 us
    ppermute x1, starting transfers between devices, per_device(): lax.ppermute(features[-EDGE:], 'frames', [(i, i + 1) for i in range(15)])  3.03 us
    pallas_call x1, Pallas kernels, per_device(): pl.pallas_call(prepare_kernel, name='prepare', out_shape=[jax.ShapeDtypeS...  2.89 us
  transfers between devices with their start and end apart: 21, of which 11 were waited for; matrix products, arithmetic and copies ran while one was open for 3% of the time, Pallas kernels for 5%

profile of v6, /device:TPU:0, one launch (start us, length us, event | category | flops | bytes accessed | tf_op | source)
XLA Modules:
  0.0 92.8 jit_solution(8020511450625816594)
XLA Ops:
  0.7 2.9 %prepare.1 = (bf16[128,1024]{1,0:T(8,128)(2,1)}, bf16[64,384]{1,0:T(8,128)(2,1)}, bf16[64,384]{1,0:T(8,128)(2,1)}, bf16[64,384]{1,0:T(8,128)(2,1)}, bf16[64,384]{1,0:T(8,128)(2,1)}, /*index=5*/bf16[32,3584]{1,0:T(8,128)(2,1)}) custom-call(s32[1]{0:T(128)S(6)} %copy.12.scalars, bf16[128,1024]{1,0:T(8,128)(2,1)} %feats_in.1, f32[1,1024]{1,0:T(1,128)} %bitcast.7, ...), custom_call_target="tpu_custom_call" | custom-call | tf_op jit(solution)/shard_map/prepare/pallas_call | solution.py:309
  3.6 5.1 %collective-permute-start.1 = (bf16[64,384]{1,0:T(8,128)(2,1)}, bf16[64,384]{1,0:T(8,128)(2,1)S(1)}, u32[]{:S(2)}, u32[]{:S(2)}) collective-permute-start(bf16[64,384]{1,0:T(8,128)(2,1)} %get-tuple-element.25), channel_id=1, source_target_pairs={{0,12},{1,13},{2,14},{3,15},{4,8},{5,9},{6,10},{7,11},{8,4},{9,5},... | collective-permute-start | bytes 147464 | tf_op jit(solution)/shard_map/ppermute | solution.py:117
  8.7 0.6 collective-permute-start.3
  9.3 2.3 %collective-permute-start = (bf16[32,3584]{1,0:T(8,128)(2,1)}, bf16[32,3584]{1,0:T(8,128)(2,1)S(1)}, u32[]{:S(2)}, u32[]{:S(2)}) collective-permute-start(bf16[32,3584]{1,0:T(8,128)(2,1)} %get-tuple-element.23), channel_id=1, source_target_pairs={{0,8},{1,9},{2,10},{3,11},{4,12},{5,13},{6,14},{7,15},{8,0},{9,1},... | collective-permute-start | bytes 688136 | tf_op jit(solution)/shard_map/ppermute | solution.py:119
  11.6 0.8 fusion
  12.4 1.3 %collective-permute-start.7 = (bf16[16,1024]{1,0:T(8,128)(2,1)S(1)}, bf16[16,1024]{1,0:T(8,128)(2,1)S(1)}, u32[]{:S(2)}, u32[]{:S(2)}) collective-permute-start(bf16[16,1024]{1,0:T(8,128)(2,1)S(1)} %get-tuple-element.41), channel_id=1, source_target_pairs={{1,0},{2,1},{3,2},{4,3},{5,4},{6,5},{7,6},{8,7},{9,8},{10,9},{11,1... | collective-permute-start | bytes 98312 | tf_op jit(solution)/shard_map/ppermute | solution.py:331
  13.7 3.0 %collective-permute-start.6 = (bf16[16,1024]{1,0:T(8,128)(2,1)S(1)}, bf16[16,1024]{1,0:T(8,128)(2,1)S(1)}, u32[]{:S(2)}, u32[]{:S(2)}) collective-permute-start(bf16[16,1024]{1,0:T(8,128)(2,1)S(1)} %get-tuple-element.42), channel_id=1, source_target_pairs={{0,1},{1,2},{2,3},{3,4},{4,5},{5,6},{6,7},{7,8},{8,9},{9,10},{10,1... | collective-permute-start | bytes 98312 | tf_op jit(solution)/shard_map/ppermute | solution.py:330
  16.7 2.3 %collective-permute-start.5 = (bf16[128,1024]{1,0:T(8,128)(2,1)}, bf16[128,1024]{1,0:T(8,128)(2,1)S(1)}, u32[]{:S(2)}, u32[]{:S(2)}) collective-permute-start(bf16[128,1024]{1,0:T(8,128)(2,1)} %get-tuple-element.28), channel_id=1, source_target_pairs={{0,8},{1,3},{2,10},{3,1},{4,12},{5,7},{6,14},{7,5},{8,0},{9,11},{1... | collective-permute-start | bytes 786440 | tf_op jit(solution)/shard_map/ppermute | solution.py:117
  19.1 1.2 %collective-permute-done.3 = bf16[64,384]{1,0:T(8,128)(2,1)S(1)} collective-permute-done((bf16[64,384]{1,0:T(8,128)(2,1)}, bf16[64,384]{1,0:T(8,128)(2,1)S(1)}, u32[]{:S(2)}, u32[]{:S(2)}) %collective-permute-start.3) | collective-permute-done | bytes 49184 | tf_op jit(solution)/shard_map/ppermute | solution.py:117
  20.3 0.8 pad_maximum_fusion.7
  21.1 1.6 %collective-permute-start.4 = (bf16[256,384]{1,0:T(8,128)(2,1)S(1)}, bf16[256,384]{1,0:T(8,128)(2,1)S(1)}, u32[]{:S(2)}, u32[]{:S(2)}) collective-permute-start(bf16[256,384]{1,0:T(8,128)(2,1)S(1)} %pad_maximum_fusion.7), channel_id=1, source_target_pairs={{0,2},{1,3},{2,0},{3,1},{4,6},{5,7},{6,4},{7,5},{8,10},{9,11},{10,... | collective-permute-start | bytes 589832 | tf_op jit(solution)/shard_map/ppermute | solution.py:117
  22.7 4.0 %collective-permute-done = bf16[32,3584]{1,0:T(8,128)(2,1)S(1)} collective-permute-done((bf16[32,3584]{1,0:T(8,128)(2,1)}, bf16[32,3584]{1,0:T(8,128)(2,1)S(1)}, u32[]{:S(2)}, u32[]{:S(2)}) %collective-permute-start) | collective-permute-done | bytes 229408 | tf_op jit(solution)/shard_map/ppermute | solution.py:119
  26.7 1.0 %pad_maximum_fusion.4 = bf16[64,3584]{1,0:T(8,128)(2,1)S(1)} fusion(bf16[32,3584]{1,0:T(8,128)(2,1)S(1)} %collective-permute-done, bf16[32,3584]{1,0:T(8,128)(2,1)} %get-tuple-element.23), kind=kLoop, calls=%fused_computation.4 | loop fusion | flops 917504 | bytes 917504 | tf_op jit(solution)/shard_map/concatenate | solution.py:325
  27.7 0.3 collective-permute-done.4
  28.0 1.8 %collective-permute-done.5 = bf16[128,1024]{1,0:T(8,128)(2,1)S(1)} collective-permute-done((bf16[128,1024]{1,0:T(8,128)(2,1)}, bf16[128,1024]{1,0:T(8,128)(2,1)S(1)}, u32[]{:S(2)}, u32[]{:S(2)}) %collective-permute-start.5) | collective-permute-done | bytes 262176 | tf_op jit(solution)/shard_map/ppermute | solution.py:117
  29.9 1.2 %collective-permute-start.16 = (bf16[64,3584]{1,0:T(8,128)(2,1)S(1)}, bf16[64,3584]{1,0:T(8,128)(2,1)S(1)}, u32[]{:S(2)}, u32[]{:S(2)}) collective-permute-start(bf16[64,3584]{1,0:T(8,128)(2,1)S(1)} %pad_maximum_fusion.4), channel_id=1, source_target_pairs={{0,2},{1,5},{2,0},{3,7},{4,6},{5,1},{6,4},{7,3},{8,10},{9,13},{10,... | collective-permute-start | bytes 1376264 | tf_op jit(solution)/shard_map/ppermute | solution.py:119
  31.1 7.3 %collective-permute-done.16 = bf16[64,3584]{1,0:T(8,128)(2,1)S(1)} collective-permute-done((bf16[64,3584]{1,0:T(8,128)(2,1)S(1)}, bf16[64,3584]{1,0:T(8,128)(2,1)S(1)}, u32[]{:S(2)}, u32[]{:S(2)}) %collective-permute-start.16) | collective-permute-done | bytes 458784 | tf_op jit(solution)/shard_map/ppermute | solution.py:119
  38.5 1.6 %collective-permute-start.17 = (bf16[128,3584]{1,0:T(8,128)(2,1)S(1)}, bf16[128,3584]{1,0:T(8,128)(2,1)S(1)}, u32[]{:S(2)}, u32[]{:S(2)}) collective-permute-start(bf16[128,3584]{1,0:T(8,128)(2,1)S(1)} %pad_maximum_fusion.2), channel_id=1, source_target_pairs={{0,16},{1,17},{2,18},{3,19},{4,20},{5,21},{6,22},{7,23},{8,24},{9,... | collective-permute-start | bytes 2752520 | tf_op jit(solution)/shard_map/ppermute | solution.py:119
  40.1 5.0 %collective-permute-start.9 = (bf16[512,384]{1,0:T(8,128)(2,1)S(1)}, bf16[512,384]{1,0:T(8,128)(2,1)S(1)}, u32[]{:S(2)}, u32[]{:S(2)}) collective-permute-start(bf16[512,384]{1,0:T(8,128)(2,1)S(1)} %pad_maximum_fusion.5.own_w), channel_id=1, source_target_pairs={{0,1},{1,0},{2,3},{3,2},{4,5},{5,4},{6,7},{7,6},{8,9},{9,8},{10,11... | collective-permute-start | bytes 1179656 | tf_op jit(solution)/shard_map/ppermute | solution.py:117
  45.0 1.8 %collective-permute-done.8 = bf16[256,1024]{1,0:T(8,128)(2,1)S(1)} collective-permute-done((bf16[256,1024]{1,0:T(8,128)(2,1)S(1)}, bf16[256,1024]{1,0:T(8,128)(2,1)S(1)}, u32[]{:S(2)}, u32[]{:S(2)}) %collective-permute-start.8) | collective-permute-done | bytes 524320 | tf_op jit(solution)/shard_map/ppermute | solution.py:117
  46.9 1.6 %collective-permute-start.10 = (bf16[512,1024]{1,0:T(8,128)(2,1)S(1)}, bf16[512,1024]{1,0:T(8,128)(2,1)S(1)}, u32[]{:S(2)}, u32[]{:S(2)}) collective-permute-start(bf16[512,1024]{1,0:T(8,128)(2,1)S(1)} %pad_maximum_fusion.1.xa), channel_id=1, source_target_pairs={{0,2},{1,5},{2,0},{3,7},{4,6},{5,1},{6,4},{7,3},{8,10},{9,13},{10,... | collective-permute-start | bytes 3145736 | tf_op jit(solution)/shard_map/ppermute | solution.py:117
  48.5 8.9 %collective-permute-done.17 = bf16[128,3584]{1,0:T(8,128)(2,1)S(1)} collective-permute-done((bf16[128,3584]{1,0:T(8,128)(2,1)S(1)}, bf16[128,3584]{1,0:T(8,128)(2,1)S(1)}, u32[]{:S(2)}, u32[]{:S(2)}) %collective-permute-start.17) | collective-permute-done | bytes 917536 | tf_op jit(solution)/shard_map/ppermute | solution.py:119
  57.7 5.3 %collective-permute-start.11 = (bf16[512,1024]{1,0:T(8,128)(2,1)S(1)}, bf16[512,1024]{1,0:T(8,128)(2,1)S(1)}, u32[]{:S(2)}, u32[]{:S(2)}) collective-permute-start(bf16[512,1024]{1,0:T(8,128)(2,1)S(1)} %pad_maximum_fusion.1.xa), channel_id=1, source_target_pairs={{0,1},{1,0},{2,3},{3,2},{4,5},{5,4},{6,7},{7,6},{8,9},{9,8},{10,11... | collective-permute-start | bytes 3145736 | tf_op jit(solution)/shard_map/ppermute | solution.py:117
  63.1 2.3 %collective-permute-done.11.xa_other = bf16[512,1024]{1,0:T(8,128)(2,1)S(1)} collective-permute-done((bf16[512,1024]{1,0:T(8,128)(2,1)S(1)}, bf16[512,1024]{1,0:T(8,128)(2,1)S(1)}, u32[]{:S(2)}, u32[]{:S(2)}) %collective-permute-start.11) | collective-permute-done | bytes 1048608 | tf_op jit(solution)/shard_map/ppermute | solution.py:117
  65.3 1.5 %collective-permute-done.12.xb_other = bf16[512,1024]{1,0:T(8,128)(2,1)S(1)} collective-permute-done((bf16[512,1024]{1,0:T(8,128)(2,1)S(1)}, bf16[512,1024]{1,0:T(8,128)(2,1)S(1)}, u32[]{:S(2)}, u32[]{:S(2)}) %collective-permute-start.12) | collective-permute-done | bytes 1048608 | tf_op jit(solution)/shard_map/ppermute | solution.py:117
  66.8 4.8 %attention.1 = (bf16[160,128]{1,0:T(8,128)(2,1)S(1)}, bf16[160,128]{1,0:T(8,128)(2,1)S(1)}, bf16[160,128]{1,0:T(8,128)(2,1)S(1)}, bf16[160,128]{1,0:T(8,128)(2,1)S(1)}) custom-call(s32[1]{0:T(128)S(6)} %copy.12.scalars, bf16[512,1024]{1,0:T(8,128)(2,1)S(1)} %pad_maximum_fusion.1.xa, bf16[512,1024]{1,0:T(8,128)(2,1)S(1)} %collective-permute-done.10.xb, ...), custom_call_target="tpu_custom_call" | custom-call | flops 6000000000 | bytes 8388608 | tf_op jit(solution)/shard_map/attention/pallas_call | solution.py:354
  71.6 2.7 %collective-permute-start.13 = (bf16[160,128]{1,0:T(8,128)(2,1)S(1)}, bf16[160,128]{1,0:T(8,128)(2,1)S(1)}, u32[]{:S(2)}, u32[]{:S(2)}) collective-permute-start(bf16[160,128]{1,0:T(8,128)(2,1)S(1)} %get-tuple-element.34), channel_id=1, source_target_pairs={{0,12},{1,13},{2,14},{3,15},{4,8},{5,9},{6,10},{7,11},{8,4},{9,5},... | collective-permute-start | bytes 122888 | tf_op jit(solution)/shard_map/ppermute | solution.py:117
  74.3 1.8 %collective-permute-start.15 = (bf16[160,128]{1,0:T(8,128)(2,1)S(1)}, bf16[160,128]{1,0:T(8,128)(2,1)S(1)}, u32[]{:S(2)}, u32[]{:S(2)}) collective-permute-start(bf16[160,128]{1,0:T(8,128)(2,1)S(1)} %get-tuple-element.36), channel_id=1, source_target_pairs={{0,8},{1,9},{2,10},{3,11},{4,12},{5,13},{6,14},{7,15},{8,0},{9,1},... | collective-permute-start | bytes 122888 | tf_op jit(solution)/shard_map/ppermute | solution.py:117
  76.1 8.0 %collective-permute-done.13.c1 = bf16[160,128]{1,0:T(8,128)(2,1)S(1)} collective-permute-done((bf16[160,128]{1,0:T(8,128)(2,1)S(1)}, bf16[160,128]{1,0:T(8,128)(2,1)S(1)}, u32[]{:S(2)}, u32[]{:S(2)}) %collective-permute-start.13) | collective-permute-done | bytes 40992 | tf_op jit(solution)/shard_map/ppermute | solution.py:117
  84.1 0.1 collective-permute-start.20
  84.3 3.7 %collective-permute-done.20.pb_other = bf16[256,3584]{1,0:T(8,128)(2,1)S(1)} collective-permute-done((bf16[256,3584]{1,0:T(8,128)(2,1)S(1)}, bf16[256,3584]{1,0:T(8,128)(2,1)S(1)}, u32[]{:S(2)}, u32[]{:S(2)}) %collective-permute-start.20) | collective-permute-done | bytes 1835040 | tf_op jit(solution)/shard_map/ppermute | solution.py:117
  88.0 4.8 %tail.1 = bf16[128,1024]{1,0:T(8,128)(2,1)} custom-call(s32[1]{0:T(128)S(6)} %copy.12.scalars, bf16[160,128]{1,0:T(8,128)(2,1)S(1)} %get-tuple-element.33.c0, bf16[160,128]{1,0:T(8,128)(2,1)S(1)} %collective-permute-done.13.c1, bf16[160,128]{1,0:T(8,128)(2,1)S(1)} %collective-permute-done.14.c2, bf16[160,128]{1,0:T(8,128)(2,1)S(1)} %collective-permute-done.15.c3, ...), custom_call_target="tpu_custom_call" | custom-call | flops 1200000000 | bytes 8388608 | tf_op jit(solution)/shard_map/tail/pallas_call | solution.py:378
  (34 shorter events, 0.5 us)
Async XLA Ops:
  3.5 26.3 %copy-start.5 = (bf16[128,1024]{1,0:T(8,128)(2,1)S(1)}, bf16[128,1024]{1,0:T(8,128)(2,1)}, u32[]{:S(2)}) copy-start(bf16[128,1024]{1,0:T(8,128)(2,1)} %get-tuple-element.28) | copy-start | bytes 786436
  3.6 10.1 %collective-permute-start.1 = (bf16[64,384]{1,0:T(8,128)(2,1)}, bf16[64,384]{1,0:T(8,128)(2,1)S(1)}, u32[]{:S(2)}, u32[]{:S(2)}) collective-permute-start(bf16[64,384]{1,0:T(8,128)(2,1)} %get-tuple-element.25), channel_id=1, source_target_pairs={{0,12},{1,13},{2,14},{3,15},{4,8},{5,9},{6,10},{7,11},{8,4},{9,5},... | collective-permute-start | bytes 147464 | tf_op jit(solution)/shard_map/ppermute | solution.py:117
  8.7 8.0 %collective-permute-start.2 = (bf16[64,384]{1,0:T(8,128)(2,1)}, bf16[64,384]{1,0:T(8,128)(2,1)S(1)}, u32[]{:S(2)}, u32[]{:S(2)}) collective-permute-start(bf16[64,384]{1,0:T(8,128)(2,1)} %get-tuple-element.26), channel_id=1, source_target_pairs={{0,4},{1,5},{2,6},{3,7},{4,0},{5,1},{6,2},{7,3},{8,12},{9,13},{10,... | collective-permute-start | bytes 147464 | tf_op jit(solution)/shard_map/ppermute | solution.py:117
  8.7 11.6 %collective-permute-start.3 = (bf16[64,384]{1,0:T(8,128)(2,1)}, bf16[64,384]{1,0:T(8,128)(2,1)S(1)}, u32[]{:S(2)}, u32[]{:S(2)}) collective-permute-start(bf16[64,384]{1,0:T(8,128)(2,1)} %get-tuple-element.27), channel_id=1, source_target_pairs={{0,8},{1,9},{2,10},{3,11},{4,12},{5,13},{6,14},{7,15},{8,0},{9,1},... | collective-permute-start | bytes 147464 | tf_op jit(solution)/shard_map/ppermute | solution.py:117
  9.3 17.4 %collective-permute-start = (bf16[32,3584]{1,0:T(8,128)(2,1)}, bf16[32,3584]{1,0:T(8,128)(2,1)S(1)}, u32[]{:S(2)}, u32[]{:S(2)}) collective-permute-start(bf16[32,3584]{1,0:T(8,128)(2,1)} %get-tuple-element.23), channel_id=1, source_target_pairs={{0,8},{1,9},{2,10},{3,11},{4,12},{5,13},{6,14},{7,15},{8,0},{9,1},... | collective-permute-start | bytes 688136 | tf_op jit(solution)/shard_map/ppermute | solution.py:119
  12.4 17.5 %collective-permute-start.7 = (bf16[16,1024]{1,0:T(8,128)(2,1)S(1)}, bf16[16,1024]{1,0:T(8,128)(2,1)S(1)}, u32[]{:S(2)}, u32[]{:S(2)}) collective-permute-start(bf16[16,1024]{1,0:T(8,128)(2,1)S(1)} %get-tuple-element.41), channel_id=1, source_target_pairs={{1,0},{2,1},{3,2},{4,3},{5,4},{6,5},{7,6},{8,7},{9,8},{10,9},{11,1... | collective-permute-start | bytes 98312 | tf_op jit(solution)/shard_map/ppermute | solution.py:331
  13.7 16.2 %collective-permute-start.6 = (bf16[16,1024]{1,0:T(8,128)(2,1)S(1)}, bf16[16,1024]{1,0:T(8,128)(2,1)S(1)}, u32[]{:S(2)}, u32[]{:S(2)}) collective-permute-start(bf16[16,1024]{1,0:T(8,128)(2,1)S(1)} %get-tuple-element.42), channel_id=1, source_target_pairs={{0,1},{1,2},{2,3},{3,4},{4,5},{5,6},{6,7},{7,8},{8,9},{9,10},{10,1... | collective-permute-start | bytes 98312 | tf_op jit(solution)/shard_map/ppermute | solution.py:330
  16.7 13.1 %collective-permute-start.5 = (bf16[128,1024]{1,0:T(8,128)(2,1)}, bf16[128,1024]{1,0:T(8,128)(2,1)S(1)}, u32[]{:S(2)}, u32[]{:S(2)}) collective-permute-start(bf16[128,1024]{1,0:T(8,128)(2,1)} %get-tuple-element.28), channel_id=1, source_target_pairs={{0,8},{1,3},{2,10},{3,1},{4,12},{5,7},{6,14},{7,5},{8,0},{9,11},{1... | collective-permute-start | bytes 786440 | tf_op jit(solution)/shard_map/ppermute | solution.py:117
  21.1 6.9 %collective-permute-start.4 = (bf16[256,384]{1,0:T(8,128)(2,1)S(1)}, bf16[256,384]{1,0:T(8,128)(2,1)S(1)}, u32[]{:S(2)}, u32[]{:S(2)}) collective-permute-start(bf16[256,384]{1,0:T(8,128)(2,1)S(1)} %pad_maximum_fusion.7), channel_id=1, source_target_pairs={{0,2},{1,3},{2,0},{3,1},{4,6},{5,7},{6,4},{7,5},{8,10},{9,11},{10,... | collective-permute-start | bytes 589832 | tf_op jit(solution)/shard_map/ppermute | solution.py:117
  29.9 8.5 %collective-permute-start.16 = (bf16[64,3584]{1,0:T(8,128)(2,1)S(1)}, bf16[64,3584]{1,0:T(8,128)(2,1)S(1)}, u32[]{:S(2)}, u32[]{:S(2)}) collective-permute-start(bf16[64,3584]{1,0:T(8,128)(2,1)S(1)} %pad_maximum_fusion.4), channel_id=1, source_target_pairs={{0,2},{1,5},{2,0},{3,7},{4,6},{5,1},{6,4},{7,3},{8,10},{9,13},{10,... | collective-permute-start | bytes 1376264 | tf_op jit(solution)/shard_map/ppermute | solution.py:119
  31.1 15.7 %collective-permute-start.8 = (bf16[256,1024]{1,0:T(8,128)(2,1)S(1)}, bf16[256,1024]{1,0:T(8,128)(2,1)S(1)}, u32[]{:S(2)}, u32[]{:S(2)}) collective-permute-start(bf16[256,1024]{1,0:T(8,128)(2,1)S(1)} %pad_maximum_fusion.3), channel_id=1, source_target_pairs={{0,4},{1,9},{2,6},{3,11},{4,0},{5,13},{6,2},{7,15},{8,12},{9,1},{1... | collective-permute-start | bytes 1572872 | tf_op jit(solution)/shard_map/ppermute | solution.py:117
  38.5 19.0 %collective-permute-start.17 = (bf16[128,3584]{1,0:T(8,128)(2,1)S(1)}, bf16[128,3584]{1,0:T(8,128)(2,1)S(1)}, u32[]{:S(2)}, u32[]{:S(2)}) collective-permute-start(bf16[128,3584]{1,0:T(8,128)(2,1)S(1)} %pad_maximum_fusion.2), channel_id=1, source_target_pairs={{0,16},{1,17},{2,18},{3,19},{4,20},{5,21},{6,22},{7,23},{8,24},{9,... | collective-permute-start | bytes 2752520 | tf_op jit(solution)/shard_map/ppermute | solution.py:119
  40.1 6.8 %collective-permute-start.9 = (bf16[512,384]{1,0:T(8,128)(2,1)S(1)}, bf16[512,384]{1,0:T(8,128)(2,1)S(1)}, u32[]{:S(2)}, u32[]{:S(2)}) collective-permute-start(bf16[512,384]{1,0:T(8,128)(2,1)S(1)} %pad_maximum_fusion.5.own_w), channel_id=1, source_target_pairs={{0,1},{1,0},{2,3},{3,2},{4,5},{5,4},{6,7},{7,6},{8,9},{9,8},{10,11... | collective-permute-start | bytes 1179656 | tf_op jit(solution)/shard_map/ppermute | solution.py:117
  46.9 16.2 %collective-permute-start.10 = (bf16[512,1024]{1,0:T(8,128)(2,1)S(1)}, bf16[512,1024]{1,0:T(8,128)(2,1)S(1)}, u32[]{:S(2)}, u32[]{:S(2)}) collective-permute-start(bf16[512,1024]{1,0:T(8,128)(2,1)S(1)} %pad_maximum_fusion.1.xa), channel_id=1, source_target_pairs={{0,2},{1,5},{2,0},{3,7},{4,6},{5,1},{6,4},{7,3},{8,10},{9,13},{10,... | collective-permute-start | bytes 3145736 | tf_op jit(solution)/shard_map/ppermute | solution.py:117
  57.6 26.7 %copy-start.4 = (bf16[128,1024]{1,0:T(8,128)(2,1)S(1)}, bf16[128,1024]{1,0:T(8,128)(2,1)}, u32[]{:S(2)}) copy-start(bf16[128,1024]{1,0:T(8,128)(2,1)} %feats_in.1) | copy-start | bytes 786436
  57.6 30.4 %copy-start = (f32[9,1024]{1,0:T(8,128)S(1)}, f32[9,1024]{1,0:T(8,128)}, u32[]{:S(2)}) copy-start(f32[9,1024]{1,0:T(8,128)} %taps.1) | copy-start | bytes 110596
  57.6 30.4 %copy-start.1 = (f32[1024]{0:T(1024)S(1)}, f32[1024]{0:T(1024)}, u32[]{:S(2)}) copy-start(f32[1024]{0:T(1024)} %param.16) | copy-start | bytes 12292
  57.6 30.3 %copy-start.2 = (f32[1024]{0:T(1024)S(1)}, f32[1024]{0:T(1024)}, u32[]{:S(2)}) copy-start(f32[1024]{0:T(1024)} %param.19) | copy-start | bytes 12292
  57.6 30.3 %copy-start.3 = (f32[1024]{0:T(1024)S(1)}, f32[1024]{0:T(1024)}, u32[]{:S(2)}) copy-start(f32[1024]{0:T(1024)} %param.20) | copy-start | bytes 12292
  57.7 26.5 %collective-permute-start.18 = (bf16[256,3584]{1,0:T(8,128)(2,1)S(1)}, bf16[256,3584]{1,0:T(8,128)(2,1)S(1)}, u32[]{:S(2)}, u32[]{:S(2)}) collective-permute-start(bf16[256,3584]{1,0:T(8,128)(2,1)S(1)} %pad_maximum_fusion.pa), channel_id=1, source_target_pairs={{0,4},{1,3},{2,6},{3,1},{4,0},{5,7},{6,2},{7,5},{8,12},{9,11},{10,... | collective-permute-start | bytes 5505032 | tf_op jit(solution)/shard_map/ppermute | solution.py:119
  57.7 7.6 %collective-permute-start.11 = (bf16[512,1024]{1,0:T(8,128)(2,1)S(1)}, bf16[512,1024]{1,0:T(8,128)(2,1)S(1)}, u32[]{:S(2)}, u32[]{:S(2)}) collective-permute-start(bf16[512,1024]{1,0:T(8,128)(2,1)S(1)} %pad_maximum_fusion.1.xa), channel_id=1, source_target_pairs={{0,1},{1,0},{2,3},{3,2},{4,5},{5,4},{6,7},{7,6},{8,9},{9,8},{10,11... | collective-permute-start | bytes 3145736 | tf_op jit(solution)/shard_map/ppermute | solution.py:117
  63.1 3.8 %collective-permute-start.12 = (bf16[512,1024]{1,0:T(8,128)(2,1)S(1)}, bf16[512,1024]{1,0:T(8,128)(2,1)S(1)}, u32[]{:S(2)}, u32[]{:S(2)}) collective-permute-start(bf16[512,1024]{1,0:T(8,128)(2,1)S(1)} %collective-permute-done.10.xb), channel_id=1, source_target_pairs={{0,1},{1,0},{2,3},{3,2},{4,5},{5,4},{6,7},{7,6},{8,9},{9,8},{10,11... | collective-permute-start | bytes 3145736 | tf_op jit(solution)/shard_map/ppermute | solution.py:117
  71.6 12.5 %collective-permute-start.13 = (bf16[160,128]{1,0:T(8,128)(2,1)S(1)}, bf16[160,128]{1,0:T(8,128)(2,1)S(1)}, u32[]{:S(2)}, u32[]{:S(2)}) collective-permute-start(bf16[160,128]{1,0:T(8,128)(2,1)S(1)} %get-tuple-element.34), channel_id=1, source_target_pairs={{0,12},{1,13},{2,14},{3,15},{4,8},{5,9},{6,10},{7,11},{8,4},{9,5},... | collective-permute-start | bytes 122888 | tf_op jit(solution)/shard_map/ppermute | solution.py:117
  74.3 9.8 %collective-permute-start.14 = (bf16[160,128]{1,0:T(8,128)(2,1)S(1)}, bf16[160,128]{1,0:T(8,128)(2,1)S(1)}, u32[]{:S(2)}, u32[]{:S(2)}) collective-permute-start(bf16[160,128]{1,0:T(8,128)(2,1)S(1)} %get-tuple-element.35), channel_id=1, source_target_pairs={{0,4},{1,5},{2,6},{3,7},{4,0},{5,1},{6,2},{7,3},{8,12},{9,13},{10,... | collective-permute-start | bytes 122888 | tf_op jit(solution)/shard_map/ppermute | solution.py:117
  74.3 9.8 %collective-permute-start.15 = (bf16[160,128]{1,0:T(8,128)(2,1)S(1)}, bf16[160,128]{1,0:T(8,128)(2,1)S(1)}, u32[]{:S(2)}, u32[]{:S(2)}) collective-permute-start(bf16[160,128]{1,0:T(8,128)(2,1)S(1)} %get-tuple-element.36), channel_id=1, source_target_pairs={{0,8},{1,9},{2,10},{3,11},{4,12},{5,13},{6,14},{7,15},{8,0},{9,1},... | collective-permute-start | bytes 122888 | tf_op jit(solution)/shard_map/ppermute | solution.py:117
  76.1 8.2 %collective-permute-start.19 = (bf16[256,3584]{1,0:T(8,128)(2,1)S(1)}, bf16[256,3584]{1,0:T(8,128)(2,1)S(1)}, u32[]{:S(2)}, u32[]{:S(2)}) collective-permute-start(bf16[256,3584]{1,0:T(8,128)(2,1)S(1)} %pad_maximum_fusion.pa), channel_id=1, source_target_pairs={{0,1},{1,0},{2,3},{3,2},{4,5},{5,4},{6,7},{7,6},{8,9},{9,8},{10,11... | collective-permute-start | bytes 5505032 | tf_op jit(solution)/shard_map/ppermute | solution.py:117
  84.1 3.9 %collective-permute-start.20 = (bf16[256,3584]{1,0:T(8,128)(2,1)S(1)}, bf16[256,3584]{1,0:T(8,128)(2,1)S(1)}, u32[]{:S(2)}, u32[]{:S(2)}) collective-permute-start(bf16[256,3584]{1,0:T(8,128)(2,1)S(1)} %collective-permute-done.18.pb), channel_id=1, source_target_pairs={{0,1},{1,0},{2,3},{3,2},{4,5},{5,4},{6,7},{7,6},{8,9},{9,8},{10,11... | collective-permute-start | bytes 5505032 | tf_op jit(solution)/shard_map/ppermute | solution.py:117

commit v7 on v6

--- a/solution.py
+++ b/solution.py
@@ -367,7 +367,7 @@
         ],
         compiler_params=pltpu.CompilerParams(vmem_limit_bytes=40 << 20),
         cost_estimate=pl.CostEstimate(
-            flops=6_000_000_000, bytes_accessed=8 << 20, transcendentals=4 * wide * count
+            flops=5_000_000_000, bytes_accessed=8 << 20, transcendentals=4 * wide * count
         ),
     )(scalars, xa, xb, xa_other, xb_other, w8, w_other)
     mine = [contexts[0]] + [swap(part, mask) for part, mask in zip(contexts[1:], ALONG_Z[1:])]

time: 93.1 us -> 93.1 us (level)
  no operation moved by 1% of the time
where the time goes in v7:
time: 93.1 us; the launch traced here: 92.8 us
  waiting for transfers between devices  40.9 us (44%)
  starting transfers between devices  35.7 us (38%)
  Pallas kernels  12.5 us (13%)
  other arithmetic  2.13 us (2%)
    ppermute x15, starting transfers between devices, swap(): return lax.ppermute(array, 'frames', pairs)  26.2 us
    ppermute x15, waiting for transfers between devices, swap(): return lax.ppermute(array, 'frames', pairs)  20.6 us
    ppermute x4, waiting for transfers between devices, swap(): return lax.ppermute(array, ('groups', 'frames'), pairs)  20.2 us
    ppermute x4, starting transfers between devices, swap(): return lax.ppermute(array, ('groups', 'frames'), pairs)  5.15 us
    pallas_call x1, Pallas kernels, per_device(): pl.pallas_call(functools.partial(tail_kernel, rows=rows), name='tail', ou...  4.79 us
    pallas_call x1, Pallas kernels, per_device(): pl.pallas_call(functools.partial(attention_kernel, rows=rows, even=even,...  4.78 us
    ppermute x1, starting transfers between devices, per_device(): lax.ppermute(features[-EDGE:], 'frames', [(i, i + 1) for i in range(15)])  3.03 us
    pallas_call x1, Pallas kernels, per_device(): pl.pallas_call(prepare_kernel, name='prepare', out_shape=[jax.ShapeDtypeS...  2.89 us
  transfers between devices with their start and end apart: 21, of which 11 were waited for; matrix products, arithmetic and copies ran while one was open for 3% of the time, Pallas kernels for 5%

profile of v7, /device:TPU:0, one launch (start us, length us, event | category | flops | bytes accessed | tf_op | source)
XLA Modules:
  0.0 92.8 jit_solution(8020511450625816594)
XLA Ops:
  0.7 2.9 %prepare.1 = (bf16[128,1024]{1,0:T(8,128)(2,1)}, bf16[64,384]{1,0:T(8,128)(2,1)}, bf16[64,384]{1,0:T(8,128)(2,1)}, bf16[64,384]{1,0:T(8,128)(2,1)}, bf16[64,384]{1,0:T(8,128)(2,1)}, /*index=5*/bf16[32,3584]{1,0:T(8,128)(2,1)}) custom-call(s32[1]{0:T(128)S(6)} %copy.12.scalars, bf16[128,1024]{1,0:T(8,128)(2,1)} %feats_in.1, f32[1,1024]{1,0:T(1,128)} %bitcast.7, ...), custom_call_target="tpu_custom_call" | custom-call | tf_op jit(solution)/shard_map/prepare/pallas_call | solution.py:309
  3.6 5.1 %collective-permute-start.1 = (bf16[64,384]{1,0:T(8,128)(2,1)}, bf16[64,384]{1,0:T(8,128)(2,1)S(1)}, u32[]{:S(2)}, u32[]{:S(2)}) collective-permute-start(bf16[64,384]{1,0:T(8,128)(2,1)} %get-tuple-element.25), channel_id=1, source_target_pairs={{0,12},{1,13},{2,14},{3,15},{4,8},{5,9},{6,10},{7,11},{8,4},{9,5},... | collective-permute-start | bytes 147464 | tf_op jit(solution)/shard_map/ppermute | solution.py:117
  8.7 0.6 collective-permute-start.3
  9.3 2.3 %collective-permute-start = (bf16[32,3584]{1,0:T(8,128)(2,1)}, bf16[32,3584]{1,0:T(8,128)(2,1)S(1)}, u32[]{:S(2)}, u32[]{:S(2)}) collective-permute-start(bf16[32,3584]{1,0:T(8,128)(2,1)} %get-tuple-element.23), channel_id=1, source_target_pairs={{0,8},{1,9},{2,10},{3,11},{4,12},{5,13},{6,14},{7,15},{8,0},{9,1},... | collective-permute-start | bytes 688136 | tf_op jit(solution)/shard_map/ppermute | solution.py:119
  11.6 0.8 fusion
  12.4 1.3 %collective-permute-start.7 = (bf16[16,1024]{1,0:T(8,128)(2,1)S(1)}, bf16[16,1024]{1,0:T(8,128)(2,1)S(1)}, u32[]{:S(2)}, u32[]{:S(2)}) collective-permute-start(bf16[16,1024]{1,0:T(8,128)(2,1)S(1)} %get-tuple-element.41), channel_id=1, source_target_pairs={{1,0},{2,1},{3,2},{4,3},{5,4},{6,5},{7,6},{8,7},{9,8},{10,9},{11,1... | collective-permute-start | bytes 98312 | tf_op jit(solution)/shard_map/ppermute | solution.py:331
  13.7 3.0 %collective-permute-start.6 = (bf16[16,1024]{1,0:T(8,128)(2,1)S(1)}, bf16[16,1024]{1,0:T(8,128)(2,1)S(1)}, u32[]{:S(2)}, u32[]{:S(2)}) collective-permute-start(bf16[16,1024]{1,0:T(8,128)(2,1)S(1)} %get-tuple-element.42), channel_id=1, source_target_pairs={{0,1},{1,2},{2,3},{3,4},{4,5},{5,6},{6,7},{7,8},{8,9},{9,10},{10,1... | collective-permute-start | bytes 98312 | tf_op jit(solution)/shard_map/ppermute | solution.py:330
  16.7 2.3 %collective-permute-start.5 = (bf16[128,1024]{1,0:T(8,128)(2,1)}, bf16[128,1024]{1,0:T(8,128)(2,1)S(1)}, u32[]{:S(2)}, u32[]{:S(2)}) collective-permute-start(bf16[128,1024]{1,0:T(8,128)(2,1)} %get-tuple-element.28), channel_id=1, source_target_pairs={{0,8},{1,3},{2,10},{3,1},{4,12},{5,7},{6,14},{7,5},{8,0},{9,11},{1... | collective-permute-start | bytes 786440 | tf_op jit(solution)/shard_map/ppermute | solution.py:117
  19.1 1.2 %collective-permute-done.3 = bf16[64,384]{1,0:T(8,128)(2,1)S(1)} collective-permute-done((bf16[64,384]{1,0:T(8,128)(2,1)}, bf16[64,384]{1,0:T(8,128)(2,1)S(1)}, u32[]{:S(2)}, u32[]{:S(2)}) %collective-permute-start.3) | collective-permute-done | bytes 49184 | tf_op jit(solution)/shard_map/ppermute | solution.py:117
  20.3 0.8 pad_maximum_fusion.7
  21.1 1.6 %collective-permute-start.4 = (bf16[256,384]{1,0:T(8,128)(2,1)S(1)}, bf16[256,384]{1,0:T(8,128)(2,1)S(1)}, u32[]{:S(2)}, u32[]{:S(2)}) collective-permute-start(bf16[256,384]{1,0:T(8,128)(2,1)S(1)} %pad_maximum_fusion.7), channel_id=1, source_target_pairs={{0,2},{1,3},{2,0},{3,1},{4,6},{5,7},{6,4},{7,5},{8,10},{9,11},{10,... | collective-permute-start | bytes 589832 | tf_op jit(solution)/shard_map/ppermute | solution.py:117
  22.7 4.0 %collective-permute-done = bf16[32,3584]{1,0:T(8,128)(2,1)S(1)} collective-permute-done((bf16[32,3584]{1,0:T(8,128)(2,1)}, bf16[32,3584]{1,0:T(8,128)(2,1)S(1)}, u32[]{:S(2)}, u32[]{:S(2)}) %collective-permute-start) | collective-permute-done | bytes 229408 | tf_op jit(solution)/shard_map/ppermute | solution.py:119
  26.7 1.0 %pad_maximum_fusion.4 = bf16[64,3584]{1,0:T(8,128)(2,1)S(1)} fusion(bf16[32,3584]{1,0:T(8,128)(2,1)S(1)} %collective-permute-done, bf16[32,3584]{1,0:T(8,128)(2,1)} %get-tuple-element.23), kind=kLoop, calls=%fused_computation.4 | loop fusion | flops 917504 | bytes 917504 | tf_op jit(solution)/shard_map/concatenate | solution.py:325
  27.7 0.3 collective-permute-done.4
  28.0 1.8 %collective-permute-done.5 = bf16[128,1024]{1,0:T(8,128)(2,1)S(1)} collective-permute-done((bf16[128,1024]{1,0:T(8,128)(2,1)}, bf16[128,1024]{1,0:T(8,128)(2,1)S(1)}, u32[]{:S(2)}, u32[]{:S(2)}) %collective-permute-start.5) | collective-permute-done | bytes 262176 | tf_op jit(solution)/shard_map/ppermute | solution.py:117
  29.9 1.2 %collective-permute-start.16 = (bf16[64,3584]{1,0:T(8,128)(2,1)S(1)}, bf16[64,3584]{1,0:T(8,128)(2,1)S(1)}, u32[]{:S(2)}, u32[]{:S(2)}) collective-permute-start(bf16[64,3584]{1,0:T(8,128)(2,1)S(1)} %pad_maximum_fusion.4), channel_id=1, source_target_pairs={{0,2},{1,5},{2,0},{3,7},{4,6},{5,1},{6,4},{7,3},{8,10},{9,13},{10,... | collective-permute-start | bytes 1376264 | tf_op jit(solution)/shard_map/ppermute | solution.py:119
  31.1 7.3 %collective-permute-done.16 = bf16[64,3584]{1,0:T(8,128)(2,1)S(1)} collective-permute-done((bf16[64,3584]{1,0:T(8,128)(2,1)S(1)}, bf16[64,3584]{1,0:T(8,128)(2,1)S(1)}, u32[]{:S(2)}, u32[]{:S(2)}) %collective-permute-start.16) | collective-permute-done | bytes 458784 | tf_op jit(solution)/shard_map/ppermute | solution.py:119
  38.5 1.6 %collective-permute-start.17 = (bf16[128,3584]{1,0:T(8,128)(2,1)S(1)}, bf16[128,3584]{1,0:T(8,128)(2,1)S(1)}, u32[]{:S(2)}, u32[]{:S(2)}) collective-permute-start(bf16[128,3584]{1,0:T(8,128)(2,1)S(1)} %pad_maximum_fusion.2), channel_id=1, source_target_pairs={{0,16},{1,17},{2,18},{3,19},{4,20},{5,21},{6,22},{7,23},{8,24},{9,... | collective-permute-start | bytes 2752520 | tf_op jit(solution)/shard_map/ppermute | solution.py:119
  40.1 5.0 %collective-permute-start.9 = (bf16[512,384]{1,0:T(8,128)(2,1)S(1)}, bf16[512,384]{1,0:T(8,128)(2,1)S(1)}, u32[]{:S(2)}, u32[]{:S(2)}) collective-permute-start(bf16[512,384]{1,0:T(8,128)(2,1)S(1)} %pad_maximum_fusion.5.own_w), channel_id=1, source_target_pairs={{0,1},{1,0},{2,3},{3,2},{4,5},{5,4},{6,7},{7,6},{8,9},{9,8},{10,11... | collective-permute-start | bytes 1179656 | tf_op jit(solution)/shard_map/ppermute | solution.py:117
  45.0 1.8 %collective-permute-done.8 = bf16[256,1024]{1,0:T(8,128)(2,1)S(1)} collective-permute-done((bf16[256,1024]{1,0:T(8,128)(2,1)S(1)}, bf16[256,1024]{1,0:T(8,128)(2,1)S(1)}, u32[]{:S(2)}, u32[]{:S(2)}) %collective-permute-start.8) | collective-permute-done | bytes 524320 | tf_op jit(solution)/shard_map/ppermute | solution.py:117
  46.9 1.6 %collective-permute-start.10 = (bf16[512,1024]{1,0:T(8,128)(2,1)S(1)}, bf16[512,1024]{1,0:T(8,128)(2,1)S(1)}, u32[]{:S(2)}, u32[]{:S(2)}) collective-permute-start(bf16[512,1024]{1,0:T(8,128)(2,1)S(1)} %pad_maximum_fusion.1.xa), channel_id=1, source_target_pairs={{0,2},{1,5},{2,0},{3,7},{4,6},{5,1},{6,4},{7,3},{8,10},{9,13},{10,... | collective-permute-start | bytes 3145736 | tf_op jit(solution)/shard_map/ppermute | solution.py:117
  48.5 8.9 %collective-permute-done.17 = bf16[128,3584]{1,0:T(8,128)(2,1)S(1)} collective-permute-done((bf16[128,3584]{1,0:T(8,128)(2,1)S(1)}, bf16[128,3584]{1,0:T(8,128)(2,1)S(1)}, u32[]{:S(2)}, u32[]{:S(2)}) %collective-permute-start.17) | collective-permute-done | bytes 917536 | tf_op jit(solution)/shard_map/ppermute | solution.py:119
  57.7 5.3 %collective-permute-start.11 = (bf16[512,1024]{1,0:T(8,128)(2,1)S(1)}, bf16[512,1024]{1,0:T(8,128)(2,1)S(1)}, u32[]{:S(2)}, u32[]{:S(2)}) collective-permute-start(bf16[512,1024]{1,0:T(8,128)(2,1)S(1)} %pad_maximum_fusion.1.xa), channel_id=1, source_target_pairs={{0,1},{1,0},{2,3},{3,2},{4,5},{5,4},{6,7},{7,6},{8,9},{9,8},{10,11... | collective-permute-start | bytes 3145736 | tf_op jit(solution)/shard_map/ppermute | solution.py:117
  63.1 2.3 %collective-permute-done.11.xa_other = bf16[512,1024]{1,0:T(8,128)(2,1)S(1)} collective-permute-done((bf16[512,1024]{1,0:T(8,128)(2,1)S(1)}, bf16[512,1024]{1,0:T(8,128)(2,1)S(1)}, u32[]{:S(2)}, u32[]{:S(2)}) %collective-permute-start.11) | collective-permute-done | bytes 1048608 | tf_op jit(solution)/shard_map/ppermute | solution.py:117
  65.3 1.5 %collective-permute-done.12.xb_other = bf16[512,1024]{1,0:T(8,128)(2,1)S(1)} collective-permute-done((bf16[512,1024]{1,0:T(8,128)(2,1)S(1)}, bf16[512,1024]{1,0:T(8,128)(2,1)S(1)}, u32[]{:S(2)}, u32[]{:S(2)}) %collective-permute-start.12) | collective-permute-done | bytes 1048608 | tf_op jit(solution)/shard_map/ppermute | solution.py:117
  66.8 4.8 %attention.1 = (bf16[160,128]{1,0:T(8,128)(2,1)S(1)}, bf16[160,128]{1,0:T(8,128)(2,1)S(1)}, bf16[160,128]{1,0:T(8,128)(2,1)S(1)}, bf16[160,128]{1,0:T(8,128)(2,1)S(1)}) custom-call(s32[1]{0:T(128)S(6)} %copy.12.scalars, bf16[512,1024]{1,0:T(8,128)(2,1)S(1)} %pad_maximum_fusion.1.xa, bf16[512,1024]{1,0:T(8,128)(2,1)S(1)} %collective-permute-done.10.xb, ...), custom_call_target="tpu_custom_call" | custom-call | flops 5000000000 | bytes 8388608 | tf_op jit(solution)/shard_map/attention/pallas_call | solution.py:354
  71.6 2.7 %collective-permute-start.13 = (bf16[160,128]{1,0:T(8,128)(2,1)S(1)}, bf16[160,128]{1,0:T(8,128)(2,1)S(1)}, u32[]{:S(2)}, u32[]{:S(2)}) collective-permute-start(bf16[160,128]{1,0:T(8,128)(2,1)S(1)} %get-tuple-element.34), channel_id=1, source_target_pairs={{0,12},{1,13},{2,14},{3,15},{4,8},{5,9},{6,10},{7,11},{8,4},{9,5},... | collective-permute-start | bytes 122888 | tf_op jit(solution)/shard_map/ppermute | solution.py:117
  74.3 1.8 %collective-permute-start.15 = (bf16[160,128]{1,0:T(8,128)(2,1)S(1)}, bf16[160,128]{1,0:T(8,128)(2,1)S(1)}, u32[]{:S(2)}, u32[]{:S(2)}) collective-permute-start(bf16[160,128]{1,0:T(8,128)(2,1)S(1)} %get-tuple-element.36), channel_id=1, source_target_pairs={{0,8},{1,9},{2,10},{3,11},{4,12},{5,13},{6,14},{7,15},{8,0},{9,1},... | collective-permute-start | bytes 122888 | tf_op jit(solution)/shard_map/ppermute | solution.py:117
  76.1 8.0 %collective-permute-done.13.c1 = bf16[160,128]{1,0:T(8,128)(2,1)S(1)} collective-permute-done((bf16[160,128]{1,0:T(8,128)(2,1)S(1)}, bf16[160,128]{1,0:T(8,128)(2,1)S(1)}, u32[]{:S(2)}, u32[]{:S(2)}) %collective-permute-start.13) | collective-permute-done | bytes 40992 | tf_op jit(solution)/shard_map/ppermute | solution.py:117
  84.1 0.1 collective-permute-start.20
  84.3 3.7 %collective-permute-done.20.pb_other = bf16[256,3584]{1,0:T(8,128)(2,1)S(1)} collective-permute-done((bf16[256,3584]{1,0:T(8,128)(2,1)S(1)}, bf16[256,3584]{1,0:T(8,128)(2,1)S(1)}, u32[]{:S(2)}, u32[]{:S(2)}) %collective-permute-start.20) | collective-permute-done | bytes 1835040 | tf_op jit(solution)/shard_map/ppermute | solution.py:117
  88.0 4.8 %tail.1 = bf16[128,1024]{1,0:T(8,128)(2,1)} custom-call(s32[1]{0:T(128)S(6)} %copy.12.scalars, bf16[160,128]{1,0:T(8,128)(2,1)S(1)} %get-tuple-element.33.c0, bf16[160,128]{1,0:T(8,128)(2,1)S(1)} %collective-permute-done.13.c1, bf16[160,128]{1,0:T(8,128)(2,1)S(1)} %collective-permute-done.14.c2, bf16[160,128]{1,0:T(8,128)(2,1)S(1)} %collective-permute-done.15.c3, ...), custom_call_target="tpu_custom_call" | custom-call | flops 1200000000 | bytes 8388608 | tf_op jit(solution)/shard_map/tail/pallas_call | solution.py:378
  (34 shorter events, 0.5 us)
Async XLA Ops:
  3.5 26.3 %copy-start.5 = (bf16[128,1024]{1,0:T(8,128)(2,1)S(1)}, bf16[128,1024]{1,0:T(8,128)(2,1)}, u32[]{:S(2)}) copy-start(bf16[128,1024]{1,0:T(8,128)(2,1)} %get-tuple-element.28) | copy-start | bytes 786436
  3.6 10.1 %collective-permute-start.1 = (bf16[64,384]{1,0:T(8,128)(2,1)}, bf16[64,384]{1,0:T(8,128)(2,1)S(1)}, u32[]{:S(2)}, u32[]{:S(2)}) collective-permute-start(bf16[64,384]{1,0:T(8,128)(2,1)} %get-tuple-element.25), channel_id=1, source_target_pairs={{0,12},{1,13},{2,14},{3,15},{4,8},{5,9},{6,10},{7,11},{8,4},{9,5},... | collective-permute-start | bytes 147464 | tf_op jit(solution)/shard_map/ppermute | solution.py:117
  8.7 8.0 %collective-permute-start.2 = (bf16[64,384]{1,0:T(8,128)(2,1)}, bf16[64,384]{1,0:T(8,128)(2,1)S(1)}, u32[]{:S(2)}, u32[]{:S(2)}) collective-permute-start(bf16[64,384]{1,0:T(8,128)(2,1)} %get-tuple-element.26), channel_id=1, source_target_pairs={{0,4},{1,5},{2,6},{3,7},{4,0},{5,1},{6,2},{7,3},{8,12},{9,13},{10,... | collective-permute-start | bytes 147464 | tf_op jit(solution)/shard_map/ppermute | solution.py:117
  8.7 11.6 %collective-permute-start.3 = (bf16[64,384]{1,0:T(8,128)(2,1)}, bf16[64,384]{1,0:T(8,128)(2,1)S(1)}, u32[]{:S(2)}, u32[]{:S(2)}) collective-permute-start(bf16[64,384]{1,0:T(8,128)(2,1)} %get-tuple-element.27), channel_id=1, source_target_pairs={{0,8},{1,9},{2,10},{3,11},{4,12},{5,13},{6,14},{7,15},{8,0},{9,1},... | collective-permute-start | bytes 147464 | tf_op jit(solution)/shard_map/ppermute | solution.py:117
  9.3 17.4 %collective-permute-start = (bf16[32,3584]{1,0:T(8,128)(2,1)}, bf16[32,3584]{1,0:T(8,128)(2,1)S(1)}, u32[]{:S(2)}, u32[]{:S(2)}) collective-permute-start(bf16[32,3584]{1,0:T(8,128)(2,1)} %get-tuple-element.23), channel_id=1, source_target_pairs={{0,8},{1,9},{2,10},{3,11},{4,12},{5,13},{6,14},{7,15},{8,0},{9,1},... | collective-permute-start | bytes 688136 | tf_op jit(solution)/shard_map/ppermute | solution.py:119
  12.4 17.5 %collective-permute-start.7 = (bf16[16,1024]{1,0:T(8,128)(2,1)S(1)}, bf16[16,1024]{1,0:T(8,128)(2,1)S(1)}, u32[]{:S(2)}, u32[]{:S(2)}) collective-permute-start(bf16[16,1024]{1,0:T(8,128)(2,1)S(1)} %get-tuple-element.41), channel_id=1, source_target_pairs={{1,0},{2,1},{3,2},{4,3},{5,4},{6,5},{7,6},{8,7},{9,8},{10,9},{11,1... | collective-permute-start | bytes 98312 | tf_op jit(solution)/shard_map/ppermute | solution.py:331
  13.7 16.2 %collective-permute-start.6 = (bf16[16,1024]{1,0:T(8,128)(2,1)S(1)}, bf16[16,1024]{1,0:T(8,128)(2,1)S(1)}, u32[]{:S(2)}, u32[]{:S(2)}) collective-permute-start(bf16[16,1024]{1,0:T(8,128)(2,1)S(1)} %get-tuple-element.42), channel_id=1, source_target_pairs={{0,1},{1,2},{2,3},{3,4},{4,5},{5,6},{6,7},{7,8},{8,9},{9,10},{10,1... | collective-permute-start | bytes 98312 | tf_op jit(solution)/shard_map/ppermute | solution.py:330
  16.7 13.1 %collective-permute-start.5 = (bf16[128,1024]{1,0:T(8,128)(2,1)}, bf16[128,1024]{1,0:T(8,128)(2,1)S(1)}, u32[]{:S(2)}, u32[]{:S(2)}) collective-permute-start(bf16[128,1024]{1,0:T(8,128)(2,1)} %get-tuple-element.28), channel_id=1, source_target_pairs={{0,8},{1,3},{2,10},{3,1},{4,12},{5,7},{6,14},{7,5},{8,0},{9,11},{1... | collective-permute-start | bytes 786440 | tf_op jit(solution)/shard_map/ppermute | solution.py:117
  21.1 6.9 %collective-permute-start.4 = (bf16[256,384]{1,0:T(8,128)(2,1)S(1)}, bf16[256,384]{1,0:T(8,128)(2,1)S(1)}, u32[]{:S(2)}, u32[]{:S(2)}) collective-permute-start(bf16[256,384]{1,0:T(8,128)(2,1)S(1)} %pad_maximum_fusion.7), channel_id=1, source_target_pairs={{0,2},{1,3},{2,0},{3,1},{4,6},{5,7},{6,4},{7,5},{8,10},{9,11},{10,... | collective-permute-start | bytes 589832 | tf_op jit(solution)/shard_map/ppermute | solution.py:117
  29.9 8.5 %collective-permute-start.16 = (bf16[64,3584]{1,0:T(8,128)(2,1)S(1)}, bf16[64,3584]{1,0:T(8,128)(2,1)S(1)}, u32[]{:S(2)}, u32[]{:S(2)}) collective-permute-start(bf16[64,3584]{1,0:T(8,128)(2,1)S(1)} %pad_maximum_fusion.4), channel_id=1, source_target_pairs={{0,2},{1,5},{2,0},{3,7},{4,6},{5,1},{6,4},{7,3},{8,10},{9,13},{10,... | collective-permute-start | bytes 1376264 | tf_op jit(solution)/shard_map/ppermute | solution.py:119
  31.1 15.7 %collective-permute-start.8 = (bf16[256,1024]{1,0:T(8,128)(2,1)S(1)}, bf16[256,1024]{1,0:T(8,128)(2,1)S(1)}, u32[]{:S(2)}, u32[]{:S(2)}) collective-permute-start(bf16[256,1024]{1,0:T(8,128)(2,1)S(1)} %pad_maximum_fusion.3), channel_id=1, source_target_pairs={{0,4},{1,9},{2,6},{3,11},{4,0},{5,13},{6,2},{7,15},{8,12},{9,1},{1... | collective-permute-start | bytes 1572872 | tf_op jit(solution)/shard_map/ppermute | solution.py:117
  38.5 19.0 %collective-permute-start.17 = (bf16[128,3584]{1,0:T(8,128)(2,1)S(1)}, bf16[128,3584]{1,0:T(8,128)(2,1)S(1)}, u32[]{:S(2)}, u32[]{:S(2)}) collective-permute-start(bf16[128,3584]{1,0:T(8,128)(2,1)S(1)} %pad_maximum_fusion.2), channel_id=1, source_target_pairs={{0,16},{1,17},{2,18},{3,19},{4,20},{5,21},{6,22},{7,23},{8,24},{9,... | collective-permute-start | bytes 2752520 | tf_op jit(solution)/shard_map/ppermute | solution.py:119
  40.1 6.8 %collective-permute-start.9 = (bf16[512,384]{1,0:T(8,128)(2,1)S(1)}, bf16[512,384]{1,0:T(8,128)(2,1)S(1)}, u32[]{:S(2)}, u32[]{:S(2)}) collective-permute-start(bf16[512,384]{1,0:T(8,128)(2,1)S(1)} %pad_maximum_fusion.5.own_w), channel_id=1, source_target_pairs={{0,1},{1,0},{2,3},{3,2},{4,5},{5,4},{6,7},{7,6},{8,9},{9,8},{10,11... | collective-permute-start | bytes 1179656 | tf_op jit(solution)/shard_map/ppermute | solution.py:117
  46.9 16.2 %collective-permute-start.10 = (bf16[512,1024]{1,0:T(8,128)(2,1)S(1)}, bf16[512,1024]{1,0:T(8,128)(2,1)S(1)}, u32[]{:S(2)}, u32[]{:S(2)}) collective-permute-start(bf16[512,1024]{1,0:T(8,128)(2,1)S(1)} %pad_maximum_fusion.1.xa), channel_id=1, source_target_pairs={{0,2},{1,5},{2,0},{3,7},{4,6},{5,1},{6,4},{7,3},{8,10},{9,13},{10,... | collective-permute-start | bytes 3145736 | tf_op jit(solution)/shard_map/ppermute | solution.py:117
  57.6 26.7 %copy-start.4 = (bf16[128,1024]{1,0:T(8,128)(2,1)S(1)}, bf16[128,1024]{1,0:T(8,128)(2,1)}, u32[]{:S(2)}) copy-start(bf16[128,1024]{1,0:T(8,128)(2,1)} %feats_in.1) | copy-start | bytes 786436
  57.6 30.4 %copy-start = (f32[9,1024]{1,0:T(8,128)S(1)}, f32[9,1024]{1,0:T(8,128)}, u32[]{:S(2)}) copy-start(f32[9,1024]{1,0:T(8,128)} %taps.1) | copy-start | bytes 110596
  57.6 30.4 %copy-start.1 = (f32[1024]{0:T(1024)S(1)}, f32[1024]{0:T(1024)}, u32[]{:S(2)}) copy-start(f32[1024]{0:T(1024)} %param.16) | copy-start | bytes 12292
  57.6 30.3 %copy-start.2 = (f32[1024]{0:T(1024)S(1)}, f32[1024]{0:T(1024)}, u32[]{:S(2)}) copy-start(f32[1024]{0:T(1024)} %param.19) | copy-start | bytes 12292
  57.6 30.3 %copy-start.3 = (f32[1024]{0:T(1024)S(1)}, f32[1024]{0:T(1024)}, u32[]{:S(2)}) copy-start(f32[1024]{0:T(1024)} %param.20) | copy-start | bytes 12292
  57.7 26.5 %collective-permute-start.18 = (bf16[256,3584]{1,0:T(8,128)(2,1)S(1)}, bf16[256,3584]{1,0:T(8,128)(2,1)S(1)}, u32[]{:S(2)}, u32[]{:S(2)}) collective-permute-start(bf16[256,3584]{1,0:T(8,128)(2,1)S(1)} %pad_maximum_fusion.pa), channel_id=1, source_target_pairs={{0,4},{1,3},{2,6},{3,1},{4,0},{5,7},{6,2},{7,5},{8,12},{9,11},{10,... | collective-permute-start | bytes 5505032 | tf_op jit(solution)/shard_map/ppermute | solution.py:119
  57.7 7.6 %collective-permute-start.11 = (bf16[512,1024]{1,0:T(8,128)(2,1)S(1)}, bf16[512,1024]{1,0:T(8,128)(2,1)S(1)}, u32[]{:S(2)}, u32[]{:S(2)}) collective-permute-start(bf16[512,1024]{1,0:T(8,128)(2,1)S(1)} %pad_maximum_fusion.1.xa), channel_id=1, source_target_pairs={{0,1},{1,0},{2,3},{3,2},{4,5},{5,4},{6,7},{7,6},{8,9},{9,8},{10,11... | collective-permute-start | bytes 3145736 | tf_op jit(solution)/shard_map/ppermute | solution.py:117
  63.1 3.8 %collective-permute-start.12 = (bf16[512,1024]{1,0:T(8,128)(2,1)S(1)}, bf16[512,1024]{1,0:T(8,128)(2,1)S(1)}, u32[]{:S(2)}, u32[]{:S(2)}) collective-permute-start(bf16[512,1024]{1,0:T(8,128)(2,1)S(1)} %collective-permute-done.10.xb), channel_id=1, source_target_pairs={{0,1},{1,0},{2,3},{3,2},{4,5},{5,4},{6,7},{7,6},{8,9},{9,8},{10,11... | collective-permute-start | bytes 3145736 | tf_op jit(solution)/shard_map/ppermute | solution.py:117
  71.6 12.5 %collective-permute-start.13 = (bf16[160,128]{1,0:T(8,128)(2,1)S(1)}, bf16[160,128]{1,0:T(8,128)(2,1)S(1)}, u32[]{:S(2)}, u32[]{:S(2)}) collective-permute-start(bf16[160,128]{1,0:T(8,128)(2,1)S(1)} %get-tuple-element.34), channel_id=1, source_target_pairs={{0,12},{1,13},{2,14},{3,15},{4,8},{5,9},{6,10},{7,11},{8,4},{9,5},... | collective-permute-start | bytes 122888 | tf_op jit(solution)/shard_map/ppermute | solution.py:117
  74.3 9.8 %collective-permute-start.14 = (bf16[160,128]{1,0:T(8,128)(2,1)S(1)}, bf16[160,128]{1,0:T(8,128)(2,1)S(1)}, u32[]{:S(2)}, u32[]{:S(2)}) collective-permute-start(bf16[160,128]{1,0:T(8,128)(2,1)S(1)} %get-tuple-element.35), channel_id=1, source_target_pairs={{0,4},{1,5},{2,6},{3,7},{4,0},{5,1},{6,2},{7,3},{8,12},{9,13},{10,... | collective-permute-start | bytes 122888 | tf_op jit(solution)/shard_map/ppermute | solution.py:117
  74.3 9.8 %collective-permute-start.15 = (bf16[160,128]{1,0:T(8,128)(2,1)S(1)}, bf16[160,128]{1,0:T(8,128)(2,1)S(1)}, u32[]{:S(2)}, u32[]{:S(2)}) collective-permute-start(bf16[160,128]{1,0:T(8,128)(2,1)S(1)} %get-tuple-element.36), channel_id=1, source_target_pairs={{0,8},{1,9},{2,10},{3,11},{4,12},{5,13},{6,14},{7,15},{8,0},{9,1},... | collective-permute-start | bytes 122888 | tf_op jit(solution)/shard_map/ppermute | solution.py:117
  76.1 8.2 %collective-permute-start.19 = (bf16[256,3584]{1,0:T(8,128)(2,1)S(1)}, bf16[256,3584]{1,0:T(8,128)(2,1)S(1)}, u32[]{:S(2)}, u32[]{:S(2)}) collective-permute-start(bf16[256,3584]{1,0:T(8,128)(2,1)S(1)} %pad_maximum_fusion.pa), channel_id=1, source_target_pairs={{0,1},{1,0},{2,3},{3,2},{4,5},{5,4},{6,7},{7,6},{8,9},{9,8},{10,11... | collective-permute-start | bytes 5505032 | tf_op jit(solution)/shard_map/ppermute | solution.py:117
  84.1 3.9 %collective-permute-start.20 = (bf16[256,3584]{1,0:T(8,128)(2,1)S(1)}, bf16[256,3584]{1,0:T(8,128)(2,1)S(1)}, u32[]{:S(2)}, u32[]{:S(2)}) collective-permute-start(bf16[256,3584]{1,0:T(8,128)(2,1)S(1)} %collective-permute-done.18.pb), channel_id=1, source_target_pairs={{0,1},{1,0},{2,3},{3,2},{4,5},{5,4},{6,7},{7,6},{8,9},{9,8},{10,11... | collective-permute-start | bytes 5505032 | tf_op jit(solution)/shard_map/ppermute | solution.py:117
